TPU v7x, 128 devices: a whole 4x4x4 slice. The times are simulated.
128 devices in a mesh: brick: 16 (over x, y), slab: 8 (over z, core).
Axes of the slice: x: 4, y: 4, z: 4, core: 2. Of those that a mesh axis runs over, the one named last changes fastest.
Arguments:
- positions: float32 [16384, 3, 128], P(('brick', 'slab')), may hold values from 0 to 4
- charges: float32 [16384, 128], P(('brick', 'slab')), may hold values from 0.5 to 2
- drag: float32 [16384, 128], P(('brick', 'slab')), may hold values from 2 to 8
- right_side: float32 [16384, 128], P(('brick', 'slab')), may hold values from -2.5 to 6.5
- neighbours: int32 [16384, 4], P(('brick', 'slab')), may hold values from 0 to 16383, as said below
- owners: int32 [16384, 1], P(('brick', 'slab')), may hold values from 0 to 15; in each aligned block of 128 rows (0 to 127, 128 to 255, ...) at most 24 rows name the same one
Outputs:
- owned_solution: float32 [49152, 128], P(('brick', 'slab'))
- owned_residual: float32 [49152, 128], P(('brick', 'slab'))
Inputs may be any that keep to these rules, and one draw needn't show every extreme that they name: A tile's neighbours lie on the same brick index and the same or an adjacent slab index; in each slot k pairing goes both ways (u is t's neighbour in slot k exactly when t is u's); never the tile itself. `owners`: among the 128 tiles of one device at most 24 name the same owner, a bound that some block reaches of them.
All inputs are finite; a program needn't handle non-finite values.
Results may differ from a plain program's by a relative error of at most 0.0009.
Values may be sent and summed in bfloat16 or wider, within the bound.
No kernel may reach another device: no remote copies, remote signals or barrier semaphores. Data moves between devices by JAX's collectives and lax.ppermute only.
A program may use at most 64 MiB of HBM per device.

v0:
```python
import jax
import jax.numpy as jnp
from jax import lax
from jax.sharding import PartitionSpec as P

ITERS = 3


def extended(block, sides, width):
    for axis, dim in sides:
        count = lax.axis_size(axis)
        forward = [(i, i + 1) for i in range(count - 1)]
        backward = [(target, source) for source, target in forward]
        low = lax.ppermute(
            lax.slice_in_dim(block, block.shape[dim] - width, None, axis=dim), axis, forward
        )
        high = lax.ppermute(lax.slice_in_dim(block, 0, width, axis=dim), axis, backward)
        block = jnp.concatenate([low, block, high], axis=dim)
    return block


def couplings(own_tile, other_tiles, scale):
    delta_x = own_tile[:, None, 0, :, None] - other_tiles[:, :, 0, None, :]
    delta_y = own_tile[:, None, 1, :, None] - other_tiles[:, :, 1, None, :]
    delta_z = own_tile[:, None, 2, :, None] - other_tiles[:, :, 2, None, :]
    squared = delta_x * delta_x + delta_y * delta_y + delta_z * delta_z
    distance = jnp.sqrt(squared + 0.01)
    charge_product = own_tile[:, None, 3, :, None] * other_tiles[:, :, 3, None, :]
    return (1.0 / (squared + 0.5) + charge_product * jnp.exp(-distance)) * scale


def split_parts(direction):
    high_part = direction.astype(jnp.bfloat16)
    low_part = (direction - high_part.astype(jnp.float32)).astype(jnp.bfloat16)
    return jnp.stack([high_part, low_part], axis=1)


def squares(residual):
    return lax.psum(jnp.sum(residual * residual), ("brick", "slab"))


def conjugate(apply_matrix, forces):
    solution = jnp.zeros_like(forces)
    residual = forces
    direction = forces
    norm_now = squares(residual)
    for iteration in range(ITERS):
        product = apply_matrix(direction)
        step_size = norm_now / lax.psum(jnp.sum(direction * product), ("brick", "slab"))
        solution = solution + step_size * direction
        residual = residual - step_size * product
        norm_next = squares(residual)
        direction = residual + norm_next / norm_now * direction
        norm_now = norm_next
    return (solution, residual)


def local(positions, charges, drag, right_side, neighbours, owners):
    tile_count = positions.shape[0]
    tile_width = positions.shape[2]
    reach_count = neighbours.shape[1] + 1
    brick_count = lax.axis_size("brick")
    slab_count = lax.axis_size("slab")
    per_owner = max(3, 3 * tile_count // brick_count)
    slot_count = brick_count * per_owner
    brick_at = lax.axis_index("brick")
    slab_at = lax.axis_index("slab")
    first_tile = (brick_at * slab_count + slab_at) * tile_count
    packed = jnp.concatenate([positions, charges[:, None, :]], axis=1)
    window = extended(packed, (("slab", 0),), tile_count)
    local_rows = neighbours - first_tile + tile_count
    own_rows = jnp.arange(tile_count, dtype=jnp.int32) + tile_count
    index_all = jnp.concatenate([own_rows[:, None], local_rows], axis=1)
    scale = 8.0 / (reach_count * tile_width)
    first_slot = (jnp.arange(reach_count) == 0).astype(jnp.float32)
    self_mask = 1.0 - first_slot[:, None, None] * jnp.eye(tile_width, dtype=jnp.float32)
    weights = couplings(packed, window[index_all], scale) * self_mask
    diagonal = drag + jnp.sum(weights, axis=(1, 3))
    blocks = weights.astype(jnp.bfloat16)
    own_owner = owners[:, 0]
    matching = own_owner[:, None] == own_owner[None, :]
    earlier = jnp.arange(tile_count)[None, :] < jnp.arange(tile_count)[:, None]
    position = jnp.sum((matching & earlier).astype(jnp.int32), axis=1)
    target = own_owner * per_owner + position
    select = (jnp.arange(slot_count, dtype=jnp.int32)[:, None] == target[None, :]).astype(jnp.int32)
    source = jnp.sum(select * jnp.arange(tile_count, dtype=jnp.int32)[None, :], axis=1)
    filled = jnp.sum(select, axis=1)
    filled_float = filled.astype(jnp.float32)

    def apply_home(direction):
        parts = split_parts(direction)
        stacked = extended(parts, (("slab", 0),), tile_count)
        coupled = jnp.einsum(
            "tkac,tksc->ta", blocks, stacked[index_all], preferred_element_type=jnp.float32
        )
        return diagonal * direction - coupled

    solution, residual = conjugate(apply_home, right_side)
    outgoing = jnp.stack([solution[source], residual[source]], axis=1) * filled_float[:, None, None]
    arrived = lax.all_to_all(outgoing, "brick", split_axis=0, concat_axis=0, tiled=True)
    return (arrived[:, 0], arrived[:, 1])


def solution(mesh):
    placed = (
        P(("brick", "slab"), None, None),
        P(("brick", "slab"), None),
        P(("brick", "slab"), None),
        P(("brick", "slab"), None),
        P(("brick", "slab"), None),
        P(("brick", "slab"), None),
    )
    return jax.shard_map(
        local,
        mesh=mesh,
        in_specs=placed,
        out_specs=(P(("brick", "slab"), None), P(("brick", "slab"), None)),
        check_vma=False,
    )
```

profile of v0, /device:TPU:0, one launch (start us, length us, event | category | flops | bytes accessed | tf_op | source)
XLA Modules:
  0.0 481.7 jit_solution(7967243695039604517)
XLA Ops:
  2.7 1.3 collective-permute-start
  4.0 1.3 collective-permute-start.1
  6.5 5.3 %collective-permute-start.2 = (bf16[128,2,128]{2,1,0:T(2,128)(2,1)S(1)}, bf16[128,2,128]{2,1,0:T(2,128)(2,1)S(1)}, u32[]{:S(2)}, u32[]{:S(2)}) collective-permute-start(bf16[128,2,128]{2,1,0:T(2,128)(2,1)S(1)} %pad_maximum_fusion.5), channel_id=1, source_target_pairs={{0,1},{1,2},{2,3},{3,4},{4,5},{5,6},{6,7},{8,9},{9,10},{10,11},{11... | collective-permute-start | bytes 196616 | tf_op jit(solution)/shard_map/ppermute | solution.py:14
  11.8 1.3 collective-permute-start.3
  17.1 2.8 gather_fusion.1
  21.9 2.8 gather_fusion
  25.8 49.8 %fusion.1 = (f32[128,128]{1,0:T(8,128)S(1)}, bf16[128,5,128,128]{3,2,1,0:T(8,128)(2,1)}) fusion(f32[5,128,128]{2,1,0:T(8,128)S(1)} %subtract_multiply_fusion, f32[128,5,128]{2,1,0:T(8,128)S(1)} %get-tuple-element.32, f32[128,128]{1,0:T(8,128)} %param.7, f32[128,5,128]{2,1,0:T(8,128)S(1)} %get-tuple-element.33, f32[128,128]{1,0:T(8,128)S(1)} %get-tuple-element.24, ...), kind=kLoop, calls=%fused_computation.8 | loop fusion | flops 188727296 | bytes 22937600 | tf_op jit(solution)/shard_map/reduce_sum | solution.py:78
  75.6 10.7 %fusion.10 = f32[128,1,128,1]{2,1,3,0:T(1,128)S(1)} fusion(bf16[128,5,128,128]{3,2,1,0:T(8,128)(2,1)} %get-tuple-element.16, f32[128,5,128,1]{2,3,1,0:T(1,128)S(1)} %bitcast.65), kind=kOutput, calls=%fused_computation.72 | convolution fusion | flops 20971520 | bytes 21364736 | tf_op jit(solution)/shard_map/tkac,tksc->ta/dot_general | solution.py:93
  86.9 69.0 %all-reduce = (f32[]{:T(128)}, f32[]{:T(128)}) all-reduce(f32[]{:T(128)} %get-tuple-element.3, f32[]{:T(128)} %get-tuple-element.2), channel_id=1, replica_groups=mesh['brick'=16,'slab'=8] {'brick','slab'}, use_global_device_ids=true, to_apply=%region_1.0 | all-reduce | flops 2 | bytes 16 | tf_op jit(solution)/shard_map/psum | solution.py:39
  157.9 63.3 %psum.44 = f32[]{:T(128)} all-reduce(f32[]{:T(128)} %get-tuple-element.12), channel_id=1, replica_groups=mesh['brick'=16,'slab'=8] {'brick','slab'}, use_global_device_ids=true, to_apply=%region_7.0 | all-reduce | flops 1 | bytes 8 | tf_op jit(solution)/shard_map/psum | solution.py:39
  222.9 1.8 collective-permute-start.4
  224.7 1.3 collective-permute-start.5
  226.2 2.0 collective-permute-done.5
  228.5 2.8 gather_fusion.2
  232.1 10.7 %fusion.11 = f32[128,1,128,1]{2,1,3,0:T(1,128)S(1)} fusion(bf16[128,5,128,128]{3,2,1,0:T(8,128)(2,1)} %get-tuple-element.16, f32[128,5,128,1]{2,3,1,0:T(1,128)S(1)} %bitcast.67), kind=kOutput, calls=%fused_computation.73 | convolution fusion | flops 20971520 | bytes 21364736 | tf_op jit(solution)/shard_map/tkac,tksc->ta/dot_general | solution.py:93
  243.5 66.2 %psum.45 = f32[]{:T(128)} all-reduce(f32[]{:T(128)} %multiply_reduce_fusion.2), channel_id=1, replica_groups=mesh['brick'=16,'slab'=8] {'brick','slab'}, use_global_device_ids=true, to_apply=%region_10.0 | all-reduce | flops 1 | bytes 8 | tf_op jit(solution)/shard_map/psum | solution.py:49
  311.6 62.7 %psum.46 = f32[]{:T(128)} all-reduce(f32[]{:T(128)} %get-tuple-element.8), channel_id=1, replica_groups=mesh['brick'=16,'slab'=8] {'brick','slab'}, use_global_device_ids=true, to_apply=%region_12.0 | all-reduce | flops 1 | bytes 8 | tf_op jit(solution)/shard_map/psum | solution.py:39
  375.9 1.8 collective-permute-start.6
  377.7 1.3 collective-permute-start.7
  379.1 2.9 collective-permute-done.7
  382.2 2.8 gather_fusion.3
  385.9 10.7 %fusion.12 = f32[128,1,128,1]{2,1,3,0:T(1,128)S(1)} fusion(bf16[128,5,128,128]{3,2,1,0:T(8,128)(2,1)} %get-tuple-element.16, f32[128,5,128,1]{2,3,1,0:T(1,128)S(1)} %bitcast.66), kind=kOutput, calls=%fused_computation.74 | convolution fusion | flops 20971520 | bytes 21364736 | tf_op jit(solution)/shard_map/tkac,tksc->ta/dot_general | solution.py:93
  397.2 65.5 %psum.47 = f32[]{:T(128)} all-reduce(f32[]{:T(128)} %multiply_reduce_fusion), channel_id=1, replica_groups=mesh['brick'=16,'slab'=8] {'brick','slab'}, use_global_device_ids=true, to_apply=%region_15.0 | all-reduce | flops 1 | bytes 8 | tf_op jit(solution)/shard_map/psum | solution.py:49
  466.8 13.9 %all_to_all.5 = f32[384,2,128]{2,1,0:T(2,128)S(1)} all-to-all(f32[384,2,128]{2,1,0:T(2,128)S(1)} %copy.113), channel_id=1, replica_groups=mesh['brick'=16,'slab'=8] {'brick'}, dimensions={0} | all-to-all | bytes 786432 | tf_op jit(solution)/shard_map/all_to_all | solution.py:100
  (62 shorter events, 20.1 us)
Async XLA Ops:
  2.7 18.1 %collective-permute-start = (f32[128,4,128]{2,1,0:T(4,128)S(1)}, f32[128,4,128]{2,1,0:T(4,128)S(1)}, u32[]{:S(2)}, u32[]{:S(2)}) collective-permute-start(f32[128,4,128]{2,1,0:T(4,128)S(1)} %pad_maximum_fusion.1), channel_id=1, source_target_pairs={{0,1},{1,2},{2,3},{3,4},{4,5},{5,6},{6,7},{8,9},{9,10},{10,11},{11... | collective-permute-start | bytes 786440 | tf_op jit(solution)/shard_map/ppermute | solution.py:14
  4.0 16.8 %collective-permute-start.1 = (f32[128,4,128]{2,1,0:T(4,128)S(1)}, f32[128,4,128]{2,1,0:T(4,128)S(1)}, u32[]{:S(2)}, u32[]{:S(2)}) collective-permute-start(f32[128,4,128]{2,1,0:T(4,128)S(1)} %pad_maximum_fusion.1), channel_id=1, source_target_pairs={{1,0},{2,1},{3,2},{4,3},{5,4},{6,5},{7,6},{9,8},{10,9},{11,10},{12... | collective-permute-start | bytes 786440 | tf_op jit(solution)/shard_map/ppermute | solution.py:17
  6.5 10.3 %collective-permute-start.2 = (bf16[128,2,128]{2,1,0:T(2,128)(2,1)S(1)}, bf16[128,2,128]{2,1,0:T(2,128)(2,1)S(1)}, u32[]{:S(2)}, u32[]{:S(2)}) collective-permute-start(bf16[128,2,128]{2,1,0:T(2,128)(2,1)S(1)} %pad_maximum_fusion.5), channel_id=1, source_target_pairs={{0,1},{1,2},{2,3},{3,4},{4,5},{5,6},{6,7},{8,9},{9,10},{10,11},{11... | collective-permute-start | bytes 196616 | tf_op jit(solution)/shard_map/ppermute | solution.py:14
  11.8 5.0 %collective-permute-start.3 = (bf16[128,2,128]{2,1,0:T(2,128)(2,1)S(1)}, bf16[128,2,128]{2,1,0:T(2,128)(2,1)S(1)}, u32[]{:S(2)}, u32[]{:S(2)}) collective-permute-start(bf16[128,2,128]{2,1,0:T(2,128)(2,1)S(1)} %pad_maximum_fusion.5), channel_id=1, source_target_pairs={{1,0},{2,1},{3,2},{4,3},{5,4},{6,5},{7,6},{9,8},{10,9},{11,10},{12... | collective-permute-start | bytes 196616 | tf_op jit(solution)/shard_map/ppermute | solution.py:17
  75.6 10.7 %copy-start = (f32[128,128]{1,0:T(8,128)S(1)}, f32[128,128]{1,0:T(8,128)}, u32[]{:S(2)}) copy-start(f32[128,128]{1,0:T(8,128)} %param.9) | copy-start | bytes 196612
  75.6 10.7 %copy-start.1 = (f32[128,128]{1,0:T(8,128)S(1)}, f32[128,128]{1,0:T(8,128)}, u32[]{:S(2)}) copy-start(f32[128,128]{1,0:T(8,128)} %param.8) | copy-start | bytes 196612
  222.9 3.3 collective-permute-start.4
  224.7 3.5 collective-permute-start.5
  375.9 3.1 collective-permute-start.6
  377.7 4.2 collective-permute-start.7
where the time goes:
time: 483 us; the launch traced here: 482 us
  blocking collectives  341 us (71%)
  other arithmetic  62.6 us (13%)
  matrix products  32 us (7%)
  local copies, waits for them, and re-layouts  18.5 us (4%)
  starting transfers between devices  15.3 us (3%)
  between operations  7.76 us (2%)
  waiting for transfers between devices  4.97 us (1%)
    psum x3, blocking collectives, squares(): return lax.psum(jnp.sum(residual * residual), ('brick', 'slab'))  195 us
    psum x2, blocking collectives, conjugate(): lax.psum(jnp.sum(direction * product), ('brick', 'slab'))  132 us
    reduce_sum x1, other arithmetic, local(): diagonal = drag + jnp.sum(weights, axis=(1, 3))  49.8 us
    dot_general x3, matrix products, apply_home(): jnp.einsum('tkac,tksc->ta', blocks, stacked[index_all], preferred_element...  32 us
    all_to_all x1, blocking collectives, local(): lax.all_to_all(outgoing, 'brick', split_axis=0, concat_axis=0, tiled=True)  13.9 us
    ppermute x4, starting transfers between devices, extended(): lax.ppermute(lax.slice_in_dim(block, block.shape[dim] - width, None, axis...  10.1 us
  transfers between devices with their start and end apart: 8, of which 2 were waited for; matrix products, arithmetic and copies ran while one was open for 2% of the time, Pallas kernels for 0%

commit v1 on v0

v1 whole, which is shorter than its diff:
```python
import functools

import jax
import jax.numpy as jnp
from jax import lax
from jax.experimental import pallas as pl
from jax.experimental.pallas import tpu as pltpu
from jax.sharding import PartitionSpec as P

ITERS = 3
SHIFT = 7.0
LOG2E = 1.4426950408889634
F32 = jnp.float32
BF16 = jnp.bfloat16
BOTH = ("brick", "slab")
PAIRS = {
    (0, 0): 0,
    (0, 1): 1,
    (1, 1): 2,
    (0, 2): 3,
    (1, 2): 4,
    (2, 2): 5,
    (0, 3): 6,
    (1, 3): 7,
    (2, 3): 8,
}
VMEM = pl.BlockSpec(memory_space=pltpu.VMEM)


def split3(value):
    high = value.astype(BF16)
    rest = value - high.astype(F32)
    middle = rest.astype(BF16)
    low = (rest - middle.astype(F32)).astype(BF16)
    return high, middle, low


def split2(value):
    high = value.astype(BF16).astype(F32)
    low = (value - high).astype(BF16).astype(F32)
    return high, low


def rows_at(ref, row, count):
    return ref[pl.ds(row, count, stride=8), :]


def put_rows(ref, row, value):
    ref[pl.ds(row, value.shape[0], stride=8), :] = value


def add_dots(row, vectors):
    lane = lax.broadcasted_iota(jnp.int32, (1, 128), 1)
    newest = len(vectors) - 1
    for (i, j), place in PAIRS.items():
        if j == newest or (newest == 1 and j == 0):
            product = vectors[i] * vectors[j]
            total = jnp.sum(jnp.sum(product, axis=0, keepdims=True), axis=1, keepdims=True)
            row = row + jnp.where(lane == place, total, 0.0)
    return row


def pack_kernel(pos_ref, charge_ref, force_ref, out_ref):
    count = charge_ref.shape[0]
    for j in range(3):
        out_ref[pl.ds(j * count, count), :] = pos_ref[:, j, :] - 2.0
    out_ref[pl.ds(3 * count, count), :] = jnp.log2(charge_ref[...])
    out_ref[pl.ds(4 * count, count), :] = force_ref[...]


def weights_kernel(
    scale, step_tiles, index_ref, own_ref, near_ref, far_ref, drag_ref,
    blocks_ref, vector_ref, diagonal_ref, row_ref, raw, mine, sums, images,
):
    step = pl.program_id(0)
    count = drag_ref.shape[0]
    square = LOG2E * LOG2E

    @pl.when(step == 0)
    def _():
        one = jnp.ones((count, 128), F32)
        zero = jnp.zeros((count, 128), F32)
        for part, ref in enumerate((own_ref, near_ref, far_ref)):
            base = part * count * 8
            x, y, z, charge, force = (ref[pl.ds(j * count, count), :] for j in range(5))
            norm = x * x + y * y + z * z
            high, low = split2(force)
            for j, value in enumerate((x, y, z, charge, norm, one, high, low)):
                put_rows(raw, base + j, value)
            if part == 0:
                first = (-2.0 / scale) * x, (-2.0 / scale) * y, (-2.0 / scale) * z
                rows = (*first, zero, one / scale, (norm + 0.5) / scale, zero, zero)
                second = (-2.0 * square) * x, (-2.0 * square) * y, (-2.0 * square) * z
                rows += (*second, zero, one * square, (norm + 0.01) * square, zero, zero)
                rows += (zero, zero, zero, one, zero, charge + jnp.log2(scale * one), zero, zero)
                for j, value in enumerate(rows):
                    mine[pl.ds(j, count, stride=24), :] = value

    same = lax.broadcasted_iota(jnp.int32, (128, 128), 0) == lax.broadcasted_iota(
        jnp.int32, (128, 128), 1
    )

    def tile(i, carry):
        t = step * step_tiles + i
        rights = []
        for j in range(3):
            high, middle, low = split3(mine[pl.ds(pl.multiple_of(t * 24 + 8 * j, 8), 8), :])
            rights.append(jnp.concatenate([high, middle, low, high, middle, high], axis=0))
        right = jnp.concatenate(rights, axis=1)
        total = jnp.zeros((8, 128), F32)
        image = jnp.zeros((8, 128), F32)
        for k in range(5):
            u = t if k == 0 else index_ref[t * 4 + k - 1]
            high, middle, low = split3(raw[pl.ds(pl.multiple_of(u * 8, 8), 8), :])
            left = jnp.concatenate([high, high, high, middle, middle, low], axis=0)
            terms = lax.dot_general(
                left, right, (((0,), (0,)), ((), ())), preferred_element_type=F32
            )
            inverse = pl.reciprocal(terms[:, :128], approx=False)
            shifted = terms[:, 128:256]
            distance = shifted * lax.rsqrt(shifted)
            weight = inverse + jnp.exp2(terms[:, 256:] - distance)
            if k == 0:
                weight = jnp.where(same, 0.0, weight)
            total = total + jnp.sum(weight.reshape(16, 8, 128), axis=0)
            block = weight.astype(BF16)
            blocks_ref[i, pl.ds(128 * k, 128), :] = block
            image = image + jnp.dot(high, block, preferred_element_type=F32)
        place = pl.ds(pl.multiple_of(t * 8, 8), 8)
        sums[place, :] = total
        images[place, :] = image
        return carry

    lax.fori_loop(0, step_tiles, tile, 0)

    @pl.when(step == pl.num_programs(0) - 1)
    def _():
        diagonal = drag_ref[...]
        for j in range(8):
            diagonal = diagonal + rows_at(sums, j, count)
        coupled = rows_at(images, 6, count) + rows_at(images, 7, count)
        force = own_ref[pl.ds(4 * count, count), :]
        vector = (diagonal - SHIFT) * force - coupled
        diagonal_ref[...] = diagonal
        vector_ref[...] = vector
        row_ref[...] = add_dots(jnp.zeros((1, 128), F32), [force, vector])


def weights(index, own, near, far, drag, scale, step_tiles):
    count = drag.shape[0]
    whole = lambda shape: pl.BlockSpec(shape, lambda i, *_: (0,) * len(shape))
    return pl.pallas_call(
        functools.partial(weights_kernel, scale, step_tiles),
        grid_spec=pltpu.PrefetchScalarGridSpec(
            num_scalar_prefetch=1,
            grid=(count // step_tiles,),
            in_specs=[whole(own.shape)] * 3 + [whole(drag.shape)],
            out_specs=[
                pl.BlockSpec((step_tiles, 640, 128), lambda i, *_: (i, 0, 0)),
                whole(drag.shape),
                whole(drag.shape),
                whole((1, 128)),
            ],
            scratch_shapes=[
                pltpu.VMEM((3 * count * 8, 128), F32),
                pltpu.VMEM((count * 24, 128), F32),
                pltpu.VMEM((count * 8, 128), F32),
                pltpu.VMEM((count * 8, 128), F32),
            ],
        ),
        out_shape=[
            jax.ShapeDtypeStruct((count, 640, 128), BF16),
            jax.ShapeDtypeStruct(drag.shape, F32),
            jax.ShapeDtypeStruct(drag.shape, F32),
            jax.ShapeDtypeStruct((1, 128), F32),
        ],
        name="weights",
    )(index, own, near, far, drag)


def image_kernel(
    step_tiles, history, slots, index_ref, blocks_ref, diagonal_ref, row_ref, near_ref, far_ref, *refs
):
    past = refs[:history]
    if slots:
        owner_column, owner_row = refs[history : history + 2]
        refs = refs[2:]
    if slots:
        out_ref, totals_ref, parts, images = refs[history:]
    else:
        vector_ref, totals_ref, parts, images = refs[history:]
    step = pl.program_id(0)
    count = diagonal_ref.shape[0]

    @pl.when(step == 0)
    def _():
        for part, ref in enumerate((past[-1], near_ref, far_ref)):
            high, low = split2(ref[...])
            put_rows(parts, part * count * 8, high)
            put_rows(parts, part * count * 8 + 1, low)

    def tile(i, carry):
        t = step * step_tiles + i
        lefts = []
        for k in range(5):
            u = t if k == 0 else index_ref[t * 4 + k - 1]
            lefts.append(parts[pl.ds(pl.multiple_of(u * 8, 8), 8), :].astype(BF16))
        left = jnp.concatenate(lefts, axis=1)
        images[pl.ds(pl.multiple_of(t * 8, 8), 8), :] = jnp.dot(
            left, blocks_ref[i], preferred_element_type=F32
        )
        return carry

    lax.fori_loop(0, step_tiles, tile, 0, unroll=2)

    @pl.when(step == pl.num_programs(0) - 1)
    def _():
        coupled = rows_at(images, 0, count) + rows_at(images, 1, count)
        vectors = [ref[...] for ref in past]
        vector = (diagonal_ref[...] - SHIFT) * vectors[-1] - coupled
        vectors.append(vector)
        row = add_dots(row_ref[...], vectors)
        if not slots:
            vector_ref[...] = vector
            totals_ref[...] = row
            return
        totals_ref[...] = jnp.broadcast_to(row, totals_ref.shape)
        owners, rows_each, _ = out_ref.shape
        each = rows_each // 4
        earlier = lax.broadcasted_iota(jnp.int32, (count, count), 0) < lax.broadcasted_iota(
            jnp.int32, (count, count), 1
        )
        matching = (owner_column[...] == owner_row[...]) & earlier
        position = jnp.sum(matching.astype(jnp.int32), axis=0, keepdims=True)
        target = owner_row[...] * each + position
        slot = lax.broadcasted_iota(jnp.int32, (owners * each, count), 0)
        chosen = (slot == target).astype(F32).astype(BF16)
        for j, value in enumerate(vectors):
            placed = sum(
                jnp.dot(chosen, piece, preferred_element_type=F32) for piece in split3(value)
            )
            for owner in range(owners):
                out_ref[owner, pl.ds(each * j, each), :] = placed[each * owner : each * (owner + 1)]


def image(index, blocks, diagonal, row, near, far, past, step_tiles, owners=None, slots=None):
    count = diagonal.shape[0]
    whole = lambda shape: pl.BlockSpec(shape, lambda i, *_: (0,) * len(shape))
    extra = [] if owners is None else list(owners)
    operands = [diagonal, row, near, far, *past, *extra]
    if owners is None:
        outs = [jax.ShapeDtypeStruct(diagonal.shape, F32), jax.ShapeDtypeStruct((1, 128), F32)]
    else:
        outs = [jax.ShapeDtypeStruct(slots[0], F32), jax.ShapeDtypeStruct(slots[1], F32)]
    return pl.pallas_call(
        functools.partial(image_kernel, step_tiles, len(past), owners is not None),
        grid_spec=pltpu.PrefetchScalarGridSpec(
            num_scalar_prefetch=1,
            grid=(count // step_tiles,),
            in_specs=[pl.BlockSpec((step_tiles, 640, 128), lambda i, *_: (i, 0, 0))]
            + [whole(value.shape) for value in operands],
            out_specs=[whole(value.shape) for value in outs],
            scratch_shapes=[
                pltpu.VMEM((3 * count * 8, 128), F32),
                pltpu.VMEM((count * 8, 128), F32),
            ],
        ),
        out_shape=outs,
        name="image",
    )(index, blocks, *operands)


def coefficients(totals):
    lane = lax.broadcasted_iota(jnp.int32, (1, 128), 1)
    gram = {}
    for (i, j), place in PAIRS.items():
        value = jnp.sum(jnp.where(lane == place, totals, 0.0), axis=1, keepdims=True)
        gram[i, j] = gram[j, i] = value

    def dot(a, b):
        return sum(x * sum(gram[i, j] * y for j, y in enumerate(b)) for i, x in enumerate(a))

    one = jnp.ones((1, 1), F32)
    zero = jnp.zeros((1, 1), F32)
    solution, residual, direction = [], [one], [one]
    norm = gram[0, 0]
    for iteration in range(ITERS):
        padded = direction + [zero]
        product = [SHIFT * value for value in padded]
        product = [value + (padded[j - 1] if j else zero) for j, value in enumerate(product)]
        step = norm / dot(direction, product)
        solution = [a + step * b for a, b in zip(solution + [zero], direction)]
        residual = [a - step * b for a, b in zip(residual + [zero], product)]
        if iteration < ITERS - 1:
            following = dot(residual, residual)
            direction = [a + (following / norm) * b for a, b in zip(residual, padded)]
            norm = following
    return solution, residual


def finish_kernel(arrived_ref, totals_ref, solution_ref, residual_ref):
    solution, residual = coefficients(jnp.sum(totals_ref[...], axis=0, keepdims=True))
    owners, rows_each, _ = arrived_ref.shape
    each = rows_each // 4
    for owner in range(owners):
        basis = [arrived_ref[owner, pl.ds(each * j, each), :] for j in range(4)]
        place = pl.ds(each * owner, each)
        solution_ref[place, :] = sum(a * v for a, v in zip(solution, basis))
        residual_ref[place, :] = sum(a * v for a, v in zip(residual, basis))


def local(positions, charges, drag, right_side, neighbours, owners):
    count = positions.shape[0]
    brick_count = lax.axis_size("brick")
    slab_count = lax.axis_size("slab")
    devices = brick_count * slab_count
    each = max(3, 3 * count // brick_count)
    slab_at = lax.axis_index("slab")
    first_tile = (lax.axis_index("brick") * slab_count + slab_at) * count
    inner = [(i, i ^ 1) for i in range(slab_count)]
    outer = [(i, i + 1) for i in range(1, slab_count - 1, 2)]
    outer = outer + [(target, source) for source, target in outer]

    packed = pl.pallas_call(
        pack_kernel,
        out_shape=jax.ShapeDtypeStruct((5 * count, 128), F32),
        in_specs=[VMEM] * 3,
        out_specs=VMEM,
        name="pack",
    )(positions, charges, right_side)

    offset = neighbours - first_tile
    layer = jnp.floor_divide(offset, count)
    partner = 1 - 2 * (slab_at % 2)
    part = jnp.where(layer == 0, 0, jnp.where(layer == partner, 1, 2))
    index = (offset - layer * count + part * count).reshape(-1)

    def both_sides(value):
        far = lax.ppermute(value, "slab", outer)
        near = lax.ppermute(value, "slab", inner)
        return near, far

    scale = 8.0 / ((neighbours.shape[1] + 1) * 128)
    near, far = both_sides(packed)
    blocks, first, diagonal, row = weights(index, packed, near, far, drag, scale, 16)
    near, far = both_sides(first)
    second, row = image(index, blocks, diagonal, row, near, far, [right_side, first], 16)
    near, far = both_sides(second)
    outgoing, totals = image(
        index,
        blocks,
        diagonal,
        row,
        near,
        far,
        [right_side, first, second],
        16,
        owners=(owners, owners.reshape(1, count)),
        slots=((brick_count, 4 * each, 128), (devices, 128)),
    )
    arrived = lax.all_to_all(outgoing, "brick", split_axis=0, concat_axis=0, tiled=True)
    totals = lax.all_to_all(
        totals.reshape(devices, 1, 128), BOTH, split_axis=0, concat_axis=0, tiled=True
    )
    shape = jax.ShapeDtypeStruct((brick_count * each, 128), F32)
    return pl.pallas_call(
        finish_kernel,
        out_shape=(shape, shape),
        in_specs=[VMEM] * 2,
        out_specs=(VMEM, VMEM),
        name="finish",
    )(arrived, totals.reshape(devices, 128))


def solution(mesh):
    placed = (
        P(BOTH, None, None),
        P(BOTH, None),
        P(BOTH, None),
        P(BOTH, None),
        P(BOTH, None),
        P(BOTH, None),
    )
    return jax.shard_map(
        local,
        mesh=mesh,
        in_specs=placed,
        out_specs=(P(BOTH, None), P(BOTH, None)),
        check_vma=False,
    )
```

time: 483 us -> 213 us (0.44)
  blocking collectives: 341 us -> 39.8 us
  Pallas kernels: 0 us -> 148 us
  other arithmetic: 62.6 us -> 0.69 us
  matrix products: 32 us -> 0 us
  local copies, waits for them, and re-layouts: 18.5 us -> 6.01 us
  between operations: 7.76 us -> 0.68 us
    psum x5 -> x0, blocking collectives: 327 us -> none  [the longest x3 195 us: squares(): return lax.psum(jnp.sum(residual * residual), ('brick', 'slab'))]
    pallas_call x0 -> x5, Pallas kernels: none -> 148 us  [the longest x1 112 us: weights(): pl.pallas_call(functools.partial(weights_kernel, scale, step_tiles), grid...]
    reduce_sum x11 -> x0, other arithmetic: 56.6 us -> none  [the longest x1 49.8 us: local(): diagonal = drag + jnp.sum(weights, axis=(1, 3))]
    dot_general x3 -> x0, matrix products: 32 us -> none  [apply_home(): jnp.einsum('tkac,tksc->ta', blocks, stacked[index_all], preferred_element...]
    all_to_all x0 -> x1, blocking collectives: none -> 21.7 us  [local(): lax.all_to_all(totals.reshape(devices, 1, 128), BOTH, split_axis=0, conca...]
    gather x6 -> x0, local copies, waits for them, and re-layouts: 13.4 us -> none  [the longest x3 8.41 us: apply_home(): stacked[index_all]]
    ppermute x8 -> x6, starting transfers between devices: 15.3 us -> 15.9 us  [the longest x3 13.9 us: both_sides(): near = lax.ppermute(value, 'slab', inner)]
  transfers between devices with their start and end apart: 8 -> 6, of which waited for: 2 -> 2; matrix products, arithmetic and copies ran while one was open for 2% -> 1% of each run, Pallas kernels for 0% -> 0%
where the time goes in v1:
time: 213 us
  Pallas kernels  148 us (69%)
  blocking collectives  39.8 us (19%)
  starting transfers between devices  15.9 us (7%)
  local copies, waits for them, and re-layouts  6.01 us (3%)
    pallas_call x1, Pallas kernels, weights(): pl.pallas_call(functools.partial(weights_kernel, scale, step_tiles), grid...  112 us
    pallas_call x2, Pallas kernels, image(): pl.pallas_call(functools.partial(image_kernel, step_tiles, len(past), own...  31.9 us
    all_to_all x1, blocking collectives, local(): lax.all_to_all(totals.reshape(devices, 1, 128), BOTH, split_axis=0, conca...  21.7 us
    all_to_all x1, blocking collectives, local(): lax.all_to_all(outgoing, 'brick', split_axis=0, concat_axis=0, tiled=True)  18.1 us
    ppermute x3, starting transfers between devices, both_sides(): near = lax.ppermute(value, 'slab', inner)  13.9 us
    unnamed x16, local copies, waits for them, and re-layouts  5.2 us
  transfers between devices with their start and end apart: 6, of which 2 were waited for; matrix products, arithmetic and copies ran while one was open for 1% of the time, Pallas kernels for 0%

profile of v1, /device:TPU:0, one launch (start us, length us, event | category | flops | bytes accessed | tf_op | source)
XLA Modules:
  0.0 212.7 jit_solution(3578184020909187601)
XLA Ops:
  0.6 1.8 copy.14.pos_ref
  2.4 1.9 pack.1.own_ref
  4.3 0.7 collective-permute-start.1
  5.0 3.5 %collective-permute-start = (f32[640,128]{1,0:T(8,128)}, f32[640,128]{1,0:T(8,128)S(1)}, u32[]{:S(2)}, u32[]{:S(2)}) collective-permute-start(f32[640,128]{1,0:T(8,128)} %pack.1.own_ref), channel_id=1, source_target_pairs={{0,1},{1,0},{2,3},{3,2},{4,5},{5,4},{6,7},{7,6},{8,9},{9,8},{10,11... | collective-permute-start | bytes 983048 | tf_op jit(solution)/shard_map/ppermute | solution.py:340
  8.4 0.7 multiply_add_fusion
  9.2 0.7 reshape.16.index_ref
  9.9 0.7 copy-done
  10.6 0.7 copy-done.1
  11.4 112.2 %weights.1 = (bf16[128,640,128]{2,1,0:T(8,128)(2,1)}, f32[128,128]{1,0:T(8,128)}, f32[128,128]{1,0:T(8,128)}, f32[1,128]{1,0:T(1,128)}) custom-call(s32[512]{0:T(512)} %reshape.16.index_ref, f32[640,128]{1,0:T(8,128)} %pack.1.own_ref, f32[640,128]{1,0:T(8,128)} %copy-done.1, f32[640,128]{1,0:T(8,128)} %copy-done, f32[128,128]{1,0:T(8,128)} %drag_ref.1), custom_call_target="tpu_custom_call" | custom-call | tf_op jit(solution)/shard_map/weights/pallas_call | solution.py:152
  123.6 0.7 collective-permute-start.3
  124.3 6.4 %collective-permute-start.2 = (f32[128,128]{1,0:T(8,128)}, f32[128,128]{1,0:T(8,128)S(1)}, u32[]{:S(2)}, u32[]{:S(2)}) collective-permute-start(f32[128,128]{1,0:T(8,128)} %get-tuple-element.13.refs_1_), channel_id=1, source_target_pairs={{0,1},{1,0},{2,3},{3,2},{4,5},{5,4},{6,7},{7,6},{8,9},{9,8},{10,11... | collective-permute-start | bytes 196616 | tf_op jit(solution)/shard_map/ppermute | solution.py:340
  130.7 1.1 collective-permute-done.2.near_ref
  131.8 0.6 copy-done.5
  132.4 15.6 %image.2 = (f32[128,128]{1,0:T(8,128)}, f32[1,128]{1,0:T(1,128)}) custom-call(s32[512]{0:T(512)} %reshape.16.index_ref, bf16[128,640,128]{2,1,0:T(8,128)(2,1)} %get-tuple-element.10.blocks_ref, f32[128,128]{1,0:T(8,128)} %get-tuple-element.11.diagonal_ref, f32[1,128]{1,0:T(1,128)} %get-tuple-element.12.row_ref, f32[128,128]{1,0:T(8,128)} %copy-done.5, ...), custom_call_target="tpu_custom_call" | custom-call | tf_op jit(solution)/shard_map/image/pallas_call | solution.py:255
  148.0 0.7 collective-permute-start.5
  148.7 4.0 %collective-permute-start.4 = (f32[128,128]{1,0:T(8,128)}, f32[128,128]{1,0:T(8,128)S(1)}, u32[]{:S(2)}, u32[]{:S(2)}) collective-permute-start(f32[128,128]{1,0:T(8,128)} %get-tuple-element.15.refs_2_), channel_id=1, source_target_pairs={{0,1},{1,0},{2,3},{3,2},{4,5},{5,4},{6,7},{7,6},{8,9},{9,8},{10,11... | collective-permute-start | bytes 196616 | tf_op jit(solution)/shard_map/ppermute | solution.py:340
  152.7 0.7 copy.15.refs_3_
  153.5 0.4 collective-permute-done.4.near_ref
  153.9 0.2 copy-done.2
  154.1 0.4 copy-done.3
  154.5 16.3 %image.3 = (f32[16,96,128]{2,1,0:T(8,128)}, f32[128,128]{1,0:T(8,128)}) custom-call(s32[512]{0:T(512)} %reshape.16.index_ref, bf16[128,640,128]{2,1,0:T(8,128)(2,1)} %get-tuple-element.10.blocks_ref, f32[128,128]{1,0:T(8,128)} %get-tuple-element.11.diagonal_ref, f32[1,128]{1,0:T(1,128)} %get-tuple-element.14.row_ref, f32[128,128]{1,0:T(8,128)} %copy-done.3, ...), custom_call_target="tpu_custom_call" | custom-call | tf_op jit(solution)/shard_map/image/pallas_call | solution.py:255
  170.8 21.7 %all_to_all.10 = f32[128,1,128]{2,1,0:T(1,128)} all-to-all(f32[128,1,128]{2,1,0:T(1,128)} %bitcast.6), channel_id=1, replica_groups=mesh['brick'=16,'slab'=8] {'brick','slab'}, dimensions={0} | all-to-all | bytes 131072 | tf_op jit(solution)/shard_map/all_to_all | solution.py:362
  192.5 18.1 %all_to_all.11.arrived_ref = f32[16,96,128]{2,1,0:T(8,128)} all-to-all(f32[16,96,128]{2,1,0:T(8,128)} %get-tuple-element.16), channel_id=1, replica_groups=mesh['brick'=16,'slab'=8] {'brick'}, dimensions={0} | all-to-all | bytes 1572864 | tf_op jit(solution)/shard_map/all_to_all | solution.py:361
  210.6 2.1 finish.1
  (14 shorter events, 0.1 us)
Async XLA Ops:
  0.6 152.1 %copy-start.6 = (s32[128,1]{0,1:T(1,128)S(1)}, s32[128,1]{0,1:T(1,128)}, u32[]{:S(2)}) copy-start(s32[128,1]{0,1:T(1,128)} %param.11) | copy-start | bytes 1540
  4.3 5.6 %collective-permute-start.1 = (f32[640,128]{1,0:T(8,128)}, f32[640,128]{1,0:T(8,128)S(1)}, u32[]{:S(2)}, u32[]{:S(2)}) collective-permute-start(f32[640,128]{1,0:T(8,128)} %pack.1.own_ref), channel_id=1, source_target_pairs={{1,2},{3,4},{5,6},{2,1},{4,3},{6,5},{9,10},{11,12},{13,14},{10,9},... | collective-permute-start | bytes 983048 | tf_op jit(solution)/shard_map/ppermute | solution.py:339
  5.0 5.0 %collective-permute-start = (f32[640,128]{1,0:T(8,128)}, f32[640,128]{1,0:T(8,128)S(1)}, u32[]{:S(2)}, u32[]{:S(2)}) collective-permute-start(f32[640,128]{1,0:T(8,128)} %pack.1.own_ref), channel_id=1, source_target_pairs={{0,1},{1,0},{2,3},{3,2},{4,5},{5,4},{6,7},{7,6},{8,9},{9,8},{10,11... | collective-permute-start | bytes 983048 | tf_op jit(solution)/shard_map/ppermute | solution.py:340
  9.9 0.7 copy-start
  10.6 0.7 copy-start.1
  123.6 7.1 %collective-permute-start.3 = (f32[128,128]{1,0:T(8,128)}, f32[128,128]{1,0:T(8,128)S(1)}, u32[]{:S(2)}, u32[]{:S(2)}) collective-permute-start(f32[128,128]{1,0:T(8,128)} %get-tuple-element.13.refs_1_), channel_id=1, source_target_pairs={{1,2},{3,4},{5,6},{2,1},{4,3},{6,5},{9,10},{11,12},{13,14},{10,9},... | collective-permute-start | bytes 196616 | tf_op jit(solution)/shard_map/ppermute | solution.py:339
  124.3 7.5 %collective-permute-start.2 = (f32[128,128]{1,0:T(8,128)}, f32[128,128]{1,0:T(8,128)S(1)}, u32[]{:S(2)}, u32[]{:S(2)}) collective-permute-start(f32[128,128]{1,0:T(8,128)} %get-tuple-element.13.refs_1_), channel_id=1, source_target_pairs={{0,1},{1,0},{2,3},{3,2},{4,5},{5,4},{6,7},{7,6},{8,9},{9,8},{10,11... | collective-permute-start | bytes 196616 | tf_op jit(solution)/shard_map/ppermute | solution.py:340
  130.7 1.1 copy-start.4
  131.8 0.6 copy-start.5
  148.0 5.4 %collective-permute-start.5 = (f32[128,128]{1,0:T(8,128)}, f32[128,128]{1,0:T(8,128)S(1)}, u32[]{:S(2)}, u32[]{:S(2)}) collective-permute-start(f32[128,128]{1,0:T(8,128)} %get-tuple-element.15.refs_2_), channel_id=1, source_target_pairs={{1,2},{3,4},{5,6},{2,1},{4,3},{6,5},{9,10},{11,12},{13,14},{10,9},... | collective-permute-start | bytes 196616 | tf_op jit(solution)/shard_map/ppermute | solution.py:339
  148.7 5.1 %collective-permute-start.4 = (f32[128,128]{1,0:T(8,128)}, f32[128,128]{1,0:T(8,128)S(1)}, u32[]{:S(2)}, u32[]{:S(2)}) collective-permute-start(f32[128,128]{1,0:T(8,128)} %get-tuple-element.15.refs_2_), channel_id=1, source_target_pairs={{0,1},{1,0},{2,3},{3,2},{4,5},{5,4},{6,7},{7,6},{8,9},{9,8},{10,11... | collective-permute-start | bytes 196616 | tf_op jit(solution)/shard_map/ppermute | solution.py:340
  153.5 0.6 copy-start.2
  153.9 0.6 copy-start.3

commit v2 on v1

v2 whole, which is shorter than its diff:
```python
import functools

import jax
import jax.numpy as jnp
from jax import lax
from jax.experimental import pallas as pl
from jax.experimental.pallas import tpu as pltpu
from jax.sharding import PartitionSpec as P

ITERS = 3
SHIFT = 7.0
MIX = 6
UNROLL = 4
LOG2E = 1.4426950408889634
F32 = jnp.float32
BF16 = jnp.bfloat16
BOTH = ("brick", "slab")
PAIRS = {
    (0, 0): 0,
    (0, 1): 1,
    (1, 1): 2,
    (0, 2): 3,
    (1, 2): 4,
    (2, 2): 5,
    (0, 3): 6,
    (1, 3): 7,
    (2, 3): 8,
}
VMEM = pl.BlockSpec(memory_space=pltpu.VMEM)
SMEM = pl.BlockSpec(memory_space=pltpu.SMEM)
LIMIT = 12 << 20


def split3(value):
    high = value.astype(BF16)
    rest = value - high.astype(F32)
    middle = rest.astype(BF16)
    low = (rest - middle.astype(F32)).astype(BF16)
    return high, middle, low


def split2(value):
    high = value.astype(BF16).astype(F32)
    low = (value - high).astype(BF16).astype(F32)
    return high, low


def rows_at(ref, row, count):
    return ref[pl.ds(row, count, stride=8), :]


def put_rows(ref, row, value):
    ref[pl.ds(row, value.shape[0], stride=8), :] = value


def add_dots(row, vectors):
    lane = lax.broadcasted_iota(jnp.int32, (1, 128), 1)
    newest = len(vectors) - 1
    for (i, j), place in PAIRS.items():
        if j == newest or (newest == 1 and j == 0):
            product = vectors[i] * vectors[j]
            total = jnp.sum(jnp.sum(product, axis=0, keepdims=True), axis=1, keepdims=True)
            row = row + jnp.where(lane == place, total, 0.0)
    return row


def pack_kernel(pos_ref, charge_ref, force_ref, out_ref):
    count = charge_ref.shape[0]
    for j in range(3):
        out_ref[pl.ds(j * count, count), :] = pos_ref[:, j, :] - 2.0
    out_ref[pl.ds(3 * count, count), :] = jnp.log2(charge_ref[...])
    out_ref[pl.ds(4 * count, count), :] = force_ref[...]


def weights_kernel(
    scale, index_ref, own_ref, near_ref, far_ref, drag_ref,
    blocks_ref, vector_ref, diagonal_ref, row_ref, raw, mine, sums, images, even, odd,
):
    count = drag_ref.shape[0]
    square = LOG2E * LOG2E

    one = jnp.ones((count, 128), F32)
    zero = jnp.zeros((count, 128), F32)
    for part, ref in enumerate((own_ref, near_ref, far_ref)):
        base = part * count * 8
        x, y, z, charge, force = (ref[pl.ds(j * count, count), :] for j in range(5))
        norm = x * x + y * y + z * z
        high, low = split2(force)
        for j, value in enumerate((x, y, z, charge, norm, one, high, low)):
            put_rows(raw, base + j, value)
        if part == 0:
            doubled = (-2.0 * square) * x, (-2.0 * square) * y, (-2.0 * square) * z
            rows = (*doubled, zero, one * square, (norm + 0.5) * square, zero, zero)
            rows += (zero, zero, zero, one, zero, charge + jnp.log2(scale * one), zero, zero)
            for j, value in enumerate(rows):
                mine[pl.ds(j, count, stride=16), :] = value

    def other(t, k):
        return t if k == 0 else index_ref[t * 4 + k - 1]

    def terms(t):
        rights = []
        for j in range(2):
            high, middle, low = split3(mine[pl.ds(pl.multiple_of(t * 16 + 8 * j, 8), 8), :])
            rights.append(jnp.concatenate([high, middle, low, high, middle, high], axis=0))
        right = jnp.concatenate(rights, axis=1)
        lefts = []
        for k in range(5):
            u = other(t, k)
            high, middle, low = split3(raw[pl.ds(pl.multiple_of(u * 8, 8), 8), :])
            lefts.append(jnp.concatenate([high, high, high, middle, middle, low], axis=0))
        left = jnp.concatenate(lefts, axis=1)
        return lax.dot_general(
            left, right, (((0,), (0,)), ((), ())), preferred_element_type=F32
        )

    def block(t, source, incoming):
        totals = [None] * 4
        for pair in range(40):
            halves = []
            for half in range(2):
                chunk = 2 * pair + half
                place = pl.ds(8 * chunk, 8)
                wide = source[place, :128]
                shifted = wide - 0.49 * square
                if chunk % MIX == MIX - 1:
                    distance = shifted * lax.rsqrt(shifted)
                    inverse = pltpu.reciprocal(wide)
                else:
                    product = wide * shifted
                    root = lax.rsqrt(product * wide)
                    distance = product * root
                    inverse = root * distance
                weight = inverse * (square * scale) + jnp.exp2(source[place, 128:] - distance)
                if chunk < 16:
                    rows = lax.broadcasted_iota(jnp.int32, (8, 128), 0) + 8 * chunk
                    lanes = lax.broadcasted_iota(jnp.int32, (8, 128), 1)
                    weight = jnp.where(rows == lanes, 0.0, weight)
                past = totals[chunk % 4]
                totals[chunk % 4] = weight if past is None else past + weight
                halves.append(weight)
            blocks_ref[t, pl.ds(16 * pair, 16), :] = jnp.concatenate(halves, axis=0).astype(BF16)
            source[pl.ds(16 * pair, 16), :] = incoming[16 * pair : 16 * pair + 16]
        total = (totals[0] + totals[1]) + (totals[2] + totals[3])
        sums[pl.ds(pl.multiple_of(t * 8, 8), 8), :] = total

    def image(t):
        lefts = []
        for k in range(5):
            u = other(t, k)
            lefts.append(raw[pl.ds(pl.multiple_of(u * 8, 8), 8), :].astype(BF16))
        images[pl.ds(pl.multiple_of(t * 8, 8), 8), :] = jnp.dot(
            jnp.concatenate(lefts, axis=1), blocks_ref[t], preferred_element_type=F32
        )

    even[...] = terms(0)
    odd[...] = terms(1)

    def pair(j, carry):
        t = 2 * j
        image(jnp.maximum(t - 2, 0))
        image(jnp.maximum(t - 1, 0))
        block(t, even, terms(jnp.minimum(t + 2, count - 1)))
        block(t + 1, odd, terms(jnp.minimum(t + 3, count - 1)))
        return carry

    lax.fori_loop(0, count // 2, pair, 0)
    image(count - 2)
    image(count - 1)

    diagonal = drag_ref[...]
    for j in range(8):
        diagonal = diagonal + rows_at(sums, j, count)
    coupled = rows_at(images, 6, count) + rows_at(images, 7, count)
    force = own_ref[pl.ds(4 * count, count), :]
    vector = (diagonal - SHIFT) * force - coupled
    diagonal_ref[...] = diagonal
    vector_ref[...] = vector
    row_ref[...] = add_dots(jnp.zeros((1, 128), F32), [force, vector])


def weights(index, own, near, far, drag, scale):
    count = drag.shape[0]
    return pl.pallas_call(
        functools.partial(weights_kernel, scale),
        in_specs=[SMEM] + [VMEM] * 4,
        out_specs=[VMEM] * 4,
        out_shape=[
            pltpu.VMEM((count, 640, 128), BF16),
            jax.ShapeDtypeStruct(drag.shape, F32),
            jax.ShapeDtypeStruct(drag.shape, F32),
            jax.ShapeDtypeStruct((1, 128), F32),
        ],
        scratch_shapes=[
            pltpu.VMEM((3 * count * 8, 128), F32),
            pltpu.VMEM((count * 16, 128), F32),
            pltpu.VMEM((count * 8, 128), F32),
            pltpu.VMEM((count * 8, 128), F32),
            pltpu.VMEM((640, 256), F32),
            pltpu.VMEM((640, 256), F32),
        ],
        compiler_params=pltpu.CompilerParams(vmem_limit_bytes=LIMIT),
        name="weights",
    )(index, own, near, far, drag)


def image_kernel(history, slots, index_ref, blocks_ref, diagonal_ref, row_ref, near_ref, far_ref, *refs):
    past, refs = refs[:history], refs[history:]
    if slots:
        owner_column, owner_row, out_ref, totals_ref, parts, images = refs
    else:
        vector_ref, totals_ref, parts, images = refs
    count = diagonal_ref.shape[0]
    for part, ref in enumerate((past[-1], near_ref, far_ref)):
        high, low = split2(ref[...])
        put_rows(parts, part * count * 8, high)
        put_rows(parts, part * count * 8 + 1, low)

    def tile(t, carry):
        lefts = []
        for k in range(5):
            u = t if k == 0 else index_ref[t * 4 + k - 1]
            lefts.append(parts[pl.ds(pl.multiple_of(u * 8, 8), 8), :].astype(BF16))
        left = jnp.concatenate(lefts, axis=1)
        images[pl.ds(pl.multiple_of(t * 8, 8), 8), :] = jnp.dot(
            left, blocks_ref[t], preferred_element_type=F32
        )
        return carry

    lax.fori_loop(0, count, tile, 0, unroll=UNROLL)

    coupled = rows_at(images, 0, count) + rows_at(images, 1, count)
    vectors = [ref[...] for ref in past]
    vector = (diagonal_ref[...] - SHIFT) * vectors[-1] - coupled
    vectors.append(vector)
    row = add_dots(row_ref[...], vectors)
    if not slots:
        vector_ref[...] = vector
        totals_ref[...] = row
        return
    totals_ref[...] = jnp.broadcast_to(row, totals_ref.shape)
    owners, rows_each, _ = out_ref.shape
    each = rows_each // 4
    earlier = lax.broadcasted_iota(jnp.int32, (count, count), 0) < lax.broadcasted_iota(
        jnp.int32, (count, count), 1
    )
    matching = (owner_column[...] == owner_row[...]) & earlier
    position = jnp.sum(matching.astype(jnp.int32), axis=0, keepdims=True)
    target = owner_row[...] * each + position
    slot = lax.broadcasted_iota(jnp.int32, (owners * each, count), 0)
    chosen = (slot == target).astype(F32).astype(BF16)
    for j, value in enumerate(vectors):
        placed = sum(jnp.dot(chosen, piece, preferred_element_type=F32) for piece in split3(value))
        for owner in range(owners):
            out_ref[owner, pl.ds(each * j, each), :] = placed[each * owner : each * (owner + 1)]


def image(index, blocks, diagonal, row, near, far, past, owners=None, slots=None):
    count = diagonal.shape[0]
    extra = [] if owners is None else list(owners)
    operands = [blocks, diagonal, row, near, far, *past, *extra]
    if owners is None:
        outs = [jax.ShapeDtypeStruct(diagonal.shape, F32), jax.ShapeDtypeStruct((1, 128), F32)]
    else:
        outs = [jax.ShapeDtypeStruct(shape, F32) for shape in slots]
    return pl.pallas_call(
        functools.partial(image_kernel, len(past), owners is not None),
        in_specs=[SMEM] + [VMEM] * len(operands),
        out_specs=[VMEM] * len(outs),
        out_shape=outs,
        scratch_shapes=[
            pltpu.VMEM((3 * count * 8, 128), F32),
            pltpu.VMEM((count * 8, 128), F32),
        ],
        compiler_params=pltpu.CompilerParams(vmem_limit_bytes=LIMIT),
        name="image",
    )(index, *operands)


def coefficients(totals):
    lane = lax.broadcasted_iota(jnp.int32, (1, 128), 1)
    gram = {}
    for (i, j), place in PAIRS.items():
        value = jnp.sum(jnp.where(lane == place, totals, 0.0), axis=1, keepdims=True)
        gram[i, j] = gram[j, i] = value

    def dot(a, b):
        return sum(x * sum(gram[i, j] * y for j, y in enumerate(b)) for i, x in enumerate(a))

    one = jnp.ones((1, 1), F32)
    zero = jnp.zeros((1, 1), F32)
    solution, residual, direction = [], [one], [one]
    norm = gram[0, 0]
    for iteration in range(ITERS):
        padded = direction + [zero]
        product = [SHIFT * value for value in padded]
        product = [value + (padded[j - 1] if j else zero) for j, value in enumerate(product)]
        step = norm / dot(direction, product)
        solution = [a + step * b for a, b in zip(solution + [zero], direction)]
        residual = [a - step * b for a, b in zip(residual + [zero], product)]
        if iteration < ITERS - 1:
            following = dot(residual, residual)
            direction = [a + (following / norm) * b for a, b in zip(residual, padded)]
            norm = following
    return solution, residual


def finish_kernel(arrived_ref, totals_ref, solution_ref, residual_ref):
    solution, residual = coefficients(jnp.sum(totals_ref[...], axis=0, keepdims=True))
    owners, rows_each, _ = arrived_ref.shape
    each = rows_each // 4
    for owner in range(owners):
        basis = [arrived_ref[owner, pl.ds(each * j, each), :] for j in range(4)]
        place = pl.ds(each * owner, each)
        solution_ref[place, :] = sum(a * v for a, v in zip(solution, basis))
        residual_ref[place, :] = sum(a * v for a, v in zip(residual, basis))


def local(positions, charges, drag, right_side, neighbours, owners):
    count = positions.shape[0]
    brick_count = lax.axis_size("brick")
    slab_count = lax.axis_size("slab")
    devices = brick_count * slab_count
    each = max(3, 3 * count // brick_count)
    slab_at = lax.axis_index("slab")
    first_tile = (lax.axis_index("brick") * slab_count + slab_at) * count
    inner = [(i, i ^ 1) for i in range(slab_count)]
    outer = [(i, i + 1) for i in range(1, slab_count - 1, 2)]
    outer = outer + [(target, source) for source, target in outer]

    packed = pl.pallas_call(
        pack_kernel,
        out_shape=jax.ShapeDtypeStruct((5 * count, 128), F32),
        in_specs=[VMEM] * 3,
        out_specs=VMEM,
        compiler_params=pltpu.CompilerParams(vmem_limit_bytes=LIMIT),
        name="pack",
    )(positions, charges, right_side)

    offset = neighbours - first_tile
    layer = jnp.floor_divide(offset, count)
    partner = 1 - 2 * (slab_at % 2)
    part = jnp.where(layer == 0, 0, jnp.where(layer == partner, 1, 2))
    index = (offset - layer * count + part * count).reshape(-1)

    def both_sides(value):
        far = lax.ppermute(value, "slab", outer)
        near = lax.ppermute(value, "slab", inner)
        return near, far

    scale = 8.0 / ((neighbours.shape[1] + 1) * 128)
    near, far = both_sides(packed)
    blocks, first, diagonal, row = weights(index, packed, near, far, drag, scale)
    near, far = both_sides(first)
    second, row = image(index, blocks, diagonal, row, near, far, [right_side, first])
    near, far = both_sides(second)
    outgoing, totals = image(
        index,
        blocks,
        diagonal,
        row,
        near,
        far,
        [right_side, first, second],
        owners=(owners, owners.reshape(1, count)),
        slots=((brick_count, 4 * each, 128), (devices, 128)),
    )
    arrived = lax.all_to_all(outgoing, "brick", split_axis=0, concat_axis=0, tiled=True)
    totals = lax.all_to_all(
        totals.reshape(devices, 1, 128), BOTH, split_axis=0, concat_axis=0, tiled=True
    )
    shape = jax.ShapeDtypeStruct((brick_count * each, 128), F32)
    return pl.pallas_call(
        finish_kernel,
        out_shape=(shape, shape),
        in_specs=[VMEM] * 2,
        out_specs=(VMEM, VMEM),
        compiler_params=pltpu.CompilerParams(vmem_limit_bytes=LIMIT),
        name="finish",
    )(arrived, totals.reshape(devices, 128))


def solution(mesh):
    placed = (
        P(BOTH, None, None),
        P(BOTH, None),
        P(BOTH, None),
        P(BOTH, None),
        P(BOTH, None),
        P(BOTH, None),
    )
    return jax.shard_map(
        local,
        mesh=mesh,
        in_specs=placed,
        out_specs=(P(BOTH, None), P(BOTH, None)),
        check_vma=False,
    )
```

time: 213 us -> 121 us (0.57)
  Pallas kernels: 148 us -> 44.3 us
  local copies, waits for them, and re-layouts: 6.01 us -> 18.7 us
    pallas_call x3, Pallas kernels: 144 us -> 43.2 us  [the longest x1 26.9 us: weights(): pl.pallas_call(functools.partial(weights_kernel, scale), in_specs=[SMEM]...]
    unnamed x16 -> x18, local copies, waits for them, and re-layouts: 5.2 us -> 18.5 us
  transfers between devices with their start and end apart: 6 -> 6, of which waited for: 2 -> 3; matrix products, arithmetic and copies ran while one was open for 1% -> 1% of each run, Pallas kernels for 0% -> 0%
where the time goes in v2:
time: 121 us; the launch traced here: 120 us
  Pallas kernels  44.3 us (37%)
  blocking collectives  38 us (31%)
  local copies, waits for them, and re-layouts  18.7 us (15%)
  starting transfers between devices  15.9 us (13%)
  waiting for transfers between devices  2.02 us (2%)
    pallas_call x1, Pallas kernels, weights(): pl.pallas_call(functools.partial(weights_kernel, scale), in_specs=[SMEM]...  26.9 us
    all_to_all x1, blocking collectives, local(): lax.all_to_all(totals.reshape(devices, 1, 128), BOTH, split_axis=0, conca...  21 us
    unnamed x18, local copies, waits for them, and re-layouts  18.5 us
    all_to_all x1, blocking collectives, local(): lax.all_to_all(outgoing, 'brick', split_axis=0, concat_axis=0, tiled=True)  17 us
    pallas_call x2, Pallas kernels, image(): pl.pallas_call(functools.partial(image_kernel, len(past), owners is not N...  16.3 us
    ppermute x3, starting transfers between devices, both_sides(): near = lax.ppermute(value, 'slab', inner)  13.9 us
  transfers between devices with their start and end apart: 6, of which 3 were waited for; matrix products, arithmetic and copies ran while one was open for 1% of the time, Pallas kernels for 0%

profile of v2, /device:TPU:0, one launch (start us, length us, event | category | flops | bytes accessed | tf_op | source)
XLA Modules:
  0.0 120.4 jit_solution(16575955678019181297)
XLA Ops:
  0.7 1.1 copy.14.pos_ref
  1.8 0.8 copy-done.2
  2.6 0.8 copy-done.6
  3.4 0.2 pack.1.own_ref
  3.6 0.7 collective-permute-start.1
  4.3 3.5 %collective-permute-start = (f32[640,128]{1,0:T(8,128)S(1)}, f32[640,128]{1,0:T(8,128)S(1)}, u32[]{:S(2)}, u32[]{:S(2)}) collective-permute-start(f32[640,128]{1,0:T(8,128)S(1)} %pack.1.own_ref), channel_id=1, source_target_pairs={{0,1},{1,0},{2,3},{3,2},{4,5},{5,4},{6,7},{7,6},{8,9},{9,8},{10,11... | collective-permute-start | bytes 983048 | tf_op jit(solution)/shard_map/ppermute | solution.py:348
  7.7 0.7 multiply_add_fusion
  8.7 0.3 collective-permute-done.near_ref
  9.0 0.8 copy-done.5
  9.8 26.9 %weights.1 = (bf16[128,640,128]{2,1,0:T(8,128)(2,1)S(1)}, f32[128,128]{1,0:T(8,128)S(1)}, f32[128,128]{1,0:T(8,128)S(1)}, f32[1,128]{1,0:T(1,128)S(1)}) custom-call(s32[512]{0:T(512)S(1)} %reshape.16.index_ref, f32[640,128]{1,0:T(8,128)S(1)} %pack.1.own_ref, f32[640,128]{1,0:T(8,128)S(1)} %collective-permute-done.near_ref, ...), custom_call_target="tpu_custom_call" | custom-call | tf_op jit(solution)/shard_map/weights/pallas_call | solution.py:184
  36.7 0.7 collective-permute-start.3
  37.4 6.5 %collective-permute-start.2 = (f32[128,128]{1,0:T(8,128)S(1)}, f32[128,128]{1,0:T(8,128)S(1)}, u32[]{:S(2)}, u32[]{:S(2)}) collective-permute-start(f32[128,128]{1,0:T(8,128)S(1)} %get-tuple-element.13.refs_1_), channel_id=1, source_target_pairs={{0,1},{1,0},{2,3},{3,2},{4,5},{5,4},{6,7},{7,6},{8,9},{9,8},{10,11... | collective-permute-start | bytes 196616 | tf_op jit(solution)/shard_map/ppermute | solution.py:348
  43.9 0.9 collective-permute-done.2.near_ref
  44.8 0.8 copy-done.3
  45.6 8.0 %image.2 = (f32[128,128]{1,0:T(8,128)S(1)}, f32[1,128]{1,0:T(1,128)S(1)}) custom-call(s32[512]{0:T(512)S(1)} %reshape.16.index_ref, bf16[128,640,128]{2,1,0:T(8,128)(2,1)S(1)} %get-tuple-element.10.blocks_ref, f32[128,128]{1,0:T(8,128)S(1)} %get-tuple-element.11.diagonal_ref, f32[1,128]{1,0:T(1,128)S(1)} %get-tuple-element.12.row_ref, ...), custom_call_target="tpu_custom_call" | custom-call | tf_op jit(solution)/shard_map/image/pallas_call | solution.py:266
  53.6 7.0 %copy-done = bf16[128,640,128]{2,1,0:T(8,128)(2,1)} copy-done((bf16[128,640,128]{2,1,0:T(8,128)(2,1)}, bf16[128,640,128]{2,1,0:T(8,128)(2,1)S(1)}, u32[]{:S(2)}) %copy-start) | copy-done | bytes 20971544
  60.5 0.7 collective-permute-start.5
  61.2 4.0 %collective-permute-start.4 = (f32[128,128]{1,0:T(8,128)S(1)}, f32[128,128]{1,0:T(8,128)S(1)}, u32[]{:S(2)}, u32[]{:S(2)}) collective-permute-start(f32[128,128]{1,0:T(8,128)S(1)} %get-tuple-element.15.refs_2_), channel_id=1, source_target_pairs={{0,1},{1,0},{2,3},{3,2},{4,5},{5,4},{6,7},{7,6},{8,9},{9,8},{10,11... | collective-permute-start | bytes 196616 | tf_op jit(solution)/shard_map/ppermute | solution.py:348
  65.3 0.8 collective-permute-done.4.near_ref
  66.1 7.0 %copy-done.1 = bf16[128,640,128]{2,1,0:T(8,128)(2,1)S(1)} copy-done((bf16[128,640,128]{2,1,0:T(8,128)(2,1)S(1)}, bf16[128,640,128]{2,1,0:T(8,128)(2,1)}, u32[]{:S(2)}) %copy-start.1) | copy-done | bytes 20971544
  73.1 8.3 %image.3 = (f32[16,96,128]{2,1,0:T(8,128)S(1)}, f32[128,128]{1,0:T(8,128)S(1)}) custom-call(s32[512]{0:T(512)S(1)} %reshape.16.index_ref, bf16[128,640,128]{2,1,0:T(8,128)(2,1)S(1)} %copy-done.1, f32[128,128]{1,0:T(8,128)S(1)} %get-tuple-element.11.diagonal_ref, f32[1,128]{1,0:T(1,128)S(1)} %get-tuple-element.14.row_ref, ...), custom_call_target="tpu_custom_call" | custom-call | tf_op jit(solution)/shard_map/image/pallas_call | solution.py:266
  81.4 21.0 %all_to_all.10 = f32[128,1,128]{2,1,0:T(1,128)S(1)} all-to-all(f32[128,1,128]{2,1,0:T(1,128)S(1)} %bitcast.6), channel_id=1, replica_groups=mesh['brick'=16,'slab'=8] {'brick','slab'}, dimensions={0} | all-to-all | bytes 131072 | tf_op jit(solution)/shard_map/all_to_all | solution.py:369
  102.4 17.0 %all_to_all.11.arrived_ref = f32[16,96,128]{2,1,0:T(8,128)S(1)} all-to-all(f32[16,96,128]{2,1,0:T(8,128)S(1)} %get-tuple-element.16), channel_id=1, replica_groups=mesh['brick'=16,'slab'=8] {'brick'}, dimensions={0} | all-to-all | bytes 1572864 | tf_op jit(solution)/shard_map/all_to_all | solution.py:368
  119.4 1.0 finish.1
  (16 shorter events, 0.4 us)
Async XLA Ops:
  0.6 65.5 %copy-start.4 = (f32[128,128]{1,0:T(8,128)S(1)}, f32[128,128]{1,0:T(8,128)}, u32[]{:S(2)}) copy-start(f32[128,128]{1,0:T(8,128)} %refs_0_.3) | copy-start | bytes 196612
  0.6 64.6 %copy-start.7 = (s32[128,1]{0,1:T(1,128)S(1)}, s32[128,1]{0,1:T(1,128)}, u32[]{:S(2)}) copy-start(s32[128,1]{0,1:T(1,128)} %param.11) | copy-start | bytes 1540
  1.8 0.8 copy-start.2
  2.6 0.8 copy-start.6
  3.6 5.1 %collective-permute-start.1 = (f32[640,128]{1,0:T(8,128)S(1)}, f32[640,128]{1,0:T(8,128)S(1)}, u32[]{:S(2)}, u32[]{:S(2)}) collective-permute-start(f32[640,128]{1,0:T(8,128)S(1)} %pack.1.own_ref), channel_id=1, source_target_pairs={{1,2},{3,4},{5,6},{2,1},{4,3},{6,5},{9,10},{11,12},{13,14},{10,9},... | collective-permute-start | bytes 983048 | tf_op jit(solution)/shard_map/ppermute | solution.py:347
  4.3 4.7 %collective-permute-start = (f32[640,128]{1,0:T(8,128)S(1)}, f32[640,128]{1,0:T(8,128)S(1)}, u32[]{:S(2)}, u32[]{:S(2)}) collective-permute-start(f32[640,128]{1,0:T(8,128)S(1)} %pack.1.own_ref), channel_id=1, source_target_pairs={{0,1},{1,0},{2,3},{3,2},{4,5},{5,4},{6,7},{7,6},{8,9},{9,8},{10,11... | collective-permute-start | bytes 983048 | tf_op jit(solution)/shard_map/ppermute | solution.py:348
  9.0 0.8 copy-start.5
  36.7 7.1 %collective-permute-start.3 = (f32[128,128]{1,0:T(8,128)S(1)}, f32[128,128]{1,0:T(8,128)S(1)}, u32[]{:S(2)}, u32[]{:S(2)}) collective-permute-start(f32[128,128]{1,0:T(8,128)S(1)} %get-tuple-element.13.refs_1_), channel_id=1, source_target_pairs={{1,2},{3,4},{5,6},{2,1},{4,3},{6,5},{9,10},{11,12},{13,14},{10,9},... | collective-permute-start | bytes 196616 | tf_op jit(solution)/shard_map/ppermute | solution.py:347
  37.4 7.4 %collective-permute-start.2 = (f32[128,128]{1,0:T(8,128)S(1)}, f32[128,128]{1,0:T(8,128)S(1)}, u32[]{:S(2)}, u32[]{:S(2)}) collective-permute-start(f32[128,128]{1,0:T(8,128)S(1)} %get-tuple-element.13.refs_1_), channel_id=1, source_target_pairs={{0,1},{1,0},{2,3},{3,2},{4,5},{5,4},{6,7},{7,6},{8,9},{9,8},{10,11... | collective-permute-start | bytes 196616 | tf_op jit(solution)/shard_map/ppermute | solution.py:348
  44.8 0.8 copy-start.3
  53.6 7.0 %copy-start = (bf16[128,640,128]{2,1,0:T(8,128)(2,1)}, bf16[128,640,128]{2,1,0:T(8,128)(2,1)S(1)}, u32[]{:S(2)}) copy-start(bf16[128,640,128]{2,1,0:T(8,128)(2,1)S(1)} %get-tuple-element.10.blocks_ref) | copy-start | bytes 62914564
  60.5 4.8 %collective-permute-start.5 = (f32[128,128]{1,0:T(8,128)S(1)}, f32[128,128]{1,0:T(8,128)S(1)}, u32[]{:S(2)}, u32[]{:S(2)}) collective-permute-start(f32[128,128]{1,0:T(8,128)S(1)} %get-tuple-element.15.refs_2_), channel_id=1, source_target_pairs={{1,2},{3,4},{5,6},{2,1},{4,3},{6,5},{9,10},{11,12},{13,14},{10,9},... | collective-permute-start | bytes 196616 | tf_op jit(solution)/shard_map/ppermute | solution.py:347
  61.2 4.9 %collective-permute-start.4 = (f32[128,128]{1,0:T(8,128)S(1)}, f32[128,128]{1,0:T(8,128)S(1)}, u32[]{:S(2)}, u32[]{:S(2)}) collective-permute-start(f32[128,128]{1,0:T(8,128)S(1)} %get-tuple-element.15.refs_2_), channel_id=1, source_target_pairs={{0,1},{1,0},{2,3},{3,2},{4,5},{5,4},{6,7},{7,6},{8,9},{9,8},{10,11... | collective-permute-start | bytes 196616 | tf_op jit(solution)/shard_map/ppermute | solution.py:348
  66.1 7.0 %copy-start.1 = (bf16[128,640,128]{2,1,0:T(8,128)(2,1)S(1)}, bf16[128,640,128]{2,1,0:T(8,128)(2,1)}, u32[]{:S(2)}) copy-start(bf16[128,640,128]{2,1,0:T(8,128)(2,1)} %copy-done) | copy-start | bytes 62914564

commit v3 on v2

v3 whole, which is shorter than its diff:
```python
import functools

import jax
import jax.numpy as jnp
from jax import lax
from jax.experimental import pallas as pl
from jax.experimental.pallas import tpu as pltpu
from jax.sharding import PartitionSpec as P

ITERS = 3
SHIFT = 7.0
MIX = 6
UNROLL = 4
LOG2E = 1.4426950408889634
F32 = jnp.float32
BF16 = jnp.bfloat16
BOTH = ("brick", "slab")
PAIRS = {
    (0, 0): 0,
    (0, 1): 1,
    (1, 1): 2,
    (0, 2): 3,
    (1, 2): 4,
    (2, 2): 5,
    (0, 3): 6,
    (1, 3): 7,
    (2, 3): 8,
}
VMEM = pl.BlockSpec(memory_space=pltpu.VMEM)
SMEM = pl.BlockSpec(memory_space=pltpu.SMEM)
HBM = pl.BlockSpec(memory_space=pltpu.HBM)
LIMIT = 12 << 20


def in_hbm(value):
    return pltpu.with_memory_space_constraint(value, pltpu.HBM)


def split3(value):
    high = value.astype(BF16)
    rest = value - high.astype(F32)
    middle = rest.astype(BF16)
    low = (rest - middle.astype(F32)).astype(BF16)
    return high, middle, low


def split2(value):
    high = value.astype(BF16).astype(F32)
    low = (value - high).astype(BF16).astype(F32)
    return high, low


def rows_at(ref, row, count):
    return ref[pl.ds(row, count, stride=8), :]


def put_rows(ref, row, value):
    ref[pl.ds(row, value.shape[0], stride=8), :] = value


def add_dots(row, vectors):
    lane = lax.broadcasted_iota(jnp.int32, (1, 128), 1)
    newest = len(vectors) - 1
    for (i, j), place in PAIRS.items():
        if j == newest or (newest == 1 and j == 0):
            product = vectors[i] * vectors[j]
            total = jnp.sum(jnp.sum(product, axis=0, keepdims=True), axis=1, keepdims=True)
            row = row + jnp.where(lane == place, total, 0.0)
    return row


def pack_kernel(each, pos_hbm, charge_hbm, force_hbm, owner_hbm, out_ref, target_ref, charge, owner, sems):
    count = charge.shape[0]
    copies = [
        pltpu.make_async_copy(source, target, sems.at[j])
        for j, (source, target) in enumerate(
            (
                (pos_hbm, out_ref.at[pl.ds(0, 3)]),
                (charge_hbm, charge),
                (force_hbm, out_ref.at[4]),
                (owner_hbm, owner),
            )
        )
    ]
    for copy in copies:
        copy.start()
    for copy in copies:
        copy.wait()
    out_ref[pl.ds(0, 3)] = out_ref[pl.ds(0, 3)] - 2.0
    out_ref[3] = jnp.log2(charge[...])
    owners = jnp.broadcast_to(owner[...].astype(F32), (count, count))
    earlier = lax.broadcasted_iota(jnp.int32, (count, count), 0) < lax.broadcasted_iota(
        jnp.int32, (count, count), 1
    )
    matching = jnp.where((owners.T == owners) & earlier, 1.0, 0.0)
    position = jnp.sum(matching, axis=0, keepdims=True).astype(jnp.int32)
    target_ref[...] = owner[...] * each + position


def weights_kernel(scale, first, blocks_count, index_ref, planes, blocks_ref, scratch, finish):
    raw, mine, sums, images, even, odd = scratch
    count = mine.shape[0] // 16
    square = LOG2E * LOG2E
    width = 128 * blocks_count
    one = jnp.ones((count, 128), F32)
    zero = jnp.zeros((count, 128), F32)
    for part, ref in enumerate(planes):
        base = part * count * 8
        x, y, z, charge, force = (ref[j] for j in range(5))
        norm = x * x + y * y + z * z
        high, low = split2(force)
        for j, value in enumerate((x, y, z, charge, norm, one, high, low)):
            put_rows(raw, base + j, value)
        if part == 0:
            doubled = (-2.0 * square) * x, (-2.0 * square) * y, (-2.0 * square) * z
            rows = (*doubled, zero, one * square, (norm + 0.5) * square, zero, zero)
            rows += (zero, zero, zero, one, zero, charge + jnp.log2(scale * one), zero, zero)
            for j, value in enumerate(rows):
                mine[pl.ds(j, count, stride=16), :] = value

    def entries(t):
        for k in range(blocks_count):
            u = t if first + k == 0 else index_ref[t * 4 + first + k - 1]
            yield raw[pl.ds(pl.multiple_of(u * 8, 8), 8), :]

    def terms(t):
        rights = []
        for j in range(2):
            high, middle, low = split3(mine[pl.ds(pl.multiple_of(t * 16 + 8 * j, 8), 8), :])
            rights.append(jnp.concatenate([high, middle, low, high, middle, high], axis=0))
        right = jnp.concatenate(rights, axis=1)
        lefts = []
        for value in entries(t):
            high, middle, low = split3(value)
            lefts.append(jnp.concatenate([high, high, high, middle, middle, low], axis=0))
        left = jnp.concatenate(lefts, axis=1)
        return lax.dot_general(
            left, right, (((0,), (0,)), ((), ())), preferred_element_type=F32
        )

    def block(t, source, incoming):
        totals = [None] * 4
        for pair in range(width // 16):
            halves = []
            for half in range(2):
                chunk = 2 * pair + half
                place = pl.ds(8 * chunk, 8)
                wide = source[place, :128]
                shifted = wide - 0.49 * square
                if chunk % MIX == MIX - 1:
                    distance = shifted * lax.rsqrt(shifted)
                    inverse = pltpu.reciprocal(wide)
                else:
                    product = wide * shifted
                    root = lax.rsqrt(product * wide)
                    distance = product * root
                    inverse = root * distance
                weight = inverse * (square * scale) + jnp.exp2(source[place, 128:] - distance)
                if first == 0 and chunk < 16:
                    rows = lax.broadcasted_iota(jnp.int32, (8, 128), 0) + 8 * chunk
                    lanes = lax.broadcasted_iota(jnp.int32, (8, 128), 1)
                    weight = jnp.where(rows == lanes, 0.0, weight)
                past = totals[chunk % 4]
                totals[chunk % 4] = weight if past is None else past + weight
                halves.append(weight)
            blocks_ref[t, pl.ds(16 * pair, 16), :] = jnp.concatenate(halves, axis=0).astype(BF16)
            source[pl.ds(16 * pair, 16), :] = incoming[16 * pair : 16 * pair + 16]
        total = (totals[0] + totals[1]) + (totals[2] + totals[3])
        sums[pl.ds(pl.multiple_of(t * 8, 8), 8), :] = total

    def image(t):
        left = jnp.concatenate([value.astype(BF16) for value in entries(t)], axis=1)
        images[pl.ds(pl.multiple_of(t * 8, 8), 8), :] = jnp.dot(
            left, blocks_ref[t], preferred_element_type=F32
        )

    even[...] = terms(0)
    odd[...] = terms(1)

    def pair(j, carry):
        t = 2 * j
        image(jnp.maximum(t - 2, 0))
        image(jnp.maximum(t - 1, 0))
        block(t, even, terms(jnp.minimum(t + 2, count - 1)))
        block(t + 1, odd, terms(jnp.minimum(t + 3, count - 1)))
        return carry

    lax.fori_loop(0, count // 2, pair, 0)
    image(count - 2)
    image(count - 1)
    total = rows_at(sums, 0, count)
    for j in range(1, 8):
        total = total + rows_at(sums, j, count)
    finish(total, rows_at(images, 6, count) + rows_at(images, 7, count))


def weights_scratch(count, parts, blocks_count):
    return [
        pltpu.VMEM((parts * count * 8, 128), F32),
        pltpu.VMEM((count * 16, 128), F32),
        pltpu.VMEM((count * 8, 128), F32),
        pltpu.VMEM((count * 8, 128), F32),
        pltpu.VMEM((128 * blocks_count, 256), F32),
        pltpu.VMEM((128 * blocks_count, 256), F32),
    ]


def own_kernel(scale, own_ref, blocks_ref, total_ref, image_ref, *scratch):
    def finish(total, coupled):
        total_ref[...] = total
        image_ref[...] = coupled

    weights_kernel(scale, 0, 1, None, [own_ref], blocks_ref, scratch, finish)


def own_weights(own, scale):
    count = own.shape[1]
    plane = jax.ShapeDtypeStruct((count, 128), F32)
    return pl.pallas_call(
        functools.partial(own_kernel, scale),
        in_specs=[VMEM],
        out_specs=[VMEM] * 3,
        out_shape=[pltpu.VMEM((count, 128, 128), BF16), plane, plane],
        scratch_shapes=weights_scratch(count, 1, 1),
        compiler_params=pltpu.CompilerParams(vmem_limit_bytes=LIMIT),
        cost_estimate=pl.CostEstimate(
            flops=count * 128 * 128 * 600, bytes_accessed=1 << 20, transcendentals=count * 128 * 256
        ),
        name="own_weights",
    )(own)


def other_kernel(
    scale, blocks_count, index_ref, own_ref, near_ref, far_ref, total_ref, image_ref, drag_hbm,
    blocks_ref, vector_ref, diagonal_ref, row_ref, drag, sem, *scratch,
):
    copy = pltpu.make_async_copy(drag_hbm, drag, sem)
    copy.start()

    def finish(total, coupled):
        copy.wait()
        diagonal = drag[...] + total_ref[...] + total
        force = own_ref[4]
        vector = (diagonal - SHIFT) * force - (image_ref[...] + coupled)
        diagonal_ref[...] = diagonal
        vector_ref[...] = vector
        row_ref[...] = add_dots(jnp.zeros((1, 128), F32), [force, vector])

    planes = [own_ref, near_ref, far_ref]
    weights_kernel(scale, 1, blocks_count, index_ref, planes, blocks_ref, scratch, finish)


def other_weights(index, own, near, far, total, image, drag, scale, blocks_count):
    count = drag.shape[0]
    plane = jax.ShapeDtypeStruct((count, 128), F32)
    return pl.pallas_call(
        functools.partial(other_kernel, scale, blocks_count),
        in_specs=[SMEM] + [VMEM] * 5 + [HBM],
        out_specs=[VMEM] * 4,
        out_shape=[
            pltpu.VMEM((count, 128 * blocks_count, 128), BF16),
            plane,
            plane,
            jax.ShapeDtypeStruct((1, 128), F32),
        ],
        scratch_shapes=[
            pltpu.VMEM((count, 128), F32),
            pltpu.SemaphoreType.DMA,
            *weights_scratch(count, 3, blocks_count),
        ],
        compiler_params=pltpu.CompilerParams(vmem_limit_bytes=LIMIT),
        name="other_weights",
    )(index, own, near, far, total, image, in_hbm(drag))


def image_kernel(
    history, index_ref, own_blocks, blocks_ref, diagonal_ref, row_ref, near_ref, far_ref, own_ref, *refs
):
    past, refs = [own_ref.at[4], *refs[:history]], refs[history:]
    vector_ref, totals_ref, parts, images = refs
    count = diagonal_ref.shape[0]
    for part, ref in enumerate((past[-1], near_ref, far_ref)):
        high, low = split2(ref[...])
        put_rows(parts, part * count * 8, high)
        put_rows(parts, part * count * 8 + 1, low)

    def tile(t, carry):
        lefts = []
        for k in range(1 + blocks_ref.shape[1] // 128):
            u = t if k == 0 else index_ref[t * 4 + k - 1]
            lefts.append(parts[pl.ds(pl.multiple_of(u * 8, 8), 8), :].astype(BF16))
        left = jnp.concatenate(lefts[1:], axis=1)
        value = jnp.dot(left, blocks_ref[t], preferred_element_type=F32)
        value = value + jnp.dot(lefts[0], own_blocks[t], preferred_element_type=F32)
        images[pl.ds(pl.multiple_of(t * 8, 8), 8), :] = value
        return carry

    lax.fori_loop(0, count, tile, 0, unroll=UNROLL)
    coupled = rows_at(images, 0, count) + rows_at(images, 1, count)
    vectors = [ref[...] for ref in past]
    vector = (diagonal_ref[...] - SHIFT) * vectors[-1] - coupled
    vectors.append(vector)
    vector_ref[...] = vector
    totals_ref[...] = add_dots(row_ref[...], vectors)


def image(index, blocks, diagonal, row, near, far, own, past):
    count = diagonal.shape[0]
    operands = [*blocks, diagonal, row, near, far, own, *past]
    return pl.pallas_call(
        functools.partial(image_kernel, len(past)),
        in_specs=[SMEM] + [VMEM] * len(operands),
        out_specs=[VMEM] * 2,
        out_shape=[
            jax.ShapeDtypeStruct(diagonal.shape, F32),
            jax.ShapeDtypeStruct(row.shape, F32),
        ],
        scratch_shapes=[
            pltpu.VMEM((3 * count * 8, 128), F32),
            pltpu.VMEM((count * 8, 128), F32),
        ],
        compiler_params=pltpu.CompilerParams(vmem_limit_bytes=LIMIT),
        name="image",
    )(index, *operands)


def slots_kernel(target_ref, own_ref, first_ref, second_ref, third_ref, out_ref):
    owners, rows_each, _ = out_ref.shape
    count = first_ref.shape[0]
    each = (rows_each - 8) // 4
    slot = lax.broadcasted_iota(jnp.int32, (owners * each, count), 0)
    chosen = (slot == target_ref[...]).astype(F32).astype(BF16)
    for j, ref in enumerate((own_ref.at[4], first_ref, second_ref, third_ref)):
        value = ref[...]
        placed = sum(jnp.dot(chosen, piece, preferred_element_type=F32) for piece in split3(value))
        for owner in range(owners):
            out_ref[owner, pl.ds(each * j, each), :] = placed[each * owner : each * (owner + 1)]


def join_kernel(parts_ref, *refs):
    sums, (_, out_ref) = refs[:-2], refs[-2:]
    row = parts_ref[...]
    for ref in sums:
        row = row + ref[...]
    owners, rows_each, _ = out_ref.shape
    for owner in range(owners):
        out_ref[owner, pl.ds(rows_each - 8, 8), :] = jnp.broadcast_to(row, (8, 128))


def coefficients(totals):
    lane = lax.broadcasted_iota(jnp.int32, (1, 128), 1)
    gram = {}
    for (i, j), place in PAIRS.items():
        value = jnp.sum(jnp.where(lane == place, totals, 0.0), axis=1, keepdims=True)
        gram[i, j] = gram[j, i] = value

    def dot(a, b):
        return sum(x * sum(gram[i, j] * y for j, y in enumerate(b)) for i, x in enumerate(a))

    one = jnp.ones((1, 1), F32)
    zero = jnp.zeros((1, 1), F32)
    solution, residual, direction = [], [one], [one]
    norm = gram[0, 0]
    for iteration in range(ITERS):
        padded = direction + [zero]
        product = [SHIFT * value for value in padded]
        product = [value + (padded[j - 1] if j else zero) for j, value in enumerate(product)]
        step = norm / dot(direction, product)
        solution = [a + step * b for a, b in zip(solution + [zero], direction)]
        residual = [a - step * b for a, b in zip(residual + [zero], product)]
        if iteration < ITERS - 1:
            following = dot(residual, residual)
            direction = [a + (following / norm) * b for a, b in zip(residual, padded)]
            norm = following
    return solution, residual


def finish_kernel(arrived_ref, solution_ref, residual_ref):
    owners, rows_each, _ = arrived_ref.shape
    each = (rows_each - 8) // 4
    totals = sum(arrived_ref[owner, pl.ds(rows_each - 8, 8), :] for owner in range(owners))
    solution, residual = coefficients(totals[:1])
    for owner in range(owners):
        basis = [arrived_ref[owner, pl.ds(each * j, each), :] for j in range(4)]
        place = pl.ds(each * owner, each)
        solution_ref[place, :] = sum(a * v for a, v in zip(solution, basis))
        residual_ref[place, :] = sum(a * v for a, v in zip(residual, basis))


def local(positions, charges, drag, right_side, neighbours, owners):
    count = positions.shape[0]
    brick_count = lax.axis_size("brick")
    slab_count = lax.axis_size("slab")
    each = max(3, 3 * count // brick_count)
    slab_at = lax.axis_index("slab")
    first_tile = (lax.axis_index("brick") * slab_count + slab_at) * count
    inner = [(i, i ^ 1) for i in range(slab_count)]
    outer = [(i, i + 1) for i in range(1, slab_count - 1, 2)]
    outer = outer + [(target, source) for source, target in outer]

    packed, target = pl.pallas_call(
        functools.partial(pack_kernel, each),
        out_shape=[
            jax.ShapeDtypeStruct((5, count, 128), F32),
            jax.ShapeDtypeStruct((1, count), jnp.int32),
        ],
        in_specs=[HBM] * 4,
        out_specs=[VMEM] * 2,
        scratch_shapes=[
            pltpu.VMEM((count, 128), F32),
            pltpu.VMEM((1, count), jnp.int32),
            pltpu.SemaphoreType.DMA((4,)),
        ],
        compiler_params=pltpu.CompilerParams(vmem_limit_bytes=LIMIT),
        name="pack",
    )(*map(in_hbm, (jnp.transpose(positions, (1, 0, 2)), charges, right_side, owners.reshape(1, count))))

    offset = neighbours - first_tile
    layer = jnp.floor_divide(offset, count)
    partner = 1 - 2 * (slab_at % 2)
    part = jnp.where(layer == 0, 0, jnp.where(layer == partner, 1, 2))
    index = (offset - layer * count + part * count).reshape(-1)

    def both_sides(value):
        far = lax.ppermute(value, "slab", outer)
        near = lax.ppermute(value, "slab", inner)
        return near, far

    scale = 8.0 / ((neighbours.shape[1] + 1) * 128)
    entries = neighbours.shape[1]
    near, far = both_sides(packed)
    own_blocks, total, coupled = own_weights(packed, scale)
    blocks, first, diagonal, row = other_weights(
        index, packed, near, far, total, coupled, drag, scale, entries
    )
    blocks = own_blocks, blocks
    near, far = both_sides(first)
    second, row = image(index, blocks, diagonal, row, near, far, packed, [first])
    near, far = both_sides(second)
    third, row = image(index, blocks, diagonal, row, near, far, packed, [first, second])
    row = row + lax.ppermute(row, "slab", inner)
    around = [
        lax.ppermute(row, "slab", [(i, (i + step) % slab_count) for i in range(slab_count)])
        for step in (slab_count // 2, *(x for x in range(2, slab_count, 2) if x != slab_count // 2))
    ]
    outgoing = jax.ShapeDtypeStruct((brick_count, 4 * each + 8, 128), F32)
    params = pltpu.CompilerParams(vmem_limit_bytes=LIMIT)
    basis = pl.pallas_call(
        slots_kernel,
        out_shape=outgoing,
        in_specs=[VMEM] * 5,
        out_specs=VMEM,
        compiler_params=params,
        cost_estimate=pl.CostEstimate(flops=1 << 30, bytes_accessed=1 << 20, transcendentals=0),
        name="slots",
    )(target, packed, first, second, third)
    outgoing = pl.pallas_call(
        join_kernel,
        out_shape=outgoing,
        in_specs=[VMEM] * (2 + len(around)),
        out_specs=VMEM,
        input_output_aliases={1 + len(around): 0},
        compiler_params=params,
        name="join",
    )(row, *around, basis)
    arrived = lax.all_to_all(outgoing, "brick", split_axis=0, concat_axis=0, tiled=True)
    shape = jax.ShapeDtypeStruct((brick_count * each, 128), F32)
    return pl.pallas_call(
        finish_kernel,
        out_shape=(shape, shape),
        in_specs=[VMEM],
        out_specs=(VMEM, VMEM),
        compiler_params=pltpu.CompilerParams(vmem_limit_bytes=LIMIT),
        name="finish",
    )(arrived)


def solution(mesh):
    placed = (
        P(BOTH, None, None),
        P(BOTH, None),
        P(BOTH, None),
        P(BOTH, None),
        P(BOTH, None),
        P(BOTH, None),
    )
    step = jax.shard_map(
        local,
        mesh=mesh,
        in_specs=placed,
        out_specs=(P(BOTH, None), P(BOTH, None)),
        check_vma=False,
    )
    return step
```

time: 121 us -> 104 us (0.86)
  local copies, waits for them, and re-layouts: 18.7 us -> 0.22 us
  blocking collectives: 38 us -> 20.5 us
  Pallas kernels: 44.3 us -> 58.1 us
  starting transfers between devices: 15.9 us -> 19.5 us
  waiting for transfers between devices: 2.02 us -> 3.75 us
    all_to_all x1 -> x0, blocking collectives: 21 us -> none  [local(): lax.all_to_all(totals.reshape(devices, 1, 128), BOTH, split_axis=0, conca...]
    unnamed x18 -> x0, local copies, waits for them, and re-layouts: 18.5 us -> none
    pallas_call x5 -> x8, Pallas kernels: 44.3 us -> 58.1 us  [the longest x1 24.4 us: other_weights(): pl.pallas_call(functools.partial(other_kernel, scale, blocks_count), in_s...]
    ppermute x0 -> x4, starting transfers between devices: none -> 6.64 us  [the longest x3 5.67 us: local(): lax.ppermute(row, 'slab', [(i, (i + step) % slab_count) for i in range(sl...]
    all_to_all x1, blocking collectives: 17 us -> 20.5 us  [local(): lax.all_to_all(outgoing, 'brick', split_axis=0, concat_axis=0, tiled=True)]
    ppermute x3, starting transfers between devices: 13.9 us -> 10.8 us  [both_sides(): near = lax.ppermute(value, 'slab', inner)]
    ppermute x0 -> x4, waiting for transfers between devices: none -> 1.94 us  [the longest x3 1.12 us: local(): lax.ppermute(row, 'slab', [(i, (i + step) % slab_count) for i in range(sl...]
  transfers between devices with their start and end apart: 6 -> 10, of which waited for: 3 -> 5; matrix products, arithmetic and copies ran while one was open for 1% -> 1% of each run, Pallas kernels for 0% -> 15%
where the time goes in v3:
time: 104 us; the launch traced here: 103 us
  Pallas kernels  58.1 us (56%)
  blocking collectives  20.5 us (20%)
  starting transfers between devices  19.5 us (19%)
  waiting for transfers between devices  3.75 us (4%)
    pallas_call x1, Pallas kernels, other_weights(): pl.pallas_call(functools.partial(other_kernel, scale, blocks_count), in_s...  24.4 us
    all_to_all x1, blocking collectives, local(): lax.all_to_all(outgoing, 'brick', split_axis=0, concat_axis=0, tiled=True)  20.5 us
    pallas_call x2, Pallas kernels, image(): pl.pallas_call(functools.partial(image_kernel, len(past)), in_specs=[SMEM...  16 us
    pallas_call x1, Pallas kernels, own_weights(): pl.pallas_call(functools.partial(own_kernel, scale), in_specs=[VMEM], out...  15.1 us
    ppermute x3, starting transfers between devices, both_sides(): near = lax.ppermute(value, 'slab', inner)  10.8 us
    ppermute x3, starting transfers between devices, local(): lax.ppermute(row, 'slab', [(i, (i + step) % slab_count) for i in range(sl...  5.67 us
  transfers between devices with their start and end apart: 10, of which 5 were waited for; matrix products, arithmetic and copies ran while one was open for 1% of the time, Pallas kernels for 15%

profile of v3, /device:TPU:0, one launch (start us, length us, event | category | flops | bytes accessed | tf_op | source)
XLA Modules:
  0.0 103.4 jit_solution(2222547489141866678)
XLA Ops:
  0.6 1.1 %pack.1 = (f32[5,128,128]{2,1,0:T(8,128)S(1)}, s32[1,128]{1,0:T(1,128)S(1)}) custom-call(f32[3,128,128]{2,1,0:T(8,128)} %bitcast.2, f32[128,128]{1,0:T(8,128)} %charge_hbm.1, f32[128,128]{1,0:T(8,128)} %force_hbm.1, s32[1,128]{1,0:T(1,128)} %bitcast.3), custom_call_target="tpu_custom_call" | custom-call | tf_op jit(solution)/shard_map/pack/pallas_call | solution.py:401
  1.8 0.7 collective-permute-start.1
  2.5 3.5 %collective-permute-start = (f32[5,128,128]{2,1,0:T(8,128)S(1)}, f32[5,128,128]{2,1,0:T(8,128)S(1)}, u32[]{:S(2)}, u32[]{:S(2)}) collective-permute-start(f32[5,128,128]{2,1,0:T(8,128)S(1)} %get-tuple-element.15.own_ref), channel_id=1, source_target_pairs={{0,1},{1,0},{2,3},{3,2},{4,5},{5,4},{6,7},{7,6},{8,9},{9,8},{10,11... | collective-permute-start | bytes 983048 | tf_op jit(solution)/shard_map/ppermute | solution.py:426
  5.9 0.7 multiply_add_fusion
  6.6 0.1 copy.9
  6.8 15.1 %own_weights.1 = (bf16[128,128,128]{2,1,0:T(8,128)(2,1)S(1)}, f32[128,128]{1,0:T(8,128)S(1)}, f32[128,128]{1,0:T(8,128)S(1)}) custom-call(f32[5,128,128]{2,1,0:T(8,128)S(1)} %get-tuple-element.15.own_ref), custom_call_target="tpu_custom_call" | custom-call | flops 1258291200 | bytes 1048576 | tf_op jit(solution)/shard_map/own_weights/pallas_call | solution.py:219
  22.0 24.4 %other_weights.1 = (bf16[128,512,128]{2,1,0:T(8,128)(2,1)S(1)}, f32[128,128]{1,0:T(8,128)S(1)}, f32[128,128]{1,0:T(8,128)S(1)}, f32[1,128]{1,0:T(1,128)S(1)}) custom-call(s32[512]{0:T(512)S(1)} %reshape.10.index_ref, f32[5,128,128]{2,1,0:T(8,128)S(1)} %get-tuple-element.15.own_ref, f32[5,128,128]{2,1,0:T(8,128)S(1)} %collective-permute-done.near_ref, ...), custom_call_target="tpu_custom_call" | custom-call | tf_op jit(solution)/shard_map/other_weights/pallas_call | solution.py:256
  46.4 0.7 collective-permute-start.3
  47.0 3.4 %collective-permute-start.2 = (f32[128,128]{1,0:T(8,128)S(1)}, f32[128,128]{1,0:T(8,128)S(1)}, u32[]{:S(2)}, u32[]{:S(2)}) collective-permute-start(f32[128,128]{1,0:T(8,128)S(1)} %get-tuple-element.22.refs_0_.first_ref), channel_id=1, source_target_pairs={{0,1},{1,0},{2,3},{3,2},{4,5},{5,4},{6,7},{7,6},{8,9},{9,8},{10,11... | collective-permute-start | bytes 196616 | tf_op jit(solution)/shard_map/ppermute | solution.py:426
  50.4 0.9 collective-permute-done.2.near_ref
  51.3 8.0 %image.2 = (f32[128,128]{1,0:T(8,128)S(1)}, f32[1,128]{1,0:T(1,128)S(1)}) custom-call(s32[512]{0:T(512)S(1)} %reshape.10.index_ref, bf16[128,128,128]{2,1,0:T(8,128)(2,1)S(1)} %get-tuple-element.16.own_blocks, bf16[128,512,128]{2,1,0:T(8,128)(2,1)S(1)} %get-tuple-element.19.blocks_ref, f32[128,128]{1,0:T(8,128)S(1)} %get-tuple-element.20.diagonal_ref, ...), custom_call_target="tpu_custom_call" | custom-call | tf_op jit(solution)/shard_map/image/pallas_call | solution.py:310
  59.3 0.7 collective-permute-start.5
  59.9 4.0 %collective-permute-start.4 = (f32[128,128]{1,0:T(8,128)S(1)}, f32[128,128]{1,0:T(8,128)S(1)}, u32[]{:S(2)}, u32[]{:S(2)}) collective-permute-start(f32[128,128]{1,0:T(8,128)S(1)} %get-tuple-element.24.refs_1_.second_ref), channel_id=1, source_target_pairs={{0,1},{1,0},{2,3},{3,2},{4,5},{5,4},{6,7},{7,6},{8,9},{9,8},{10,11... | collective-permute-start | bytes 196616 | tf_op jit(solution)/shard_map/ppermute | solution.py:426
  64.0 0.9 collective-permute-done.4.near_ref
  64.9 8.0 %image.3 = (f32[128,128]{1,0:T(8,128)S(1)}, f32[1,128]{1,0:T(1,128)S(1)}) custom-call(s32[512]{0:T(512)S(1)} %reshape.10.index_ref, bf16[128,128,128]{2,1,0:T(8,128)(2,1)S(1)} %get-tuple-element.16.own_blocks, bf16[128,512,128]{2,1,0:T(8,128)(2,1)S(1)} %get-tuple-element.19.blocks_ref, f32[128,128]{1,0:T(8,128)S(1)} %get-tuple-element.20.diagonal_ref, ...), custom_call_target="tpu_custom_call" | custom-call | tf_op jit(solution)/shard_map/image/pallas_call | solution.py:310
  72.9 1.0 collective-permute-start.6
  73.8 0.8 collective-permute-done.6
  74.7 2.2 %collective-permute-start.9 = (f32[1,128]{1,0:T(1,128)S(1)}, f32[1,128]{1,0:T(1,128)S(1)}, u32[]{:S(2)}, u32[]{:S(2)}) collective-permute-start(f32[1,128]{1,0:T(1,128)S(1)} %add.17.parts_ref), channel_id=1, source_target_pairs={{0,6},{1,7},{2,0},{3,1},{4,2},{5,3},{6,4},{7,5},{8,14},{9,15},{10,... | collective-permute-start | bytes 1544 | tf_op jit(solution)/shard_map/ppermute | solution.py:443
  76.8 3.5 %collective-permute-start.7 = (f32[1,128]{1,0:T(1,128)S(1)}, f32[1,128]{1,0:T(1,128)S(1)}, u32[]{:S(2)}, u32[]{:S(2)}) collective-permute-start(f32[1,128]{1,0:T(1,128)S(1)} %add.17.parts_ref), channel_id=1, source_target_pairs={{0,4},{1,5},{2,6},{3,7},{4,0},{5,1},{6,2},{7,3},{8,12},{9,13},{10,... | collective-permute-start | bytes 1544 | tf_op jit(solution)/shard_map/ppermute | solution.py:443
  80.3 0.5 slots.1.refs_3_
  80.8 0.8 collective-permute-done.8.refs_1_
  81.6 0.3 collective-permute-done.7.refs_0_
  81.9 20.5 %all_to_all.5.arrived_ref = f32[16,104,128]{2,1,0:T(8,128)S(1)} all-to-all(f32[16,104,128]{2,1,0:T(8,128)S(1)} %join.1), channel_id=1, replica_groups=mesh['brick'=16,'slab'=8] {'brick'}, dimensions={0} | all-to-all | bytes 1703936 | tf_op jit(solution)/shard_map/all_to_all | solution.py:466
  102.5 1.0 finish.1
  (9 shorter events, 0.1 us)
Async XLA Ops:
  1.8 20.2 %collective-permute-start.1 = (f32[5,128,128]{2,1,0:T(8,128)S(1)}, f32[5,128,128]{2,1,0:T(8,128)S(1)}, u32[]{:S(2)}, u32[]{:S(2)}) collective-permute-start(f32[5,128,128]{2,1,0:T(8,128)S(1)} %get-tuple-element.15.own_ref), channel_id=1, source_target_pairs={{1,2},{3,4},{5,6},{2,1},{4,3},{6,5},{9,10},{11,12},{13,14},{10,9},... | collective-permute-start | bytes 983048 | tf_op jit(solution)/shard_map/ppermute | solution.py:425
  2.5 19.5 %collective-permute-start = (f32[5,128,128]{2,1,0:T(8,128)S(1)}, f32[5,128,128]{2,1,0:T(8,128)S(1)}, u32[]{:S(2)}, u32[]{:S(2)}) collective-permute-start(f32[5,128,128]{2,1,0:T(8,128)S(1)} %get-tuple-element.15.own_ref), channel_id=1, source_target_pairs={{0,1},{1,0},{2,3},{3,2},{4,5},{5,4},{6,7},{7,6},{8,9},{9,8},{10,11... | collective-permute-start | bytes 983048 | tf_op jit(solution)/shard_map/ppermute | solution.py:426
  46.4 4.0 %collective-permute-start.3 = (f32[128,128]{1,0:T(8,128)S(1)}, f32[128,128]{1,0:T(8,128)S(1)}, u32[]{:S(2)}, u32[]{:S(2)}) collective-permute-start(f32[128,128]{1,0:T(8,128)S(1)} %get-tuple-element.22.refs_0_.first_ref), channel_id=1, source_target_pairs={{1,2},{3,4},{5,6},{2,1},{4,3},{6,5},{9,10},{11,12},{13,14},{10,9},... | collective-permute-start | bytes 196616 | tf_op jit(solution)/shard_map/ppermute | solution.py:425
  47.0 4.3 %collective-permute-start.2 = (f32[128,128]{1,0:T(8,128)S(1)}, f32[128,128]{1,0:T(8,128)S(1)}, u32[]{:S(2)}, u32[]{:S(2)}) collective-permute-start(f32[128,128]{1,0:T(8,128)S(1)} %get-tuple-element.22.refs_0_.first_ref), channel_id=1, source_target_pairs={{0,1},{1,0},{2,3},{3,2},{4,5},{5,4},{6,7},{7,6},{8,9},{9,8},{10,11... | collective-permute-start | bytes 196616 | tf_op jit(solution)/shard_map/ppermute | solution.py:426
  59.3 4.7 %collective-permute-start.5 = (f32[128,128]{1,0:T(8,128)S(1)}, f32[128,128]{1,0:T(8,128)S(1)}, u32[]{:S(2)}, u32[]{:S(2)}) collective-permute-start(f32[128,128]{1,0:T(8,128)S(1)} %get-tuple-element.24.refs_1_.second_ref), channel_id=1, source_target_pairs={{1,2},{3,4},{5,6},{2,1},{4,3},{6,5},{9,10},{11,12},{13,14},{10,9},... | collective-permute-start | bytes 196616 | tf_op jit(solution)/shard_map/ppermute | solution.py:425
  59.9 4.9 %collective-permute-start.4 = (f32[128,128]{1,0:T(8,128)S(1)}, f32[128,128]{1,0:T(8,128)S(1)}, u32[]{:S(2)}, u32[]{:S(2)}) collective-permute-start(f32[128,128]{1,0:T(8,128)S(1)} %get-tuple-element.24.refs_1_.second_ref), channel_id=1, source_target_pairs={{0,1},{1,0},{2,3},{3,2},{4,5},{5,4},{6,7},{7,6},{8,9},{9,8},{10,11... | collective-permute-start | bytes 196616 | tf_op jit(solution)/shard_map/ppermute | solution.py:426
  72.9 1.8 %collective-permute-start.6 = (f32[1,128]{1,0:T(1,128)S(1)}, f32[1,128]{1,0:T(1,128)S(1)}, u32[]{:S(2)}, u32[]{:S(2)}) collective-permute-start(f32[1,128]{1,0:T(1,128)S(1)} %get-tuple-element.25), channel_id=1, source_target_pairs={{0,1},{1,0},{2,3},{3,2},{4,5},{5,4},{6,7},{7,6},{8,9},{9,8},{10,11... | collective-permute-start | bytes 1544 | tf_op jit(solution)/shard_map/ppermute | solution.py:441
  74.7 6.1 %collective-permute-start.9 = (f32[1,128]{1,0:T(1,128)S(1)}, f32[1,128]{1,0:T(1,128)S(1)}, u32[]{:S(2)}, u32[]{:S(2)}) collective-permute-start(f32[1,128]{1,0:T(1,128)S(1)} %add.17.parts_ref), channel_id=1, source_target_pairs={{0,6},{1,7},{2,0},{3,1},{4,2},{5,3},{6,4},{7,5},{8,14},{9,15},{10,... | collective-permute-start | bytes 1544 | tf_op jit(solution)/shard_map/ppermute | solution.py:443
  76.8 4.8 %collective-permute-start.8 = (f32[1,128]{1,0:T(1,128)S(1)}, f32[1,128]{1,0:T(1,128)S(1)}, u32[]{:S(2)}, u32[]{:S(2)}) collective-permute-start(f32[1,128]{1,0:T(1,128)S(1)} %add.17.parts_ref), channel_id=1, source_target_pairs={{0,2},{1,3},{2,4},{3,5},{4,6},{5,7},{6,0},{7,1},{8,10},{9,11},{10,... | collective-permute-start | bytes 1544 | tf_op jit(solution)/shard_map/ppermute | solution.py:443
  76.8 5.1 %collective-permute-start.7 = (f32[1,128]{1,0:T(1,128)S(1)}, f32[1,128]{1,0:T(1,128)S(1)}, u32[]{:S(2)}, u32[]{:S(2)}) collective-permute-start(f32[1,128]{1,0:T(1,128)S(1)} %add.17.parts_ref), channel_id=1, source_target_pairs={{0,4},{1,5},{2,6},{3,7},{4,0},{5,1},{6,2},{7,3},{8,12},{9,13},{10,... | collective-permute-start | bytes 1544 | tf_op jit(solution)/shard_map/ppermute | solution.py:443

commit v4 on v3

--- a/solution.py
+++ b/solution.py
@@ -9,8 +9,10 @@
 
 ITERS = 3
 SHIFT = 7.0
-MIX = 6
-UNROLL = 4
+MIX = 7
+UNROLL = 64
+GROUP = 8
+OWN_GROUP = 16
 LOG2E = 1.4426950408889634
 F32 = jnp.float32
 BF16 = jnp.bfloat16
@@ -98,7 +100,9 @@
 
 
 def weights_kernel(scale, first, blocks_count, index_ref, planes, blocks_ref, scratch, finish):
-    raw, mine, sums, images, even, odd = scratch
+    raw, mine, sums, images, *buffers = scratch
+    buffers, ring = buffers[: len(buffers) // 2], buffers[len(buffers) // 2 :]
+    group = len(buffers)
     count = mine.shape[0] // 16
     square = LOG2E * LOG2E
     width = 128 * blocks_count
@@ -138,7 +142,7 @@
             left, right, (((0,), (0,)), ((), ())), preferred_element_type=F32
         )
 
-    def block(t, source, incoming):
+    def block(t, source, kept, incoming):
         totals = [None] * 4
         for pair in range(width // 16):
             halves = []
@@ -147,7 +151,7 @@
                 place = pl.ds(8 * chunk, 8)
                 wide = source[place, :128]
                 shifted = wide - 0.49 * square
-                if chunk % MIX == MIX - 1:
+                if (chunk * MIX) % 10 < MIX:
                     distance = shifted * lax.rsqrt(shifted)
                     inverse = pltpu.reciprocal(wide)
                 else:
@@ -163,45 +167,46 @@
                 past = totals[chunk % 4]
                 totals[chunk % 4] = weight if past is None else past + weight
                 halves.append(weight)
-            blocks_ref[t, pl.ds(16 * pair, 16), :] = jnp.concatenate(halves, axis=0).astype(BF16)
+            rounded = jnp.concatenate(halves, axis=0).astype(BF16)
+            blocks_ref[t, pl.ds(16 * pair, 16), :] = rounded
+            kept[pl.ds(16 * pair, 16), :] = rounded
             source[pl.ds(16 * pair, 16), :] = incoming[16 * pair : 16 * pair + 16]
         total = (totals[0] + totals[1]) + (totals[2] + totals[3])
         sums[pl.ds(pl.multiple_of(t * 8, 8), 8), :] = total
 
-    def image(t):
+    def image(t, kept):
         left = jnp.concatenate([value.astype(BF16) for value in entries(t)], axis=1)
         images[pl.ds(pl.multiple_of(t * 8, 8), 8), :] = jnp.dot(
-            left, blocks_ref[t], preferred_element_type=F32
+            left, kept[...], preferred_element_type=F32
         )
 
-    even[...] = terms(0)
-    odd[...] = terms(1)
-
-    def pair(j, carry):
-        t = 2 * j
-        image(jnp.maximum(t - 2, 0))
-        image(jnp.maximum(t - 1, 0))
-        block(t, even, terms(jnp.minimum(t + 2, count - 1)))
-        block(t + 1, odd, terms(jnp.minimum(t + 3, count - 1)))
+    for i in range(group):
+        buffers[i][...] = terms(i)
+
+    def tiles(j, carry):
+        t = group * j
+        for i in range(group):
+            image(jnp.maximum(t + i - group, 0), ring[i])
+            block(t + i, buffers[i], ring[i], terms(jnp.minimum(t + i + group, count - 1)))
         return carry
 
-    lax.fori_loop(0, count // 2, pair, 0)
-    image(count - 2)
-    image(count - 1)
+    lax.fori_loop(0, count // group, tiles, 0)
+    for i in range(group):
+        image(count - group + i, ring[i])
     total = rows_at(sums, 0, count)
     for j in range(1, 8):
         total = total + rows_at(sums, j, count)
     finish(total, rows_at(images, 6, count) + rows_at(images, 7, count))
 
 
-def weights_scratch(count, parts, blocks_count):
+def weights_scratch(count, parts, blocks_count, group):
     return [
         pltpu.VMEM((parts * count * 8, 128), F32),
         pltpu.VMEM((count * 16, 128), F32),
         pltpu.VMEM((count * 8, 128), F32),
         pltpu.VMEM((count * 8, 128), F32),
-        pltpu.VMEM((128 * blocks_count, 256), F32),
-        pltpu.VMEM((128 * blocks_count, 256), F32),
+        *[pltpu.VMEM((128 * blocks_count, 256), F32)] * group,
+        *[pltpu.VMEM((128 * blocks_count, 128), BF16)] * group,
     ]
 
 
@@ -221,7 +226,7 @@
         in_specs=[VMEM],
         out_specs=[VMEM] * 3,
         out_shape=[pltpu.VMEM((count, 128, 128), BF16), plane, plane],
-        scratch_shapes=weights_scratch(count, 1, 1),
+        scratch_shapes=weights_scratch(count, 1, 1, OWN_GROUP),
         compiler_params=pltpu.CompilerParams(vmem_limit_bytes=LIMIT),
         cost_estimate=pl.CostEstimate(
             flops=count * 128 * 128 * 600, bytes_accessed=1 << 20, transcendentals=count * 128 * 256
@@ -266,7 +271,7 @@
         scratch_shapes=[
             pltpu.VMEM((count, 128), F32),
             pltpu.SemaphoreType.DMA,
-            *weights_scratch(count, 3, blocks_count),
+            *weights_scratch(count, 3, blocks_count, GROUP),
         ],
         compiler_params=pltpu.CompilerParams(vmem_limit_bytes=LIMIT),
         name="other_weights",

time: 104 us -> 83 us (0.80)
  Pallas kernels: 58.1 us -> 37.4 us
    pallas_call x1, Pallas kernels: 15.1 us -> 6.42 us  [own_weights(): pl.pallas_call(functools.partial(own_kernel, scale), in_specs=[VMEM], out...]
    pallas_call x2, Pallas kernels: 16 us -> 8.75 us  [image(): pl.pallas_call(functools.partial(image_kernel, len(past)), in_specs=[SMEM...]
    pallas_call x1, Pallas kernels: 24.4 us -> 19.7 us  [other_weights(): pl.pallas_call(functools.partial(other_kernel, scale, blocks_count), in_s...]
  transfers between devices with their start and end apart: 10 -> 10, of which waited for: 5 -> 5; matrix products, arithmetic and copies ran while one was open for 1% -> 1% of each run, Pallas kernels for 15% -> 8%
where the time goes in v4:
time: 83 us; the launch traced here: 82.8 us
  Pallas kernels  37.4 us (45%)
  blocking collectives  20.5 us (25%)
  starting transfers between devices  19.4 us (23%)
  waiting for transfers between devices  3.76 us (5%)
    all_to_all x1, blocking collectives, local(): lax.all_to_all(outgoing, 'brick', split_axis=0, concat_axis=0, tiled=True)  20.5 us
    pallas_call x1, Pallas kernels, other_weights(): pl.pallas_call(functools.partial(other_kernel, scale, blocks_count), in_s...  19.7 us
    ppermute x3, starting transfers between devices, both_sides(): near = lax.ppermute(value, 'slab', inner)  10.8 us
    pallas_call x2, Pallas kernels, image(): pl.pallas_call(functools.partial(image_kernel, len(past)), in_specs=[SMEM...  8.75 us
    pallas_call x1, Pallas kernels, own_weights(): pl.pallas_call(functools.partial(own_kernel, scale), in_specs=[VMEM], out...  6.42 us
    ppermute x3, starting transfers between devices, local(): lax.ppermute(row, 'slab', [(i, (i + step) % slab_count) for i in range(sl...  5.68 us
    ppermute x3, starting transfers between devices, both_sides(): far = lax.ppermute(value, 'slab', outer)  2 us
    ppermute x3, waiting for transfers between devices, both_sides(): near = lax.ppermute(value, 'slab', inner)  1.8 us
  transfers between devices with their start and end apart: 10, of which 5 were waited for; matrix products, arithmetic and copies ran while one was open for 1% of the time, Pallas kernels for 8%

profile of v4, /device:TPU:0, one launch (start us, length us, event | category | flops | bytes accessed | tf_op | source)
XLA Modules:
  0.0 82.8 jit_solution(10110290868244095750)
XLA Ops:
  0.6 1.1 %pack.1 = (f32[5,128,128]{2,1,0:T(8,128)S(1)}, s32[1,128]{1,0:T(1,128)S(1)}) custom-call(f32[3,128,128]{2,1,0:T(8,128)} %bitcast.2, f32[128,128]{1,0:T(8,128)} %charge_hbm.1, f32[128,128]{1,0:T(8,128)} %force_hbm.1, s32[1,128]{1,0:T(1,128)} %bitcast.3), custom_call_target="tpu_custom_call" | custom-call | tf_op jit(solution)/shard_map/pack/pallas_call | solution.py:406
  1.8 0.7 collective-permute-start.1
  2.5 3.5 %collective-permute-start = (f32[5,128,128]{2,1,0:T(8,128)S(1)}, f32[5,128,128]{2,1,0:T(8,128)S(1)}, u32[]{:S(2)}, u32[]{:S(2)}) collective-permute-start(f32[5,128,128]{2,1,0:T(8,128)S(1)} %get-tuple-element.15.own_ref), channel_id=1, source_target_pairs={{0,1},{1,0},{2,3},{3,2},{4,5},{5,4},{6,7},{7,6},{8,9},{9,8},{10,11... | collective-permute-start | bytes 983048 | tf_op jit(solution)/shard_map/ppermute | solution.py:431
  5.9 0.7 multiply_add_fusion
  6.6 0.1 copy.9
  6.8 6.4 %own_weights.1 = (bf16[128,128,128]{2,1,0:T(8,128)(2,1)S(1)}, f32[128,128]{1,0:T(8,128)S(1)}, f32[128,128]{1,0:T(8,128)S(1)}) custom-call(f32[5,128,128]{2,1,0:T(8,128)S(1)} %get-tuple-element.15.own_ref), custom_call_target="tpu_custom_call" | custom-call | flops 1258291200 | bytes 1048576 | tf_op jit(solution)/shard_map/own_weights/pallas_call | solution.py:224
  13.3 19.7 %other_weights.1 = (bf16[128,512,128]{2,1,0:T(8,128)(2,1)S(1)}, f32[128,128]{1,0:T(8,128)S(1)}, f32[128,128]{1,0:T(8,128)S(1)}, f32[1,128]{1,0:T(1,128)S(1)}) custom-call(s32[512]{0:T(512)S(1)} %reshape.10.index_ref, f32[5,128,128]{2,1,0:T(8,128)S(1)} %get-tuple-element.15.own_ref, f32[5,128,128]{2,1,0:T(8,128)S(1)} %collective-permute-done.near_ref, ...), custom_call_target="tpu_custom_call" | custom-call | tf_op jit(solution)/shard_map/other_weights/pallas_call | solution.py:261
  33.0 0.7 collective-permute-start.3
  33.6 3.3 %collective-permute-start.2 = (f32[128,128]{1,0:T(8,128)S(1)}, f32[128,128]{1,0:T(8,128)S(1)}, u32[]{:S(2)}, u32[]{:S(2)}) collective-permute-start(f32[128,128]{1,0:T(8,128)S(1)} %get-tuple-element.22.refs_0_.first_ref), channel_id=1, source_target_pairs={{0,1},{1,0},{2,3},{3,2},{4,5},{5,4},{6,7},{7,6},{8,9},{9,8},{10,11... | collective-permute-start | bytes 196616 | tf_op jit(solution)/shard_map/ppermute | solution.py:431
  36.9 0.9 %collective-permute-done.2.near_ref = f32[128,128]{1,0:T(8,128)S(1)} collective-permute-done((f32[128,128]{1,0:T(8,128)S(1)}, f32[128,128]{1,0:T(8,128)S(1)}, u32[]{:S(2)}, u32[]{:S(2)}) %collective-permute-start.2) | collective-permute-done | bytes 65568 | tf_op jit(solution)/shard_map/ppermute | solution.py:431
  37.8 4.4 %image.2 = (f32[128,128]{1,0:T(8,128)S(1)}, f32[1,128]{1,0:T(1,128)S(1)}) custom-call(s32[512]{0:T(512)S(1)} %reshape.10.index_ref, bf16[128,128,128]{2,1,0:T(8,128)(2,1)S(1)} %get-tuple-element.16.own_blocks, bf16[128,512,128]{2,1,0:T(8,128)(2,1)S(1)} %get-tuple-element.19.blocks_ref, f32[128,128]{1,0:T(8,128)S(1)} %get-tuple-element.20.diagonal_ref, ...), custom_call_target="tpu_custom_call" | custom-call | tf_op jit(solution)/shard_map/image/pallas_call | solution.py:315
  42.2 0.7 collective-permute-start.5
  42.9 4.0 %collective-permute-start.4 = (f32[128,128]{1,0:T(8,128)S(1)}, f32[128,128]{1,0:T(8,128)S(1)}, u32[]{:S(2)}, u32[]{:S(2)}) collective-permute-start(f32[128,128]{1,0:T(8,128)S(1)} %get-tuple-element.24.refs_1_.second_ref), channel_id=1, source_target_pairs={{0,1},{1,0},{2,3},{3,2},{4,5},{5,4},{6,7},{7,6},{8,9},{9,8},{10,11... | collective-permute-start | bytes 196616 | tf_op jit(solution)/shard_map/ppermute | solution.py:431
  46.9 0.9 %collective-permute-done.4.near_ref = f32[128,128]{1,0:T(8,128)S(1)} collective-permute-done((f32[128,128]{1,0:T(8,128)S(1)}, f32[128,128]{1,0:T(8,128)S(1)}, u32[]{:S(2)}, u32[]{:S(2)}) %collective-permute-start.4) | collective-permute-done | bytes 65568 | tf_op jit(solution)/shard_map/ppermute | solution.py:431
  47.8 4.4 %image.3 = (f32[128,128]{1,0:T(8,128)S(1)}, f32[1,128]{1,0:T(1,128)S(1)}) custom-call(s32[512]{0:T(512)S(1)} %reshape.10.index_ref, bf16[128,128,128]{2,1,0:T(8,128)(2,1)S(1)} %get-tuple-element.16.own_blocks, bf16[128,512,128]{2,1,0:T(8,128)(2,1)S(1)} %get-tuple-element.19.blocks_ref, f32[128,128]{1,0:T(8,128)S(1)} %get-tuple-element.20.diagonal_ref, ...), custom_call_target="tpu_custom_call" | custom-call | tf_op jit(solution)/shard_map/image/pallas_call | solution.py:315
  52.2 1.0 %collective-permute-start.6 = (f32[1,128]{1,0:T(1,128)S(1)}, f32[1,128]{1,0:T(1,128)S(1)}, u32[]{:S(2)}, u32[]{:S(2)}) collective-permute-start(f32[1,128]{1,0:T(1,128)S(1)} %get-tuple-element.25), channel_id=1, source_target_pairs={{0,1},{1,0},{2,3},{3,2},{4,5},{5,4},{6,7},{7,6},{8,9},{9,8},{10,11... | collective-permute-start | bytes 1544 | tf_op jit(solution)/shard_map/ppermute | solution.py:446
  53.1 0.8 collective-permute-done.6
  54.0 2.2 %collective-permute-start.9 = (f32[1,128]{1,0:T(1,128)S(1)}, f32[1,128]{1,0:T(1,128)S(1)}, u32[]{:S(2)}, u32[]{:S(2)}) collective-permute-start(f32[1,128]{1,0:T(1,128)S(1)} %add.17.parts_ref), channel_id=1, source_target_pairs={{0,6},{1,7},{2,0},{3,1},{4,2},{5,3},{6,4},{7,5},{8,14},{9,15},{10,... | collective-permute-start | bytes 1544 | tf_op jit(solution)/shard_map/ppermute | solution.py:448
  56.2 3.5 %collective-permute-start.7 = (f32[1,128]{1,0:T(1,128)S(1)}, f32[1,128]{1,0:T(1,128)S(1)}, u32[]{:S(2)}, u32[]{:S(2)}) collective-permute-start(f32[1,128]{1,0:T(1,128)S(1)} %add.17.parts_ref), channel_id=1, source_target_pairs={{0,4},{1,5},{2,6},{3,7},{4,0},{5,1},{6,2},{7,3},{8,12},{9,13},{10,... | collective-permute-start | bytes 1544 | tf_op jit(solution)/shard_map/ppermute | solution.py:448
  59.6 0.5 slots.1.refs_3_
  60.1 0.8 %collective-permute-done.8.refs_1_ = f32[1,128]{1,0:T(1,128)S(1)} collective-permute-done((f32[1,128]{1,0:T(1,128)S(1)}, f32[1,128]{1,0:T(1,128)S(1)}, u32[]{:S(2)}, u32[]{:S(2)}) %collective-permute-start.8) | collective-permute-done | bytes 544 | tf_op jit(solution)/shard_map/ppermute | solution.py:448
  61.0 0.3 collective-permute-done.7.refs_0_
  61.3 20.5 %all_to_all.5.arrived_ref = f32[16,104,128]{2,1,0:T(8,128)S(1)} all-to-all(f32[16,104,128]{2,1,0:T(8,128)S(1)} %join.1), channel_id=1, replica_groups=mesh['brick'=16,'slab'=8] {'brick'}, dimensions={0} | all-to-all | bytes 1703936 | tf_op jit(solution)/shard_map/all_to_all | solution.py:471
  81.8 1.0 %finish.1 = (f32[384,128]{1,0:T(8,128)}, f32[384,128]{1,0:T(8,128)}) custom-call(f32[16,104,128]{2,1,0:T(8,128)S(1)} %all_to_all.5.arrived_ref), custom_call_target="tpu_custom_call" | custom-call | tf_op jit(solution)/shard_map/finish/pallas_call | solution.py:473
  (9 shorter events, 0.1 us)
Async XLA Ops:
  1.8 11.5 %collective-permute-start.1 = (f32[5,128,128]{2,1,0:T(8,128)S(1)}, f32[5,128,128]{2,1,0:T(8,128)S(1)}, u32[]{:S(2)}, u32[]{:S(2)}) collective-permute-start(f32[5,128,128]{2,1,0:T(8,128)S(1)} %get-tuple-element.15.own_ref), channel_id=1, source_target_pairs={{1,2},{3,4},{5,6},{2,1},{4,3},{6,5},{9,10},{11,12},{13,14},{10,9},... | collective-permute-start | bytes 983048 | tf_op jit(solution)/shard_map/ppermute | solution.py:430
  2.5 10.8 %collective-permute-start = (f32[5,128,128]{2,1,0:T(8,128)S(1)}, f32[5,128,128]{2,1,0:T(8,128)S(1)}, u32[]{:S(2)}, u32[]{:S(2)}) collective-permute-start(f32[5,128,128]{2,1,0:T(8,128)S(1)} %get-tuple-element.15.own_ref), channel_id=1, source_target_pairs={{0,1},{1,0},{2,3},{3,2},{4,5},{5,4},{6,7},{7,6},{8,9},{9,8},{10,11... | collective-permute-start | bytes 983048 | tf_op jit(solution)/shard_map/ppermute | solution.py:431
  33.0 4.0 %collective-permute-start.3 = (f32[128,128]{1,0:T(8,128)S(1)}, f32[128,128]{1,0:T(8,128)S(1)}, u32[]{:S(2)}, u32[]{:S(2)}) collective-permute-start(f32[128,128]{1,0:T(8,128)S(1)} %get-tuple-element.22.refs_0_.first_ref), channel_id=1, source_target_pairs={{1,2},{3,4},{5,6},{2,1},{4,3},{6,5},{9,10},{11,12},{13,14},{10,9},... | collective-permute-start | bytes 196616 | tf_op jit(solution)/shard_map/ppermute | solution.py:430
  33.6 4.2 %collective-permute-start.2 = (f32[128,128]{1,0:T(8,128)S(1)}, f32[128,128]{1,0:T(8,128)S(1)}, u32[]{:S(2)}, u32[]{:S(2)}) collective-permute-start(f32[128,128]{1,0:T(8,128)S(1)} %get-tuple-element.22.refs_0_.first_ref), channel_id=1, source_target_pairs={{0,1},{1,0},{2,3},{3,2},{4,5},{5,4},{6,7},{7,6},{8,9},{9,8},{10,11... | collective-permute-start | bytes 196616 | tf_op jit(solution)/shard_map/ppermute | solution.py:431
  42.2 4.7 %collective-permute-start.5 = (f32[128,128]{1,0:T(8,128)S(1)}, f32[128,128]{1,0:T(8,128)S(1)}, u32[]{:S(2)}, u32[]{:S(2)}) collective-permute-start(f32[128,128]{1,0:T(8,128)S(1)} %get-tuple-element.24.refs_1_.second_ref), channel_id=1, source_target_pairs={{1,2},{3,4},{5,6},{2,1},{4,3},{6,5},{9,10},{11,12},{13,14},{10,9},... | collective-permute-start | bytes 196616 | tf_op jit(solution)/shard_map/ppermute | solution.py:430
  42.9 4.9 %collective-permute-start.4 = (f32[128,128]{1,0:T(8,128)S(1)}, f32[128,128]{1,0:T(8,128)S(1)}, u32[]{:S(2)}, u32[]{:S(2)}) collective-permute-start(f32[128,128]{1,0:T(8,128)S(1)} %get-tuple-element.24.refs_1_.second_ref), channel_id=1, source_target_pairs={{0,1},{1,0},{2,3},{3,2},{4,5},{5,4},{6,7},{7,6},{8,9},{9,8},{10,11... | collective-permute-start | bytes 196616 | tf_op jit(solution)/shard_map/ppermute | solution.py:431
  52.2 1.8 %collective-permute-start.6 = (f32[1,128]{1,0:T(1,128)S(1)}, f32[1,128]{1,0:T(1,128)S(1)}, u32[]{:S(2)}, u32[]{:S(2)}) collective-permute-start(f32[1,128]{1,0:T(1,128)S(1)} %get-tuple-element.25), channel_id=1, source_target_pairs={{0,1},{1,0},{2,3},{3,2},{4,5},{5,4},{6,7},{7,6},{8,9},{9,8},{10,11... | collective-permute-start | bytes 1544 | tf_op jit(solution)/shard_map/ppermute | solution.py:446
  54.0 6.1 %collective-permute-start.9 = (f32[1,128]{1,0:T(1,128)S(1)}, f32[1,128]{1,0:T(1,128)S(1)}, u32[]{:S(2)}, u32[]{:S(2)}) collective-permute-start(f32[1,128]{1,0:T(1,128)S(1)} %add.17.parts_ref), channel_id=1, source_target_pairs={{0,6},{1,7},{2,0},{3,1},{4,2},{5,3},{6,4},{7,5},{8,14},{9,15},{10,... | collective-permute-start | bytes 1544 | tf_op jit(solution)/shard_map/ppermute | solution.py:448
  56.2 4.8 %collective-permute-start.8 = (f32[1,128]{1,0:T(1,128)S(1)}, f32[1,128]{1,0:T(1,128)S(1)}, u32[]{:S(2)}, u32[]{:S(2)}) collective-permute-start(f32[1,128]{1,0:T(1,128)S(1)} %add.17.parts_ref), channel_id=1, source_target_pairs={{0,2},{1,3},{2,4},{3,5},{4,6},{5,7},{6,0},{7,1},{8,10},{9,11},{10,... | collective-permute-start | bytes 1544 | tf_op jit(solution)/shard_map/ppermute | solution.py:448
  56.2 5.1 %collective-permute-start.7 = (f32[1,128]{1,0:T(1,128)S(1)}, f32[1,128]{1,0:T(1,128)S(1)}, u32[]{:S(2)}, u32[]{:S(2)}) collective-permute-start(f32[1,128]{1,0:T(1,128)S(1)} %add.17.parts_ref), channel_id=1, source_target_pairs={{0,4},{1,5},{2,6},{3,7},{4,0},{5,1},{6,2},{7,3},{8,12},{9,13},{10,... | collective-permute-start | bytes 1544 | tf_op jit(solution)/shard_map/ppermute | solution.py:448

commit v5 on v4

--- a/solution.py
+++ b/solution.py
@@ -71,7 +71,10 @@
     return row
 
 
-def pack_kernel(each, pos_hbm, charge_hbm, force_hbm, owner_hbm, out_ref, target_ref, charge, owner, sems):
+def pack_kernel(
+    each, pos_hbm, charge_hbm, force_hbm, owner_hbm, tiles_hbm,
+    out_ref, target_ref, index_ref, charge, owner, tiles, sems,
+):
     count = charge.shape[0]
     copies = [
         pltpu.make_async_copy(source, target, sems.at[j])
@@ -81,6 +84,7 @@
                 (charge_hbm, charge),
                 (force_hbm, out_ref.at[4]),
                 (owner_hbm, owner),
+                (tiles_hbm, tiles),
             )
         )
     ]
@@ -97,6 +101,11 @@
     matching = jnp.where((owners.T == owners) & earlier, 1.0, 0.0)
     position = jnp.sum(matching, axis=0, keepdims=True).astype(jnp.int32)
     target_ref[...] = owner[...] * each + position
+    layers = lax.axis_size("slab")
+    here = lax.axis_index("slab")
+    layer = (tiles[...] >> (count.bit_length() - 1)) & (layers - 1)
+    part = jnp.where(layer == here, 0, jnp.where(layer == (here ^ 1), 1, 2))
+    index_ref[...] = (tiles[...] & (count - 1)) + part * count
 
 
 def weights_kernel(scale, first, blocks_count, index_ref, planes, blocks_ref, scratch, finish):
@@ -124,7 +133,7 @@
 
     def entries(t):
         for k in range(blocks_count):
-            u = t if first + k == 0 else index_ref[t * 4 + first + k - 1]
+            u = t if first + k == 0 else index_ref[first + k - 1, t]
             yield raw[pl.ds(pl.multiple_of(u * 8, 8), 8), :]
 
     def terms(t):
@@ -278,30 +287,60 @@
     )(index, own, near, far, total, image, in_hbm(drag))
 
 
+def own_image_kernel(vector_ref, blocks_ref, out_ref, parts, images):
+    count = vector_ref.shape[0]
+    for j, value in enumerate(split2(vector_ref[...])):
+        put_rows(parts, j, value)
+
+    def tile(t, carry):
+        place = pl.ds(pl.multiple_of(t * 8, 8), 8)
+        images[place, :] = jnp.dot(
+            parts[place, :].astype(BF16), blocks_ref[t], preferred_element_type=F32
+        )
+        return carry
+
+    lax.fori_loop(0, count, tile, 0, unroll=UNROLL)
+    out_ref[...] = rows_at(images, 0, count) + rows_at(images, 1, count)
+
+
+def own_image(vector, blocks):
+    count = vector.shape[0]
+    return pl.pallas_call(
+        own_image_kernel,
+        in_specs=[VMEM] * 2,
+        out_specs=VMEM,
+        out_shape=jax.ShapeDtypeStruct(vector.shape, F32),
+        scratch_shapes=[pltpu.VMEM((count * 8, 128), F32)] * 2,
+        compiler_params=pltpu.CompilerParams(vmem_limit_bytes=LIMIT),
+        cost_estimate=pl.CostEstimate(
+            flops=count * 128 * 128 * 512, bytes_accessed=1 << 22, transcendentals=0
+        ),
+        name="own_image",
+    )(vector, blocks)
+
+
 def image_kernel(
-    history, index_ref, own_blocks, blocks_ref, diagonal_ref, row_ref, near_ref, far_ref, own_ref, *refs
+    history, index_ref, blocks_ref, coupled_ref, diagonal_ref, row_ref, near_ref, far_ref, own_ref, *refs
 ):
     past, refs = [own_ref.at[4], *refs[:history]], refs[history:]
     vector_ref, totals_ref, parts, images = refs
     count = diagonal_ref.shape[0]
     for part, ref in enumerate((past[-1], near_ref, far_ref)):
-        high, low = split2(ref[...])
-        put_rows(parts, part * count * 8, high)
-        put_rows(parts, part * count * 8 + 1, low)
+        for j, value in enumerate(split2(ref[...])):
+            put_rows(parts, part * count * 8 + j, value)
 
     def tile(t, carry):
         lefts = []
-        for k in range(1 + blocks_ref.shape[1] // 128):
-            u = t if k == 0 else index_ref[t * 4 + k - 1]
+        for k in range(blocks_ref.shape[1] // 128):
+            u = index_ref[k, t]
             lefts.append(parts[pl.ds(pl.multiple_of(u * 8, 8), 8), :].astype(BF16))
-        left = jnp.concatenate(lefts[1:], axis=1)
-        value = jnp.dot(left, blocks_ref[t], preferred_element_type=F32)
-        value = value + jnp.dot(lefts[0], own_blocks[t], preferred_element_type=F32)
-        images[pl.ds(pl.multiple_of(t * 8, 8), 8), :] = value
+        images[pl.ds(pl.multiple_of(t * 8, 8), 8), :] = jnp.dot(
+            jnp.concatenate(lefts, axis=1), blocks_ref[t], preferred_element_type=F32
+        )
         return carry
 
     lax.fori_loop(0, count, tile, 0, unroll=UNROLL)
-    coupled = rows_at(images, 0, count) + rows_at(images, 1, count)
+    coupled = coupled_ref[...] + rows_at(images, 0, count) + rows_at(images, 1, count)
     vectors = [ref[...] for ref in past]
     vector = (diagonal_ref[...] - SHIFT) * vectors[-1] - coupled
     vectors.append(vector)
@@ -309,9 +348,9 @@
     totals_ref[...] = add_dots(row_ref[...], vectors)
 
 
-def image(index, blocks, diagonal, row, near, far, own, past):
+def image(index, blocks, coupled, diagonal, row, near, far, own, past):
     count = diagonal.shape[0]
-    operands = [*blocks, diagonal, row, near, far, own, *past]
+    operands = [blocks, coupled, diagonal, row, near, far, own, *past]
     return pl.pallas_call(
         functools.partial(image_kernel, len(past)),
         in_specs=[SMEM] + [VMEM] * len(operands),
@@ -380,16 +419,29 @@
     return solution, residual
 
 
-def finish_kernel(arrived_ref, solution_ref, residual_ref):
+def finish_kernel(arrived_ref, solution_hbm, residual_hbm, solution_ref, residual_ref, sems):
     owners, rows_each, _ = arrived_ref.shape
     each = (rows_each - 8) // 4
     totals = sum(arrived_ref[owner, pl.ds(rows_each - 8, 8), :] for owner in range(owners))
     solution, residual = coefficients(totals[:1])
-    for owner in range(owners):
-        basis = [arrived_ref[owner, pl.ds(each * j, each), :] for j in range(4)]
-        place = pl.ds(each * owner, each)
-        solution_ref[place, :] = sum(a * v for a, v in zip(solution, basis))
-        residual_ref[place, :] = sum(a * v for a, v in zip(residual, basis))
+    pieces = sems.shape[1]
+    share = owners // pieces
+    copies = []
+    for piece in range(pieces):
+        for owner in range(share * piece, share * (piece + 1)):
+            basis = [arrived_ref[owner, pl.ds(each * j, each), :] for j in range(4)]
+            place = pl.ds(each * owner, each)
+            solution_ref[place, :] = sum(a * v for a, v in zip(solution, basis))
+            residual_ref[place, :] = sum(a * v for a, v in zip(residual, basis))
+        place = pl.ds(each * share * piece, each * share)
+        for j, (source, target) in enumerate(
+            ((solution_ref, solution_hbm), (residual_ref, residual_hbm))
+        ):
+            copy = pltpu.make_async_copy(source.at[place], target.at[place], sems.at[j, piece])
+            copy.start()
+            copies.append(copy)
+    for copy in copies:
+        copy.wait()
 
 
 def local(positions, charges, drag, right_side, neighbours, owners):
@@ -397,52 +449,50 @@
     brick_count = lax.axis_size("brick")
     slab_count = lax.axis_size("slab")
     each = max(3, 3 * count // brick_count)
-    slab_at = lax.axis_index("slab")
-    first_tile = (lax.axis_index("brick") * slab_count + slab_at) * count
+    entries = neighbours.shape[1]
+    assert count & (count - 1) == 0 and slab_count & (slab_count - 1) == 0
     inner = [(i, i ^ 1) for i in range(slab_count)]
     outer = [(i, i + 1) for i in range(1, slab_count - 1, 2)]
     outer = outer + [(target, source) for source, target in outer]
 
-    packed, target = pl.pallas_call(
+    packed, target, index = pl.pallas_call(
         functools.partial(pack_kernel, each),
         out_shape=[
             jax.ShapeDtypeStruct((5, count, 128), F32),
             jax.ShapeDtypeStruct((1, count), jnp.int32),
-        ],
-        in_specs=[HBM] * 4,
-        out_specs=[VMEM] * 2,
+            jax.ShapeDtypeStruct((entries, count), jnp.int32),
+        ],
+        in_specs=[HBM] * 5,
+        out_specs=[VMEM] * 3,
         scratch_shapes=[
             pltpu.VMEM((count, 128), F32),
             pltpu.VMEM((1, count), jnp.int32),
-            pltpu.SemaphoreType.DMA((4,)),
+            pltpu.VMEM((entries, count), jnp.int32),
+            pltpu.SemaphoreType.DMA((5,)),
         ],
         compiler_params=pltpu.CompilerParams(vmem_limit_bytes=LIMIT),
         name="pack",
-    )(*map(in_hbm, (jnp.transpose(positions, (1, 0, 2)), charges, right_side, owners.reshape(1, count))))
-
-    offset = neighbours - first_tile
-    layer = jnp.floor_divide(offset, count)
-    partner = 1 - 2 * (slab_at % 2)
-    part = jnp.where(layer == 0, 0, jnp.where(layer == partner, 1, 2))
-    index = (offset - layer * count + part * count).reshape(-1)
+    )(*map(in_hbm, (jnp.transpose(positions, (1, 0, 2)), charges, right_side, owners.T, neighbours.T)))
 
     def both_sides(value):
         far = lax.ppermute(value, "slab", outer)
         near = lax.ppermute(value, "slab", inner)
         return near, far
 
-    scale = 8.0 / ((neighbours.shape[1] + 1) * 128)
-    entries = neighbours.shape[1]
+    scale = 8.0 / ((entries + 1) * 128)
     near, far = both_sides(packed)
     own_blocks, total, coupled = own_weights(packed, scale)
     blocks, first, diagonal, row = other_weights(
         index, packed, near, far, total, coupled, drag, scale, entries
     )
-    blocks = own_blocks, blocks
     near, far = both_sides(first)
-    second, row = image(index, blocks, diagonal, row, near, far, packed, [first])
+    coupled = own_image(first, own_blocks)
+    second, row = image(index, blocks, coupled, diagonal, row, near, far, packed, [first])
     near, far = both_sides(second)
-    third, row = image(index, blocks, diagonal, row, near, far, packed, [first, second])
+    coupled = own_image(second, own_blocks)
+    third, row = image(
+        index, blocks, coupled, diagonal, row, near, far, packed, [first, second]
+    )
     row = row + lax.ppermute(row, "slab", inner)
     around = [
         lax.ppermute(row, "slab", [(i, (i + step) % slab_count) for i in range(slab_count)])
@@ -474,7 +524,12 @@
         finish_kernel,
         out_shape=(shape, shape),
         in_specs=[VMEM],
-        out_specs=(VMEM, VMEM),
+        out_specs=(HBM, HBM),
+        scratch_shapes=[
+            pltpu.VMEM(shape.shape, F32),
+            pltpu.VMEM(shape.shape, F32),
+            pltpu.SemaphoreType.DMA((2, 4)),
+        ],
         compiler_params=pltpu.CompilerParams(vmem_limit_bytes=LIMIT),
         name="finish",
     )(arrived)

time: 83 us -> 80 us (0.964)
  waiting for transfers between devices: 3.76 us -> 1.97 us
  starting transfers between devices: 19.4 us -> 18.4 us
    pallas_call x0 -> x2, Pallas kernels: none -> 2.75 us  [own_image(): pl.pallas_call(own_image_kernel, in_specs=[VMEM] * 2, out_specs=VMEM, out...]
    pallas_call x2, Pallas kernels: 8.75 us -> 6.48 us  [image(): pl.pallas_call(functools.partial(image_kernel, len(past)), in_specs=[SMEM...]
    ppermute x3, waiting for transfers between devices: 1.8 us -> 0.01 us  [both_sides(): near = lax.ppermute(value, 'slab', inner)]
  transfers between devices with their start and end apart: 10 -> 10, of which waited for: 5 -> 3; matrix products, arithmetic and copies ran while one was open for 1% -> 0% of each run, Pallas kernels for 8% -> 12%
where the time goes in v5:
time: 80 us; the launch traced here: 79.7 us
  Pallas kernels  38 us (48%)
  blocking collectives  20.5 us (26%)
  starting transfers between devices  18.4 us (23%)
  waiting for transfers between devices  1.97 us (2%)
    all_to_all x1, blocking collectives, local(): lax.all_to_all(outgoing, 'brick', split_axis=0, concat_axis=0, tiled=True)  20.5 us
    pallas_call x1, Pallas kernels, other_weights(): pl.pallas_call(functools.partial(other_kernel, scale, blocks_count), in_s...  19.8 us
    ppermute x3, starting transfers between devices, both_sides(): near = lax.ppermute(value, 'slab', inner)  10.3 us
    pallas_call x2, Pallas kernels, image(): pl.pallas_call(functools.partial(image_kernel, len(past)), in_specs=[SMEM...  6.48 us
    pallas_call x1, Pallas kernels, own_weights(): pl.pallas_call(functools.partial(own_kernel, scale), in_specs=[VMEM], out...  6.42 us
    ppermute x3, starting transfers between devices, local(): lax.ppermute(row, 'slab', [(i, (i + step) % slab_count) for i in range(sl...  5.66 us
    pallas_call x2, Pallas kernels, own_image(): pl.pallas_call(own_image_kernel, in_specs=[VMEM] * 2, out_specs=VMEM, out...  2.75 us
    ppermute x3, starting transfers between devices, both_sides(): far = lax.ppermute(value, 'slab', outer)  2 us
  transfers between devices with their start and end apart: 10, of which 3 were waited for; matrix products, arithmetic and copies ran while one was open for 0% of the time, Pallas kernels for 12%

profile of v5, /device:TPU:0, one launch (start us, length us, event | category | flops | bytes accessed | tf_op | source)
XLA Modules:
  0.0 79.7 jit_solution(2472314905005528719)
XLA Ops:
  0.6 1.1 %pack.1 = (f32[5,128,128]{2,1,0:T(8,128)S(1)}, s32[1,128]{1,0:T(1,128)S(1)}, s32[4,128]{1,0:T(4,128)S(1)}) custom-call(f32[3,128,128]{2,1,0:T(8,128)} %bitcast.3, f32[128,128]{1,0:T(8,128)} %charge_hbm.1, f32[128,128]{1,0:T(8,128)} %force_hbm.1, s32[1,128]{1,0:T(1,128)} %bitcast.5, s32[4,128]{1,0:T(4,128)} %bitcast.4), custom_call_target="tpu_custom_call" | custom-call | tf_op jit(solution)/shard_map/pack/pallas_call | solution.py:458
  1.8 0.7 collective-permute-start.1
  2.5 3.5 %collective-permute-start = (f32[5,128,128]{2,1,0:T(8,128)S(1)}, f32[5,128,128]{2,1,0:T(8,128)S(1)}, u32[]{:S(2)}, u32[]{:S(2)}) collective-permute-start(f32[5,128,128]{2,1,0:T(8,128)S(1)} %get-tuple-element.17.own_ref), channel_id=1, source_target_pairs={{0,1},{1,0},{2,3},{3,2},{4,5},{5,4},{6,7},{7,6},{8,9},{9,8},{10,11... | collective-permute-start | bytes 983048 | tf_op jit(solution)/shard_map/ppermute | solution.py:479
  5.9 6.4 %own_weights.1 = (bf16[128,128,128]{2,1,0:T(8,128)(2,1)S(1)}, f32[128,128]{1,0:T(8,128)S(1)}, f32[128,128]{1,0:T(8,128)S(1)}) custom-call(f32[5,128,128]{2,1,0:T(8,128)S(1)} %get-tuple-element.17.own_ref), custom_call_target="tpu_custom_call" | custom-call | flops 1258291200 | bytes 1048576 | tf_op jit(solution)/shard_map/own_weights/pallas_call | solution.py:233
  12.4 0.0 collective-permute-done.near_ref
  12.4 19.8 %other_weights.1 = (bf16[128,512,128]{2,1,0:T(8,128)(2,1)S(1)}, f32[128,128]{1,0:T(8,128)S(1)}, f32[128,128]{1,0:T(8,128)S(1)}, f32[1,128]{1,0:T(1,128)S(1)}) custom-call(s32[4,128]{1,0:T(4,128)S(1)} %get-tuple-element.16.index_ref, f32[5,128,128]{2,1,0:T(8,128)S(1)} %get-tuple-element.17.own_ref, f32[5,128,128]{2,1,0:T(8,128)S(1)} %collective-permute-done.near_ref, ...), custom_call_target="tpu_custom_call" | custom-call | tf_op jit(solution)/shard_map/other_weights/pallas_call | solution.py:270
  32.2 0.7 collective-permute-start.3
  32.9 3.3 %collective-permute-start.2 = (f32[128,128]{1,0:T(8,128)S(1)}, f32[128,128]{1,0:T(8,128)S(1)}, u32[]{:S(2)}, u32[]{:S(2)}) collective-permute-start(f32[128,128]{1,0:T(8,128)S(1)} %get-tuple-element.21.vector_ref.refs_0_.first_ref), channel_id=1, source_target_pairs={{0,1},{1,0},{2,3},{3,2},{4,5},{5,4},{6,7},{7,6},{8,9},{9,8},{10,11... | collective-permute-start | bytes 196616 | tf_op jit(solution)/shard_map/ppermute | solution.py:479
  36.2 1.4 %own_image.2.coupled_ref = f32[128,128]{1,0:T(8,128)S(1)} custom-call(f32[128,128]{1,0:T(8,128)S(1)} %get-tuple-element.21.vector_ref.refs_0_.first_ref, bf16[128,128,128]{2,1,0:T(8,128)(2,1)S(1)} %get-tuple-element.22.blocks_ref), custom_call_target="tpu_custom_call" | custom-call | flops 1073741824 | bytes 4194304 | tf_op jit(solution)/shard_map/own_image/pallas_call | solution.py:308
  37.6 0.0 collective-permute-done.2.near_ref
  37.6 3.2 %image.2 = (f32[128,128]{1,0:T(8,128)S(1)}, f32[1,128]{1,0:T(1,128)S(1)}) custom-call(s32[4,128]{1,0:T(4,128)S(1)} %get-tuple-element.16.index_ref, bf16[128,512,128]{2,1,0:T(8,128)(2,1)S(1)} %get-tuple-element.20.blocks_ref, f32[128,128]{1,0:T(8,128)S(1)} %own_image.2.coupled_ref, f32[128,128]{1,0:T(8,128)S(1)} %get-tuple-element.23.diagonal_ref, ...), custom_call_target="tpu_custom_call" | custom-call | tf_op jit(solution)/shard_map/image/pallas_call | solution.py:354
  40.9 0.7 collective-permute-start.5
  41.5 3.5 %collective-permute-start.4 = (f32[128,128]{1,0:T(8,128)S(1)}, f32[128,128]{1,0:T(8,128)S(1)}, u32[]{:S(2)}, u32[]{:S(2)}) collective-permute-start(f32[128,128]{1,0:T(8,128)S(1)} %get-tuple-element.25.vector_ref.refs_1_.second_ref), channel_id=1, source_target_pairs={{0,1},{1,0},{2,3},{3,2},{4,5},{5,4},{6,7},{7,6},{8,9},{9,8},{10,11... | collective-permute-start | bytes 196616 | tf_op jit(solution)/shard_map/ppermute | solution.py:479
  45.0 1.4 %own_image.3.coupled_ref = f32[128,128]{1,0:T(8,128)S(1)} custom-call(f32[128,128]{1,0:T(8,128)S(1)} %get-tuple-element.25.vector_ref.refs_1_.second_ref, bf16[128,128,128]{2,1,0:T(8,128)(2,1)S(1)} %get-tuple-element.22.blocks_ref), custom_call_target="tpu_custom_call" | custom-call | flops 1073741824 | bytes 4194304 | tf_op jit(solution)/shard_map/own_image/pallas_call | solution.py:308
  46.4 3.2 %image.3 = (f32[128,128]{1,0:T(8,128)S(1)}, f32[1,128]{1,0:T(1,128)S(1)}) custom-call(s32[4,128]{1,0:T(4,128)S(1)} %get-tuple-element.16.index_ref, bf16[128,512,128]{2,1,0:T(8,128)(2,1)S(1)} %get-tuple-element.20.blocks_ref, f32[128,128]{1,0:T(8,128)S(1)} %own_image.3.coupled_ref, f32[128,128]{1,0:T(8,128)S(1)} %get-tuple-element.23.diagonal_ref, ...), custom_call_target="tpu_custom_call" | custom-call | tf_op jit(solution)/shard_map/image/pallas_call | solution.py:354
  49.7 0.5 collective-permute-start.6
  50.2 0.8 %collective-permute-done.6 = f32[1,128]{1,0:T(1,128)S(1)} collective-permute-done((f32[1,128]{1,0:T(1,128)S(1)}, f32[1,128]{1,0:T(1,128)S(1)}, u32[]{:S(2)}, u32[]{:S(2)}) %collective-permute-start.6) | collective-permute-done | bytes 544 | tf_op jit(solution)/shard_map/ppermute | solution.py:496
  51.0 2.2 %collective-permute-start.9 = (f32[1,128]{1,0:T(1,128)S(1)}, f32[1,128]{1,0:T(1,128)S(1)}, u32[]{:S(2)}, u32[]{:S(2)}) collective-permute-start(f32[1,128]{1,0:T(1,128)S(1)} %add.3.parts_ref), channel_id=1, source_target_pairs={{0,6},{1,7},{2,0},{3,1},{4,2},{5,3},{6,4},{7,5},{8,14},{9,15},{10,... | collective-permute-start | bytes 1544 | tf_op jit(solution)/shard_map/ppermute | solution.py:498
  53.2 3.5 %collective-permute-start.7 = (f32[1,128]{1,0:T(1,128)S(1)}, f32[1,128]{1,0:T(1,128)S(1)}, u32[]{:S(2)}, u32[]{:S(2)}) collective-permute-start(f32[1,128]{1,0:T(1,128)S(1)} %add.3.parts_ref), channel_id=1, source_target_pairs={{0,4},{1,5},{2,6},{3,7},{4,0},{5,1},{6,2},{7,3},{8,12},{9,13},{10,... | collective-permute-start | bytes 1544 | tf_op jit(solution)/shard_map/ppermute | solution.py:498
  56.6 0.5 slots.1.refs_3_
  57.1 0.8 %collective-permute-done.8.refs_1_ = f32[1,128]{1,0:T(1,128)S(1)} collective-permute-done((f32[1,128]{1,0:T(1,128)S(1)}, f32[1,128]{1,0:T(1,128)S(1)}, u32[]{:S(2)}, u32[]{:S(2)}) %collective-permute-start.8) | collective-permute-done | bytes 544 | tf_op jit(solution)/shard_map/ppermute | solution.py:498
  57.9 0.3 collective-permute-done.7.refs_0_
  58.2 20.5 %all_to_all.5.arrived_ref = f32[16,104,128]{2,1,0:T(8,128)S(1)} all-to-all(f32[16,104,128]{2,1,0:T(8,128)S(1)} %join.1), channel_id=1, replica_groups=mesh['brick'=16,'slab'=8] {'brick'}, dimensions={0} | all-to-all | bytes 1703936 | tf_op jit(solution)/shard_map/all_to_all | solution.py:521
  78.8 1.0 %finish.1 = (f32[384,128]{1,0:T(8,128)}, f32[384,128]{1,0:T(8,128)}) custom-call(f32[16,104,128]{2,1,0:T(8,128)S(1)} %all_to_all.5.arrived_ref), custom_call_target="tpu_custom_call" | custom-call | tf_op jit(solution)/shard_map/finish/pallas_call | solution.py:523
  (8 shorter events, 0.0 us)
Async XLA Ops:
  1.8 10.6 %collective-permute-start.1 = (f32[5,128,128]{2,1,0:T(8,128)S(1)}, f32[5,128,128]{2,1,0:T(8,128)S(1)}, u32[]{:S(2)}, u32[]{:S(2)}) collective-permute-start(f32[5,128,128]{2,1,0:T(8,128)S(1)} %get-tuple-element.17.own_ref), channel_id=1, source_target_pairs={{1,2},{3,4},{5,6},{2,1},{4,3},{6,5},{9,10},{11,12},{13,14},{10,9},... | collective-permute-start | bytes 983048 | tf_op jit(solution)/shard_map/ppermute | solution.py:478
  2.5 9.9 %collective-permute-start = (f32[5,128,128]{2,1,0:T(8,128)S(1)}, f32[5,128,128]{2,1,0:T(8,128)S(1)}, u32[]{:S(2)}, u32[]{:S(2)}) collective-permute-start(f32[5,128,128]{2,1,0:T(8,128)S(1)} %get-tuple-element.17.own_ref), channel_id=1, source_target_pairs={{0,1},{1,0},{2,3},{3,2},{4,5},{5,4},{6,7},{7,6},{8,9},{9,8},{10,11... | collective-permute-start | bytes 983048 | tf_op jit(solution)/shard_map/ppermute | solution.py:479
  32.2 5.4 %collective-permute-start.3 = (f32[128,128]{1,0:T(8,128)S(1)}, f32[128,128]{1,0:T(8,128)S(1)}, u32[]{:S(2)}, u32[]{:S(2)}) collective-permute-start(f32[128,128]{1,0:T(8,128)S(1)} %get-tuple-element.21.vector_ref.refs_0_.first_ref), channel_id=1, source_target_pairs={{1,2},{3,4},{5,6},{2,1},{4,3},{6,5},{9,10},{11,12},{13,14},{10,9},... | collective-permute-start | bytes 196616 | tf_op jit(solution)/shard_map/ppermute | solution.py:478
  32.9 4.7 %collective-permute-start.2 = (f32[128,128]{1,0:T(8,128)S(1)}, f32[128,128]{1,0:T(8,128)S(1)}, u32[]{:S(2)}, u32[]{:S(2)}) collective-permute-start(f32[128,128]{1,0:T(8,128)S(1)} %get-tuple-element.21.vector_ref.refs_0_.first_ref), channel_id=1, source_target_pairs={{0,1},{1,0},{2,3},{3,2},{4,5},{5,4},{6,7},{7,6},{8,9},{9,8},{10,11... | collective-permute-start | bytes 196616 | tf_op jit(solution)/shard_map/ppermute | solution.py:479
  40.9 5.6 %collective-permute-start.5 = (f32[128,128]{1,0:T(8,128)S(1)}, f32[128,128]{1,0:T(8,128)S(1)}, u32[]{:S(2)}, u32[]{:S(2)}) collective-permute-start(f32[128,128]{1,0:T(8,128)S(1)} %get-tuple-element.25.vector_ref.refs_1_.second_ref), channel_id=1, source_target_pairs={{1,2},{3,4},{5,6},{2,1},{4,3},{6,5},{9,10},{11,12},{13,14},{10,9},... | collective-permute-start | bytes 196616 | tf_op jit(solution)/shard_map/ppermute | solution.py:478
  41.5 4.9 %collective-permute-start.4 = (f32[128,128]{1,0:T(8,128)S(1)}, f32[128,128]{1,0:T(8,128)S(1)}, u32[]{:S(2)}, u32[]{:S(2)}) collective-permute-start(f32[128,128]{1,0:T(8,128)S(1)} %get-tuple-element.25.vector_ref.refs_1_.second_ref), channel_id=1, source_target_pairs={{0,1},{1,0},{2,3},{3,2},{4,5},{5,4},{6,7},{7,6},{8,9},{9,8},{10,11... | collective-permute-start | bytes 196616 | tf_op jit(solution)/shard_map/ppermute | solution.py:479
  49.7 1.3 %collective-permute-start.6 = (f32[1,128]{1,0:T(1,128)S(1)}, f32[1,128]{1,0:T(1,128)S(1)}, u32[]{:S(2)}, u32[]{:S(2)}) collective-permute-start(f32[1,128]{1,0:T(1,128)S(1)} %get-tuple-element.27), channel_id=1, source_target_pairs={{0,1},{1,0},{2,3},{3,2},{4,5},{5,4},{6,7},{7,6},{8,9},{9,8},{10,11... | collective-permute-start | bytes 1544 | tf_op jit(solution)/shard_map/ppermute | solution.py:496
  51.0 6.1 %collective-permute-start.9 = (f32[1,128]{1,0:T(1,128)S(1)}, f32[1,128]{1,0:T(1,128)S(1)}, u32[]{:S(2)}, u32[]{:S(2)}) collective-permute-start(f32[1,128]{1,0:T(1,128)S(1)} %add.3.parts_ref), channel_id=1, source_target_pairs={{0,6},{1,7},{2,0},{3,1},{4,2},{5,3},{6,4},{7,5},{8,14},{9,15},{10,... | collective-permute-start | bytes 1544 | tf_op jit(solution)/shard_map/ppermute | solution.py:498
  53.2 4.8 %collective-permute-start.8 = (f32[1,128]{1,0:T(1,128)S(1)}, f32[1,128]{1,0:T(1,128)S(1)}, u32[]{:S(2)}, u32[]{:S(2)}) collective-permute-start(f32[1,128]{1,0:T(1,128)S(1)} %add.3.parts_ref), channel_id=1, source_target_pairs={{0,2},{1,3},{2,4},{3,5},{4,6},{5,7},{6,0},{7,1},{8,10},{9,11},{10,... | collective-permute-start | bytes 1544 | tf_op jit(solution)/shard_map/ppermute | solution.py:498
  53.2 5.1 %collective-permute-start.7 = (f32[1,128]{1,0:T(1,128)S(1)}, f32[1,128]{1,0:T(1,128)S(1)}, u32[]{:S(2)}, u32[]{:S(2)}) collective-permute-start(f32[1,128]{1,0:T(1,128)S(1)} %add.3.parts_ref), channel_id=1, source_target_pairs={{0,4},{1,5},{2,6},{3,7},{4,0},{5,1},{6,2},{7,3},{8,12},{9,13},{10,... | collective-permute-start | bytes 1544 | tf_op jit(solution)/shard_map/ppermute | solution.py:498

commit v6 on v5

--- a/solution.py
+++ b/solution.py
@@ -9,10 +9,9 @@
 
 ITERS = 3
 SHIFT = 7.0
-MIX = 7
 UNROLL = 64
-GROUP = 8
-OWN_GROUP = 16
+OWN = (16, 16, 7, 0)
+OTHER = (32, 4, 0, 256)
 LOG2E = 1.4426950408889634
 F32 = jnp.float32
 BF16 = jnp.bfloat16
@@ -108,11 +107,15 @@
     index_ref[...] = (tiles[...] & (count - 1)) + part * count
 
 
-def weights_kernel(scale, first, blocks_count, index_ref, planes, blocks_ref, scratch, finish):
+def weights_kernel(
+    scale, first, blocks_count, tuning, index_ref, planes, blocks_ref, scratch, finish
+):
     raw, mine, sums, images, *buffers = scratch
-    buffers, ring = buffers[: len(buffers) // 2], buffers[len(buffers) // 2 :]
-    group = len(buffers)
-    count = mine.shape[0] // 16
+    group, lag, mix, split = tuning
+    parts = 2 if split else 1
+    buffers, ring = buffers[: parts * lag], buffers[parts * lag :]
+    buffers = [buffers[i::lag] for i in range(lag)]
+    count = mine.shape[0] // 24
     square = LOG2E * LOG2E
     width = 128 * blocks_count
     one = jnp.ones((count, 128), F32)
@@ -126,10 +129,13 @@
             put_rows(raw, base + j, value)
         if part == 0:
             doubled = (-2.0 * square) * x, (-2.0 * square) * y, (-2.0 * square) * z
-            rows = (*doubled, zero, one * square, (norm + 0.5) * square, zero, zero)
+            rows = (*doubled, zero, one * square, (norm + 0.01) * square, zero, zero)
             rows += (zero, zero, zero, one, zero, charge + jnp.log2(scale * one), zero, zero)
+            if split:
+                doubled = (-2.0 / scale) * x, (-2.0 / scale) * y, (-2.0 / scale) * z
+                rows += (*doubled, zero, one / scale, (norm + 0.5) / scale, zero, zero)
             for j, value in enumerate(rows):
-                mine[pl.ds(j, count, stride=16), :] = value
+                mine[pl.ds(j, count, stride=24), :] = value
 
     def entries(t):
         for k in range(blocks_count):
@@ -138,8 +144,8 @@
 
     def terms(t):
         rights = []
-        for j in range(2):
-            high, middle, low = split3(mine[pl.ds(pl.multiple_of(t * 16 + 8 * j, 8), 8), :])
+        for j in range(3 if split else 2):
+            high, middle, low = split3(mine[pl.ds(pl.multiple_of(t * 24 + 8 * j, 8), 8), :])
             rights.append(jnp.concatenate([high, middle, low, high, middle, high], axis=0))
         right = jnp.concatenate(rights, axis=1)
         lefts = []
@@ -147,28 +153,38 @@
             high, middle, low = split3(value)
             lefts.append(jnp.concatenate([high, high, high, middle, middle, low], axis=0))
         left = jnp.concatenate(lefts, axis=1)
-        return lax.dot_general(
-            left, right, (((0,), (0,)), ((), ())), preferred_element_type=F32
-        )
+        pairs = [(left[:, :split], right)] if split else []
+        pairs.append((left[:, split:], right[:, :256]))
+        return [
+            lax.dot_general(a, b, (((0,), (0,)), ((), ())), preferred_element_type=F32)
+            for a, b in pairs
+        ]
 
     def block(t, source, kept, incoming):
         totals = [None] * 4
         for pair in range(width // 16):
             halves = []
+            part = 0 if 16 * pair < split else -1
+            base = 16 * pair - (0 if part == 0 else split)
             for half in range(2):
                 chunk = 2 * pair + half
-                place = pl.ds(8 * chunk, 8)
-                wide = source[place, :128]
-                shifted = wide - 0.49 * square
-                if (chunk * MIX) % 10 < MIX:
+                place = pl.ds(base + 8 * half, 8)
+                shifted = source[part][place, :128]
+                if part == 0:
                     distance = shifted * lax.rsqrt(shifted)
-                    inverse = pltpu.reciprocal(wide)
+                    inverse = pltpu.reciprocal(source[part][place, 256:])
                 else:
-                    product = wide * shifted
-                    root = lax.rsqrt(product * wide)
-                    distance = product * root
-                    inverse = root * distance
-                weight = inverse * (square * scale) + jnp.exp2(source[place, 128:] - distance)
+                    wide = shifted + 0.49 * square
+                    if (chunk * mix) % 10 < mix:
+                        distance = shifted * lax.rsqrt(shifted)
+                        inverse = pltpu.reciprocal(wide)
+                    else:
+                        product = wide * shifted
+                        root = lax.rsqrt(product * wide)
+                        distance = product * root
+                        inverse = root * distance
+                    inverse = inverse * (square * scale)
+                weight = inverse + jnp.exp2(source[part][place, 128:256] - distance)
                 if first == 0 and chunk < 16:
                     rows = lax.broadcasted_iota(jnp.int32, (8, 128), 0) + 8 * chunk
                     lanes = lax.broadcasted_iota(jnp.int32, (8, 128), 1)
@@ -179,7 +195,7 @@
             rounded = jnp.concatenate(halves, axis=0).astype(BF16)
             blocks_ref[t, pl.ds(16 * pair, 16), :] = rounded
             kept[pl.ds(16 * pair, 16), :] = rounded
-            source[pl.ds(16 * pair, 16), :] = incoming[16 * pair : 16 * pair + 16]
+            source[part][pl.ds(base, 16), :] = incoming[part][base : base + 16]
         total = (totals[0] + totals[1]) + (totals[2] + totals[3])
         sums[pl.ds(pl.multiple_of(t * 8, 8), 8), :] = total
 
@@ -189,33 +205,39 @@
             left, kept[...], preferred_element_type=F32
         )
 
-    for i in range(group):
-        buffers[i][...] = terms(i)
+    for i in range(lag):
+        for target, value in zip(buffers[i], terms(i)):
+            target[...] = value
 
     def tiles(j, carry):
-        t = group * j
         for i in range(group):
-            image(jnp.maximum(t + i - group, 0), ring[i])
-            block(t + i, buffers[i], ring[i], terms(jnp.minimum(t + i + group, count - 1)))
+            t = group * j + i
+            slot = i % lag
+            image(jnp.maximum(t - lag, 0), ring[slot])
+            block(t, buffers[slot], ring[slot], terms(jnp.minimum(t + lag, count - 1)))
         return carry
 
     lax.fori_loop(0, count // group, tiles, 0)
-    for i in range(group):
-        image(count - group + i, ring[i])
+    for i in range(lag):
+        image(count - lag + i, ring[i])
     total = rows_at(sums, 0, count)
     for j in range(1, 8):
         total = total + rows_at(sums, j, count)
     finish(total, rows_at(images, 6, count) + rows_at(images, 7, count))
 
 
-def weights_scratch(count, parts, blocks_count, group):
+def weights_scratch(count, parts, blocks_count, tuning):
+    _, lag, _, split = tuning
+    width = 128 * blocks_count
+    first = [pltpu.VMEM((split, 384), F32)] * lag if split else []
     return [
         pltpu.VMEM((parts * count * 8, 128), F32),
-        pltpu.VMEM((count * 16, 128), F32),
+        pltpu.VMEM((count * 24, 128), F32),
         pltpu.VMEM((count * 8, 128), F32),
         pltpu.VMEM((count * 8, 128), F32),
-        *[pltpu.VMEM((128 * blocks_count, 256), F32)] * group,
-        *[pltpu.VMEM((128 * blocks_count, 128), BF16)] * group,
+        *first,
+        *[pltpu.VMEM((width - split, 256), F32)] * lag,
+        *[pltpu.VMEM((width, 128), BF16)] * lag,
     ]
 
 
@@ -224,7 +246,7 @@
         total_ref[...] = total
         image_ref[...] = coupled
 
-    weights_kernel(scale, 0, 1, None, [own_ref], blocks_ref, scratch, finish)
+    weights_kernel(scale, 0, 1, OWN, None, [own_ref], blocks_ref, scratch, finish)
 
 
 def own_weights(own, scale):
@@ -235,7 +257,7 @@
         in_specs=[VMEM],
         out_specs=[VMEM] * 3,
         out_shape=[pltpu.VMEM((count, 128, 128), BF16), plane, plane],
-        scratch_shapes=weights_scratch(count, 1, 1, OWN_GROUP),
+        scratch_shapes=weights_scratch(count, 1, 1, OWN),
         compiler_params=pltpu.CompilerParams(vmem_limit_bytes=LIMIT),
         cost_estimate=pl.CostEstimate(
             flops=count * 128 * 128 * 600, bytes_accessed=1 << 20, transcendentals=count * 128 * 256
@@ -261,7 +283,7 @@
         row_ref[...] = add_dots(jnp.zeros((1, 128), F32), [force, vector])
 
     planes = [own_ref, near_ref, far_ref]
-    weights_kernel(scale, 1, blocks_count, index_ref, planes, blocks_ref, scratch, finish)
+    weights_kernel(scale, 1, blocks_count, OTHER, index_ref, planes, blocks_ref, scratch, finish)
 
 
 def other_weights(index, own, near, far, total, image, drag, scale, blocks_count):
@@ -280,7 +302,7 @@
         scratch_shapes=[
             pltpu.VMEM((count, 128), F32),
             pltpu.SemaphoreType.DMA,
-            *weights_scratch(count, 3, blocks_count, GROUP),
+            *weights_scratch(count, 3, blocks_count, OTHER),
         ],
         compiler_params=pltpu.CompilerParams(vmem_limit_bytes=LIMIT),
         name="other_weights",

time: 80 us -> 76.6 us (0.957)
  Pallas kernels: 38 us -> 34.5 us
    pallas_call x1, Pallas kernels: 19.8 us -> 16.6 us  [other_weights(): pl.pallas_call(functools.partial(other_kernel, scale, blocks_count), in_s...]
where the time goes in v6:
time: 76.6 us; the launch traced here: 76.4 us
  Pallas kernels  34.5 us (45%)
  blocking collectives  20.5 us (27%)
  starting transfers between devices  18.4 us (24%)
  waiting for transfers between devices  2.06 us (3%)
    all_to_all x1, blocking collectives, local(): lax.all_to_all(outgoing, 'brick', split_axis=0, concat_axis=0, tiled=True)  20.5 us
    pallas_call x1, Pallas kernels, other_weights(): pl.pallas_call(functools.partial(other_kernel, scale, blocks_count), in_s...  16.6 us
    ppermute x3, starting transfers between devices, both_sides(): near = lax.ppermute(value, 'slab', inner)  10.3 us
    pallas_call x2, Pallas kernels, image(): pl.pallas_call(functools.partial(image_kernel, len(past)), in_specs=[SMEM...  6.48 us
    pallas_call x1, Pallas kernels, own_weights(): pl.pallas_call(functools.partial(own_kernel, scale), in_specs=[VMEM], out...  6.14 us
    ppermute x3, starting transfers between devices, local(): lax.ppermute(row, 'slab', [(i, (i + step) % slab_count) for i in range(sl...  5.63 us
    pallas_call x2, Pallas kernels, own_image(): pl.pallas_call(own_image_kernel, in_specs=[VMEM] * 2, out_specs=VMEM, out...  2.75 us
    ppermute x3, starting transfers between devices, both_sides(): far = lax.ppermute(value, 'slab', outer)  2 us
  transfers between devices with their start and end apart: 10, of which 3 were waited for; matrix products, arithmetic and copies ran while one was open for 0% of the time, Pallas kernels for 12%

profile of v6, /device:TPU:0, one launch (start us, length us, event | category | flops | bytes accessed | tf_op | source)
XLA Modules:
  0.0 76.4 jit_solution(14124094517737168030)
XLA Ops:
  0.6 1.1 %pack.1 = (f32[5,128,128]{2,1,0:T(8,128)S(1)}, s32[1,128]{1,0:T(1,128)S(1)}, s32[4,128]{1,0:T(4,128)S(1)}) custom-call(f32[3,128,128]{2,1,0:T(8,128)} %bitcast.3, f32[128,128]{1,0:T(8,128)} %charge_hbm.1, f32[128,128]{1,0:T(8,128)} %force_hbm.1, s32[1,128]{1,0:T(1,128)} %bitcast.5, s32[4,128]{1,0:T(4,128)} %bitcast.4), custom_call_target="tpu_custom_call" | custom-call | tf_op jit(solution)/shard_map/pack/pallas_call | solution.py:480
  1.8 0.7 collective-permute-start.1
  2.5 3.5 %collective-permute-start = (f32[5,128,128]{2,1,0:T(8,128)S(1)}, f32[5,128,128]{2,1,0:T(8,128)S(1)}, u32[]{:S(2)}, u32[]{:S(2)}) collective-permute-start(f32[5,128,128]{2,1,0:T(8,128)S(1)} %get-tuple-element.17.own_ref), channel_id=1, source_target_pairs={{0,1},{1,0},{2,3},{3,2},{4,5},{5,4},{6,7},{7,6},{8,9},{9,8},{10,11... | collective-permute-start | bytes 983048 | tf_op jit(solution)/shard_map/ppermute | solution.py:501
  5.9 6.1 %own_weights.1 = (bf16[128,128,128]{2,1,0:T(8,128)(2,1)S(1)}, f32[128,128]{1,0:T(8,128)S(1)}, f32[128,128]{1,0:T(8,128)S(1)}) custom-call(f32[5,128,128]{2,1,0:T(8,128)S(1)} %get-tuple-element.17.own_ref), custom_call_target="tpu_custom_call" | custom-call | flops 1258291200 | bytes 1048576 | tf_op jit(solution)/shard_map/own_weights/pallas_call | solution.py:255
  12.1 0.0 collective-permute-done.1.far_ref
  12.1 16.6 %other_weights.1 = (bf16[128,512,128]{2,1,0:T(8,128)(2,1)S(1)}, f32[128,128]{1,0:T(8,128)S(1)}, f32[128,128]{1,0:T(8,128)S(1)}, f32[1,128]{1,0:T(1,128)S(1)}) custom-call(s32[4,128]{1,0:T(4,128)S(1)} %get-tuple-element.16.index_ref, f32[5,128,128]{2,1,0:T(8,128)S(1)} %get-tuple-element.17.own_ref, f32[5,128,128]{2,1,0:T(8,128)S(1)} %collective-permute-done.near_ref, ...), custom_call_target="tpu_custom_call" | custom-call | tf_op jit(solution)/shard_map/other_weights/pallas_call | solution.py:292
  28.7 0.7 collective-permute-start.3
  29.4 3.4 %collective-permute-start.2 = (f32[128,128]{1,0:T(8,128)S(1)}, f32[128,128]{1,0:T(8,128)S(1)}, u32[]{:S(2)}, u32[]{:S(2)}) collective-permute-start(f32[128,128]{1,0:T(8,128)S(1)} %get-tuple-element.21.vector_ref.refs_0_.first_ref), channel_id=1, source_target_pairs={{0,1},{1,0},{2,3},{3,2},{4,5},{5,4},{6,7},{7,6},{8,9},{9,8},{10,11... | collective-permute-start | bytes 196616 | tf_op jit(solution)/shard_map/ppermute | solution.py:501
  32.7 1.4 %own_image.2.coupled_ref = f32[128,128]{1,0:T(8,128)S(1)} custom-call(f32[128,128]{1,0:T(8,128)S(1)} %get-tuple-element.21.vector_ref.refs_0_.first_ref, bf16[128,128,128]{2,1,0:T(8,128)(2,1)S(1)} %get-tuple-element.22.blocks_ref), custom_call_target="tpu_custom_call" | custom-call | flops 1073741824 | bytes 4194304 | tf_op jit(solution)/shard_map/own_image/pallas_call | solution.py:330
  34.1 0.0 collective-permute-done.3.far_ref
  34.2 3.2 %image.2 = (f32[128,128]{1,0:T(8,128)S(1)}, f32[1,128]{1,0:T(1,128)S(1)}) custom-call(s32[4,128]{1,0:T(4,128)S(1)} %get-tuple-element.16.index_ref, bf16[128,512,128]{2,1,0:T(8,128)(2,1)S(1)} %get-tuple-element.20.blocks_ref, f32[128,128]{1,0:T(8,128)S(1)} %own_image.2.coupled_ref, f32[128,128]{1,0:T(8,128)S(1)} %get-tuple-element.23.diagonal_ref, ...), custom_call_target="tpu_custom_call" | custom-call | tf_op jit(solution)/shard_map/image/pallas_call | solution.py:376
  37.4 0.7 collective-permute-start.5
  38.1 3.5 %collective-permute-start.4 = (f32[128,128]{1,0:T(8,128)S(1)}, f32[128,128]{1,0:T(8,128)S(1)}, u32[]{:S(2)}, u32[]{:S(2)}) collective-permute-start(f32[128,128]{1,0:T(8,128)S(1)} %get-tuple-element.25.vector_ref.refs_1_.second_ref), channel_id=1, source_target_pairs={{0,1},{1,0},{2,3},{3,2},{4,5},{5,4},{6,7},{7,6},{8,9},{9,8},{10,11... | collective-permute-start | bytes 196616 | tf_op jit(solution)/shard_map/ppermute | solution.py:501
  41.6 1.4 %own_image.3.coupled_ref = f32[128,128]{1,0:T(8,128)S(1)} custom-call(f32[128,128]{1,0:T(8,128)S(1)} %get-tuple-element.25.vector_ref.refs_1_.second_ref, bf16[128,128,128]{2,1,0:T(8,128)(2,1)S(1)} %get-tuple-element.22.blocks_ref), custom_call_target="tpu_custom_call" | custom-call | flops 1073741824 | bytes 4194304 | tf_op jit(solution)/shard_map/own_image/pallas_call | solution.py:330
  43.0 3.2 %image.3 = (f32[128,128]{1,0:T(8,128)S(1)}, f32[1,128]{1,0:T(1,128)S(1)}) custom-call(s32[4,128]{1,0:T(4,128)S(1)} %get-tuple-element.16.index_ref, bf16[128,512,128]{2,1,0:T(8,128)(2,1)S(1)} %get-tuple-element.20.blocks_ref, f32[128,128]{1,0:T(8,128)S(1)} %own_image.3.coupled_ref, f32[128,128]{1,0:T(8,128)S(1)} %get-tuple-element.23.diagonal_ref, ...), custom_call_target="tpu_custom_call" | custom-call | tf_op jit(solution)/shard_map/image/pallas_call | solution.py:376
  46.2 0.5 collective-permute-start.6
  46.7 0.8 %collective-permute-done.6 = f32[1,128]{1,0:T(1,128)S(1)} collective-permute-done((f32[1,128]{1,0:T(1,128)S(1)}, f32[1,128]{1,0:T(1,128)S(1)}, u32[]{:S(2)}, u32[]{:S(2)}) %collective-permute-start.6) | collective-permute-done | bytes 544 | tf_op jit(solution)/shard_map/ppermute | solution.py:518
  47.5 2.3 %collective-permute-start.9 = (f32[1,128]{1,0:T(1,128)S(1)}, f32[1,128]{1,0:T(1,128)S(1)}, u32[]{:S(2)}, u32[]{:S(2)}) collective-permute-start(f32[1,128]{1,0:T(1,128)S(1)} %add.3.parts_ref), channel_id=1, source_target_pairs={{0,6},{1,7},{2,0},{3,1},{4,2},{5,3},{6,4},{7,5},{8,14},{9,15},{10,... | collective-permute-start | bytes 1544 | tf_op jit(solution)/shard_map/ppermute | solution.py:520
  49.8 3.4 %collective-permute-start.7 = (f32[1,128]{1,0:T(1,128)S(1)}, f32[1,128]{1,0:T(1,128)S(1)}, u32[]{:S(2)}, u32[]{:S(2)}) collective-permute-start(f32[1,128]{1,0:T(1,128)S(1)} %add.3.parts_ref), channel_id=1, source_target_pairs={{0,4},{1,5},{2,6},{3,7},{4,0},{5,1},{6,2},{7,3},{8,12},{9,13},{10,... | collective-permute-start | bytes 1544 | tf_op jit(solution)/shard_map/ppermute | solution.py:520
  53.1 0.5 slots.1.refs_3_
  53.6 0.9 %collective-permute-done.8.refs_1_ = f32[1,128]{1,0:T(1,128)S(1)} collective-permute-done((f32[1,128]{1,0:T(1,128)S(1)}, f32[1,128]{1,0:T(1,128)S(1)}, u32[]{:S(2)}, u32[]{:S(2)}) %collective-permute-start.8) | collective-permute-done | bytes 544 | tf_op jit(solution)/shard_map/ppermute | solution.py:520
  54.5 0.3 collective-permute-done.7.refs_0_
  54.9 20.5 %all_to_all.5.arrived_ref = f32[16,104,128]{2,1,0:T(8,128)S(1)} all-to-all(f32[16,104,128]{2,1,0:T(8,128)S(1)} %join.1), channel_id=1, replica_groups=mesh['brick'=16,'slab'=8] {'brick'}, dimensions={0} | all-to-all | bytes 1703936 | tf_op jit(solution)/shard_map/all_to_all | solution.py:543
  75.4 1.0 %finish.1 = (f32[384,128]{1,0:T(8,128)}, f32[384,128]{1,0:T(8,128)}) custom-call(f32[16,104,128]{2,1,0:T(8,128)S(1)} %all_to_all.5.arrived_ref), custom_call_target="tpu_custom_call" | custom-call | tf_op jit(solution)/shard_map/finish/pallas_call | solution.py:545
  (8 shorter events, 0.0 us)
Async XLA Ops:
  1.8 10.3 %collective-permute-start.1 = (f32[5,128,128]{2,1,0:T(8,128)S(1)}, f32[5,128,128]{2,1,0:T(8,128)S(1)}, u32[]{:S(2)}, u32[]{:S(2)}) collective-permute-start(f32[5,128,128]{2,1,0:T(8,128)S(1)} %get-tuple-element.17.own_ref), channel_id=1, source_target_pairs={{1,2},{3,4},{5,6},{2,1},{4,3},{6,5},{9,10},{11,12},{13,14},{10,9},... | collective-permute-start | bytes 983048 | tf_op jit(solution)/shard_map/ppermute | solution.py:500
  2.5 9.6 %collective-permute-start = (f32[5,128,128]{2,1,0:T(8,128)S(1)}, f32[5,128,128]{2,1,0:T(8,128)S(1)}, u32[]{:S(2)}, u32[]{:S(2)}) collective-permute-start(f32[5,128,128]{2,1,0:T(8,128)S(1)} %get-tuple-element.17.own_ref), channel_id=1, source_target_pairs={{0,1},{1,0},{2,3},{3,2},{4,5},{5,4},{6,7},{7,6},{8,9},{9,8},{10,11... | collective-permute-start | bytes 983048 | tf_op jit(solution)/shard_map/ppermute | solution.py:501
  28.7 5.4 %collective-permute-start.3 = (f32[128,128]{1,0:T(8,128)S(1)}, f32[128,128]{1,0:T(8,128)S(1)}, u32[]{:S(2)}, u32[]{:S(2)}) collective-permute-start(f32[128,128]{1,0:T(8,128)S(1)} %get-tuple-element.21.vector_ref.refs_0_.first_ref), channel_id=1, source_target_pairs={{1,2},{3,4},{5,6},{2,1},{4,3},{6,5},{9,10},{11,12},{13,14},{10,9},... | collective-permute-start | bytes 196616 | tf_op jit(solution)/shard_map/ppermute | solution.py:500
  29.4 4.8 %collective-permute-start.2 = (f32[128,128]{1,0:T(8,128)S(1)}, f32[128,128]{1,0:T(8,128)S(1)}, u32[]{:S(2)}, u32[]{:S(2)}) collective-permute-start(f32[128,128]{1,0:T(8,128)S(1)} %get-tuple-element.21.vector_ref.refs_0_.first_ref), channel_id=1, source_target_pairs={{0,1},{1,0},{2,3},{3,2},{4,5},{5,4},{6,7},{7,6},{8,9},{9,8},{10,11... | collective-permute-start | bytes 196616 | tf_op jit(solution)/shard_map/ppermute | solution.py:501
  37.4 5.6 %collective-permute-start.5 = (f32[128,128]{1,0:T(8,128)S(1)}, f32[128,128]{1,0:T(8,128)S(1)}, u32[]{:S(2)}, u32[]{:S(2)}) collective-permute-start(f32[128,128]{1,0:T(8,128)S(1)} %get-tuple-element.25.vector_ref.refs_1_.second_ref), channel_id=1, source_target_pairs={{1,2},{3,4},{5,6},{2,1},{4,3},{6,5},{9,10},{11,12},{13,14},{10,9},... | collective-permute-start | bytes 196616 | tf_op jit(solution)/shard_map/ppermute | solution.py:500
  38.1 4.9 %collective-permute-start.4 = (f32[128,128]{1,0:T(8,128)S(1)}, f32[128,128]{1,0:T(8,128)S(1)}, u32[]{:S(2)}, u32[]{:S(2)}) collective-permute-start(f32[128,128]{1,0:T(8,128)S(1)} %get-tuple-element.25.vector_ref.refs_1_.second_ref), channel_id=1, source_target_pairs={{0,1},{1,0},{2,3},{3,2},{4,5},{5,4},{6,7},{7,6},{8,9},{9,8},{10,11... | collective-permute-start | bytes 196616 | tf_op jit(solution)/shard_map/ppermute | solution.py:501
  46.2 1.3 %collective-permute-start.6 = (f32[1,128]{1,0:T(1,128)S(1)}, f32[1,128]{1,0:T(1,128)S(1)}, u32[]{:S(2)}, u32[]{:S(2)}) collective-permute-start(f32[1,128]{1,0:T(1,128)S(1)} %get-tuple-element.27), channel_id=1, source_target_pairs={{0,1},{1,0},{2,3},{3,2},{4,5},{5,4},{6,7},{7,6},{8,9},{9,8},{10,11... | collective-permute-start | bytes 1544 | tf_op jit(solution)/shard_map/ppermute | solution.py:518
  47.5 6.1 %collective-permute-start.9 = (f32[1,128]{1,0:T(1,128)S(1)}, f32[1,128]{1,0:T(1,128)S(1)}, u32[]{:S(2)}, u32[]{:S(2)}) collective-permute-start(f32[1,128]{1,0:T(1,128)S(1)} %add.3.parts_ref), channel_id=1, source_target_pairs={{0,6},{1,7},{2,0},{3,1},{4,2},{5,3},{6,4},{7,5},{8,14},{9,15},{10,... | collective-permute-start | bytes 1544 | tf_op jit(solution)/shard_map/ppermute | solution.py:520
  49.8 4.8 %collective-permute-start.8 = (f32[1,128]{1,0:T(1,128)S(1)}, f32[1,128]{1,0:T(1,128)S(1)}, u32[]{:S(2)}, u32[]{:S(2)}) collective-permute-start(f32[1,128]{1,0:T(1,128)S(1)} %add.3.parts_ref), channel_id=1, source_target_pairs={{0,2},{1,3},{2,4},{3,5},{4,6},{5,7},{6,0},{7,1},{8,10},{9,11},{10,... | collective-permute-start | bytes 1544 | tf_op jit(solution)/shard_map/ppermute | solution.py:520
  49.8 5.1 %collective-permute-start.7 = (f32[1,128]{1,0:T(1,128)S(1)}, f32[1,128]{1,0:T(1,128)S(1)}, u32[]{:S(2)}, u32[]{:S(2)}) collective-permute-start(f32[1,128]{1,0:T(1,128)S(1)} %add.3.parts_ref), channel_id=1, source_target_pairs={{0,4},{1,5},{2,6},{3,7},{4,0},{5,1},{6,2},{7,3},{8,12},{9,13},{10,... | collective-permute-start | bytes 1544 | tf_op jit(solution)/shard_map/ppermute | solution.py:520

commit v7 on v6

--- a/solution.py
+++ b/solution.py
@@ -501,6 +501,11 @@
         near = lax.ppermute(value, "slab", inner)
         return near, far
 
+    def near_first(value):
+        near = lax.ppermute(value, "slab", inner)
+        far = lax.ppermute(value, "slab", outer)
+        return near, far
+
     scale = 8.0 / ((entries + 1) * 128)
     near, far = both_sides(packed)
     own_blocks, total, coupled = own_weights(packed, scale)
@@ -510,15 +515,16 @@
     near, far = both_sides(first)
     coupled = own_image(first, own_blocks)
     second, row = image(index, blocks, coupled, diagonal, row, near, far, packed, [first])
-    near, far = both_sides(second)
+    near, far = near_first(second)
     coupled = own_image(second, own_blocks)
     third, row = image(
         index, blocks, coupled, diagonal, row, near, far, packed, [first, second]
     )
     row = row + lax.ppermute(row, "slab", inner)
+    half = slab_count // 2
     around = [
         lax.ppermute(row, "slab", [(i, (i + step) % slab_count) for i in range(slab_count)])
-        for step in (slab_count // 2, *(x for x in range(2, slab_count, 2) if x != slab_count // 2))
+        for step in (*(x for x in range(2, slab_count, 2) if x != half), half)
     ]
     outgoing = jax.ShapeDtypeStruct((brick_count, 4 * each + 8, 128), F32)
     params = pltpu.CompilerParams(vmem_limit_bytes=LIMIT)

time: 76.6 us -> 78.4 us (1.023)
  waiting for transfers between devices: 2.06 us -> 4.14 us
    ppermute x0 -> x2, starting transfers between devices: none -> 4.17 us  [the longest x1 3.51 us: near_first(): near = lax.ppermute(value, 'slab', inner)]
    ppermute x3 -> x2, starting transfers between devices: 10.3 us -> 6.83 us  [both_sides(): near = lax.ppermute(value, 'slab', inner)]
    ppermute x3, waiting for transfers between devices: 1.23 us -> 3.3 us  [local(): lax.ppermute(row, 'slab', [(i, (i + step) % slab_count) for i in range(sl...]
    ppermute x3 -> x2, starting transfers between devices: 2 us -> 1.35 us  [both_sides(): far = lax.ppermute(value, 'slab', outer)]
where the time goes in v7:
time: 78.4 us; the launch traced here: 78.1 us
  Pallas kernels  34.6 us (44%)
  blocking collectives  20.2 us (26%)
  starting transfers between devices  18.4 us (23%)
  waiting for transfers between devices  4.14 us (5%)
    all_to_all x1, blocking collectives, local(): lax.all_to_all(outgoing, 'brick', split_axis=0, concat_axis=0, tiled=True)  20.2 us
    pallas_call x1, Pallas kernels, other_weights(): pl.pallas_call(functools.partial(other_kernel, scale, blocks_count), in_s...  16.6 us
    ppermute x2, starting transfers between devices, both_sides(): near = lax.ppermute(value, 'slab', inner)  6.83 us
    pallas_call x2, Pallas kernels, image(): pl.pallas_call(functools.partial(image_kernel, len(past)), in_specs=[SMEM...  6.48 us
    pallas_call x1, Pallas kernels, own_weights(): pl.pallas_call(functools.partial(own_kernel, scale), in_specs=[VMEM], out...  6.14 us
    ppermute x3, starting transfers between devices, local(): lax.ppermute(row, 'slab', [(i, (i + step) % slab_count) for i in range(sl...  5.64 us
    ppermute x1, starting transfers between devices, near_first(): near = lax.ppermute(value, 'slab', inner)  3.51 us
    ppermute x3, waiting for transfers between devices, local(): lax.ppermute(row, 'slab', [(i, (i + step) % slab_count) for i in range(sl...  3.3 us
  transfers between devices with their start and end apart: 10, of which 3 were waited for; matrix products, arithmetic and copies ran while one was open for 0% of the time, Pallas kernels for 12%

profile of v7, /device:TPU:0, one launch (start us, length us, event | category | flops | bytes accessed | tf_op | source)
XLA Modules:
  0.0 78.1 jit_solution(1223938899126149938)
XLA Ops:
  0.6 1.1 %pack.1 = (f32[5,128,128]{2,1,0:T(8,128)S(1)}, s32[1,128]{1,0:T(1,128)S(1)}, s32[4,128]{1,0:T(4,128)S(1)}) custom-call(f32[3,128,128]{2,1,0:T(8,128)} %bitcast.3, f32[128,128]{1,0:T(8,128)} %charge_hbm.1, f32[128,128]{1,0:T(8,128)} %force_hbm.1, s32[1,128]{1,0:T(1,128)} %bitcast.5, s32[4,128]{1,0:T(4,128)} %bitcast.4), custom_call_target="tpu_custom_call" | custom-call | tf_op jit(solution)/shard_map/pack/pallas_call | solution.py:480
  1.8 0.7 collective-permute-start.1
  2.5 3.5 %collective-permute-start = (f32[5,128,128]{2,1,0:T(8,128)S(1)}, f32[5,128,128]{2,1,0:T(8,128)S(1)}, u32[]{:S(2)}, u32[]{:S(2)}) collective-permute-start(f32[5,128,128]{2,1,0:T(8,128)S(1)} %get-tuple-element.17.own_ref), channel_id=1, source_target_pairs={{0,1},{1,0},{2,3},{3,2},{4,5},{5,4},{6,7},{7,6},{8,9},{9,8},{10,11... | collective-permute-start | bytes 983048 | tf_op jit(solution)/shard_map/ppermute | solution.py:501
  5.9 6.1 %own_weights.1 = (bf16[128,128,128]{2,1,0:T(8,128)(2,1)S(1)}, f32[128,128]{1,0:T(8,128)S(1)}, f32[128,128]{1,0:T(8,128)S(1)}) custom-call(f32[5,128,128]{2,1,0:T(8,128)S(1)} %get-tuple-element.17.own_ref), custom_call_target="tpu_custom_call" | custom-call | flops 1258291200 | bytes 1048576 | tf_op jit(solution)/shard_map/own_weights/pallas_call | solution.py:255
  12.1 0.0 collective-permute-done.1.far_ref
  12.1 16.6 %other_weights.1 = (bf16[128,512,128]{2,1,0:T(8,128)(2,1)S(1)}, f32[128,128]{1,0:T(8,128)S(1)}, f32[128,128]{1,0:T(8,128)S(1)}, f32[1,128]{1,0:T(1,128)S(1)}) custom-call(s32[4,128]{1,0:T(4,128)S(1)} %get-tuple-element.16.index_ref, f32[5,128,128]{2,1,0:T(8,128)S(1)} %get-tuple-element.17.own_ref, f32[5,128,128]{2,1,0:T(8,128)S(1)} %collective-permute-done.near_ref, ...), custom_call_target="tpu_custom_call" | custom-call | tf_op jit(solution)/shard_map/other_weights/pallas_call | solution.py:292
  28.7 0.7 collective-permute-start.3
  29.4 3.4 %collective-permute-start.2 = (f32[128,128]{1,0:T(8,128)S(1)}, f32[128,128]{1,0:T(8,128)S(1)}, u32[]{:S(2)}, u32[]{:S(2)}) collective-permute-start(f32[128,128]{1,0:T(8,128)S(1)} %get-tuple-element.21.vector_ref.refs_0_.first_ref), channel_id=1, source_target_pairs={{0,1},{1,0},{2,3},{3,2},{4,5},{5,4},{6,7},{7,6},{8,9},{9,8},{10,11... | collective-permute-start | bytes 196616 | tf_op jit(solution)/shard_map/ppermute | solution.py:501
  32.7 1.4 %own_image.2.coupled_ref = f32[128,128]{1,0:T(8,128)S(1)} custom-call(f32[128,128]{1,0:T(8,128)S(1)} %get-tuple-element.21.vector_ref.refs_0_.first_ref, bf16[128,128,128]{2,1,0:T(8,128)(2,1)S(1)} %get-tuple-element.22.blocks_ref), custom_call_target="tpu_custom_call" | custom-call | flops 1073741824 | bytes 4194304 | tf_op jit(solution)/shard_map/own_image/pallas_call | solution.py:330
  34.1 3.2 %image.2 = (f32[128,128]{1,0:T(8,128)S(1)}, f32[1,128]{1,0:T(1,128)S(1)}) custom-call(s32[4,128]{1,0:T(4,128)S(1)} %get-tuple-element.16.index_ref, bf16[128,512,128]{2,1,0:T(8,128)(2,1)S(1)} %get-tuple-element.20.blocks_ref, f32[128,128]{1,0:T(8,128)S(1)} %own_image.2.coupled_ref, f32[128,128]{1,0:T(8,128)S(1)} %get-tuple-element.23.diagonal_ref, ...), custom_call_target="tpu_custom_call" | custom-call | tf_op jit(solution)/shard_map/image/pallas_call | solution.py:376
  37.4 0.7 collective-permute-start.5
  38.1 3.5 %collective-permute-start.4 = (f32[128,128]{1,0:T(8,128)S(1)}, f32[128,128]{1,0:T(8,128)S(1)}, u32[]{:S(2)}, u32[]{:S(2)}) collective-permute-start(f32[128,128]{1,0:T(8,128)S(1)} %get-tuple-element.25.vector_ref.refs_1_.second_ref), channel_id=1, source_target_pairs={{0,1},{1,0},{2,3},{3,2},{4,5},{5,4},{6,7},{7,6},{8,9},{9,8},{10,11... | collective-permute-start | bytes 196616 | tf_op jit(solution)/shard_map/ppermute | solution.py:505
  41.6 1.4 %own_image.3.coupled_ref = f32[128,128]{1,0:T(8,128)S(1)} custom-call(f32[128,128]{1,0:T(8,128)S(1)} %get-tuple-element.25.vector_ref.refs_1_.second_ref, bf16[128,128,128]{2,1,0:T(8,128)(2,1)S(1)} %get-tuple-element.22.blocks_ref), custom_call_target="tpu_custom_call" | custom-call | flops 1073741824 | bytes 4194304 | tf_op jit(solution)/shard_map/own_image/pallas_call | solution.py:330
  43.0 3.2 %image.3 = (f32[128,128]{1,0:T(8,128)S(1)}, f32[1,128]{1,0:T(1,128)S(1)}) custom-call(s32[4,128]{1,0:T(4,128)S(1)} %get-tuple-element.16.index_ref, bf16[128,512,128]{2,1,0:T(8,128)(2,1)S(1)} %get-tuple-element.20.blocks_ref, f32[128,128]{1,0:T(8,128)S(1)} %own_image.3.coupled_ref, f32[128,128]{1,0:T(8,128)S(1)} %get-tuple-element.23.diagonal_ref, ...), custom_call_target="tpu_custom_call" | custom-call | tf_op jit(solution)/shard_map/image/pallas_call | solution.py:376
  46.2 0.5 collective-permute-start.6
  46.7 0.8 %collective-permute-done.6 = f32[1,128]{1,0:T(1,128)S(1)} collective-permute-done((f32[1,128]{1,0:T(1,128)S(1)}, f32[1,128]{1,0:T(1,128)S(1)}, u32[]{:S(2)}, u32[]{:S(2)}) %collective-permute-start.6) | collective-permute-done | bytes 544 | tf_op jit(solution)/shard_map/ppermute | solution.py:523
  47.5 3.6 %collective-permute-start.9 = (f32[1,128]{1,0:T(1,128)S(1)}, f32[1,128]{1,0:T(1,128)S(1)}, u32[]{:S(2)}, u32[]{:S(2)}) collective-permute-start(f32[1,128]{1,0:T(1,128)S(1)} %add.3.parts_ref), channel_id=1, source_target_pairs={{0,4},{1,5},{2,6},{3,7},{4,0},{5,1},{6,2},{7,3},{8,12},{9,13},{10,... | collective-permute-start | bytes 1544 | tf_op jit(solution)/shard_map/ppermute | solution.py:526
  51.1 1.0 %collective-permute-start.8 = (f32[1,128]{1,0:T(1,128)S(1)}, f32[1,128]{1,0:T(1,128)S(1)}, u32[]{:S(2)}, u32[]{:S(2)}) collective-permute-start(f32[1,128]{1,0:T(1,128)S(1)} %add.3.parts_ref), channel_id=1, source_target_pairs={{0,6},{1,7},{2,0},{3,1},{4,2},{5,3},{6,4},{7,5},{8,14},{9,15},{10,... | collective-permute-start | bytes 1544 | tf_op jit(solution)/shard_map/ppermute | solution.py:526
  52.1 1.0 %collective-permute-start.7 = (f32[1,128]{1,0:T(1,128)S(1)}, f32[1,128]{1,0:T(1,128)S(1)}, u32[]{:S(2)}, u32[]{:S(2)}) collective-permute-start(f32[1,128]{1,0:T(1,128)S(1)} %add.3.parts_ref), channel_id=1, source_target_pairs={{0,2},{1,3},{2,4},{3,5},{4,6},{5,7},{6,0},{7,1},{8,10},{9,11},{10,... | collective-permute-start | bytes 1544 | tf_op jit(solution)/shard_map/ppermute | solution.py:526
  53.1 0.5 slots.1.refs_3_
  53.6 1.1 %collective-permute-done.8.refs_1_ = f32[1,128]{1,0:T(1,128)S(1)} collective-permute-done((f32[1,128]{1,0:T(1,128)S(1)}, f32[1,128]{1,0:T(1,128)S(1)}, u32[]{:S(2)}, u32[]{:S(2)}) %collective-permute-start.8) | collective-permute-done | bytes 544 | tf_op jit(solution)/shard_map/ppermute | solution.py:526
  54.7 2.2 %collective-permute-done.7.refs_0_ = f32[1,128]{1,0:T(1,128)S(1)} collective-permute-done((f32[1,128]{1,0:T(1,128)S(1)}, f32[1,128]{1,0:T(1,128)S(1)}, u32[]{:S(2)}, u32[]{:S(2)}) %collective-permute-start.7) | collective-permute-done | bytes 544 | tf_op jit(solution)/shard_map/ppermute | solution.py:526
  56.9 20.2 %all_to_all.5.arrived_ref = f32[16,104,128]{2,1,0:T(8,128)S(1)} all-to-all(f32[16,104,128]{2,1,0:T(8,128)S(1)} %join.1), channel_id=1, replica_groups=mesh['brick'=16,'slab'=8] {'brick'}, dimensions={0} | all-to-all | bytes 1703936 | tf_op jit(solution)/shard_map/all_to_all | solution.py:549
  77.2 1.0 %finish.1 = (f32[384,128]{1,0:T(8,128)}, f32[384,128]{1,0:T(8,128)}) custom-call(f32[16,104,128]{2,1,0:T(8,128)S(1)} %all_to_all.5.arrived_ref), custom_call_target="tpu_custom_call" | custom-call | tf_op jit(solution)/shard_map/finish/pallas_call | solution.py:551
  (8 shorter events, 0.0 us)
Async XLA Ops:
  1.8 10.3 %collective-permute-start.1 = (f32[5,128,128]{2,1,0:T(8,128)S(1)}, f32[5,128,128]{2,1,0:T(8,128)S(1)}, u32[]{:S(2)}, u32[]{:S(2)}) collective-permute-start(f32[5,128,128]{2,1,0:T(8,128)S(1)} %get-tuple-element.17.own_ref), channel_id=1, source_target_pairs={{1,2},{3,4},{5,6},{2,1},{4,3},{6,5},{9,10},{11,12},{13,14},{10,9},... | collective-permute-start | bytes 983048 | tf_op jit(solution)/shard_map/ppermute | solution.py:500
  2.5 9.6 %collective-permute-start = (f32[5,128,128]{2,1,0:T(8,128)S(1)}, f32[5,128,128]{2,1,0:T(8,128)S(1)}, u32[]{:S(2)}, u32[]{:S(2)}) collective-permute-start(f32[5,128,128]{2,1,0:T(8,128)S(1)} %get-tuple-element.17.own_ref), channel_id=1, source_target_pairs={{0,1},{1,0},{2,3},{3,2},{4,5},{5,4},{6,7},{7,6},{8,9},{9,8},{10,11... | collective-permute-start | bytes 983048 | tf_op jit(solution)/shard_map/ppermute | solution.py:501
  28.7 5.4 %collective-permute-start.3 = (f32[128,128]{1,0:T(8,128)S(1)}, f32[128,128]{1,0:T(8,128)S(1)}, u32[]{:S(2)}, u32[]{:S(2)}) collective-permute-start(f32[128,128]{1,0:T(8,128)S(1)} %get-tuple-element.21.vector_ref.refs_0_.first_ref), channel_id=1, source_target_pairs={{1,2},{3,4},{5,6},{2,1},{4,3},{6,5},{9,10},{11,12},{13,14},{10,9},... | collective-permute-start | bytes 196616 | tf_op jit(solution)/shard_map/ppermute | solution.py:500
  29.4 4.8 %collective-permute-start.2 = (f32[128,128]{1,0:T(8,128)S(1)}, f32[128,128]{1,0:T(8,128)S(1)}, u32[]{:S(2)}, u32[]{:S(2)}) collective-permute-start(f32[128,128]{1,0:T(8,128)S(1)} %get-tuple-element.21.vector_ref.refs_0_.first_ref), channel_id=1, source_target_pairs={{0,1},{1,0},{2,3},{3,2},{4,5},{5,4},{6,7},{7,6},{8,9},{9,8},{10,11... | collective-permute-start | bytes 196616 | tf_op jit(solution)/shard_map/ppermute | solution.py:501
  37.4 5.6 %collective-permute-start.5 = (f32[128,128]{1,0:T(8,128)S(1)}, f32[128,128]{1,0:T(8,128)S(1)}, u32[]{:S(2)}, u32[]{:S(2)}) collective-permute-start(f32[128,128]{1,0:T(8,128)S(1)} %get-tuple-element.25.vector_ref.refs_1_.second_ref), channel_id=1, source_target_pairs={{1,2},{3,4},{5,6},{2,1},{4,3},{6,5},{9,10},{11,12},{13,14},{10,9},... | collective-permute-start | bytes 196616 | tf_op jit(solution)/shard_map/ppermute | solution.py:506
  38.1 4.9 %collective-permute-start.4 = (f32[128,128]{1,0:T(8,128)S(1)}, f32[128,128]{1,0:T(8,128)S(1)}, u32[]{:S(2)}, u32[]{:S(2)}) collective-permute-start(f32[128,128]{1,0:T(8,128)S(1)} %get-tuple-element.25.vector_ref.refs_1_.second_ref), channel_id=1, source_target_pairs={{0,1},{1,0},{2,3},{3,2},{4,5},{5,4},{6,7},{7,6},{8,9},{9,8},{10,11... | collective-permute-start | bytes 196616 | tf_op jit(solution)/shard_map/ppermute | solution.py:505
  46.2 1.3 %collective-permute-start.6 = (f32[1,128]{1,0:T(1,128)S(1)}, f32[1,128]{1,0:T(1,128)S(1)}, u32[]{:S(2)}, u32[]{:S(2)}) collective-permute-start(f32[1,128]{1,0:T(1,128)S(1)} %get-tuple-element.27), channel_id=1, source_target_pairs={{0,1},{1,0},{2,3},{3,2},{4,5},{5,4},{6,7},{7,6},{8,9},{9,8},{10,11... | collective-permute-start | bytes 1544 | tf_op jit(solution)/shard_map/ppermute | solution.py:523
  47.5 6.1 %collective-permute-start.9 = (f32[1,128]{1,0:T(1,128)S(1)}, f32[1,128]{1,0:T(1,128)S(1)}, u32[]{:S(2)}, u32[]{:S(2)}) collective-permute-start(f32[1,128]{1,0:T(1,128)S(1)} %add.3.parts_ref), channel_id=1, source_target_pairs={{0,4},{1,5},{2,6},{3,7},{4,0},{5,1},{6,2},{7,3},{8,12},{9,13},{10,... | collective-permute-start | bytes 1544 | tf_op jit(solution)/shard_map/ppermute | solution.py:526
  51.1 3.6 %collective-permute-start.8 = (f32[1,128]{1,0:T(1,128)S(1)}, f32[1,128]{1,0:T(1,128)S(1)}, u32[]{:S(2)}, u32[]{:S(2)}) collective-permute-start(f32[1,128]{1,0:T(1,128)S(1)} %add.3.parts_ref), channel_id=1, source_target_pairs={{0,6},{1,7},{2,0},{3,1},{4,2},{5,3},{6,4},{7,5},{8,14},{9,15},{10,... | collective-permute-start | bytes 1544 | tf_op jit(solution)/shard_map/ppermute | solution.py:526
  52.1 4.8 %collective-permute-start.7 = (f32[1,128]{1,0:T(1,128)S(1)}, f32[1,128]{1,0:T(1,128)S(1)}, u32[]{:S(2)}, u32[]{:S(2)}) collective-permute-start(f32[1,128]{1,0:T(1,128)S(1)} %add.3.parts_ref), channel_id=1, source_target_pairs={{0,2},{1,3},{2,4},{3,5},{4,6},{5,7},{6,0},{7,1},{8,10},{9,11},{10,... | collective-permute-start | bytes 1544 | tf_op jit(solution)/shard_map/ppermute | solution.py:526

commit v8 on v6

--- a/solution.py
+++ b/solution.py
@@ -518,7 +518,7 @@
     row = row + lax.ppermute(row, "slab", inner)
     around = [
         lax.ppermute(row, "slab", [(i, (i + step) % slab_count) for i in range(slab_count)])
-        for step in (slab_count // 2, *(x for x in range(2, slab_count, 2) if x != slab_count // 2))
+        for step in range(2, slab_count, 2)
     ]
     outgoing = jax.ShapeDtypeStruct((brick_count, 4 * each + 8, 128), F32)
     params = pltpu.CompilerParams(vmem_limit_bytes=LIMIT)

time: 76.6 us -> 77.7 us (1.014)
  waiting for transfers between devices: 2.06 us -> 4.11 us
    ppermute x3, waiting for transfers between devices: 1.23 us -> 3.28 us  [local(): lax.ppermute(row, 'slab', [(i, (i + step) % slab_count) for i in range(sl...]
where the time goes in v8:
time: 77.7 us; the launch traced here: 77.5 us
  Pallas kernels  34.6 us (45%)
  blocking collectives  20.3 us (26%)
  starting transfers between devices  17.8 us (23%)
  waiting for transfers between devices  4.11 us (5%)
    all_to_all x1, blocking collectives, local(): lax.all_to_all(outgoing, 'brick', split_axis=0, concat_axis=0, tiled=True)  20.3 us
    pallas_call x1, Pallas kernels, other_weights(): pl.pallas_call(functools.partial(other_kernel, scale, blocks_count), in_s...  16.6 us
    ppermute x3, starting transfers between devices, both_sides(): near = lax.ppermute(value, 'slab', inner)  10.3 us
    pallas_call x2, Pallas kernels, image(): pl.pallas_call(functools.partial(image_kernel, len(past)), in_specs=[SMEM...  6.49 us
    pallas_call x1, Pallas kernels, own_weights(): pl.pallas_call(functools.partial(own_kernel, scale), in_specs=[VMEM], out...  6.14 us
    ppermute x3, starting transfers between devices, local(): lax.ppermute(row, 'slab', [(i, (i + step) % slab_count) for i in range(sl...  5.06 us
    ppermute x3, waiting for transfers between devices, local(): lax.ppermute(row, 'slab', [(i, (i + step) % slab_count) for i in range(sl...  3.28 us
    pallas_call x2, Pallas kernels, own_image(): pl.pallas_call(own_image_kernel, in_specs=[VMEM] * 2, out_specs=VMEM, out...  2.75 us
  transfers between devices with their start and end apart: 10, of which 3 were waited for; matrix products, arithmetic and copies ran while one was open for 0% of the time, Pallas kernels for 12%

profile of v8, /device:TPU:0, one launch (start us, length us, event | category | flops | bytes accessed | tf_op | source)
XLA Modules:
  0.0 77.5 jit_solution(14903667926694392165)
XLA Ops:
  0.6 1.1 %pack.1 = (f32[5,128,128]{2,1,0:T(8,128)S(1)}, s32[1,128]{1,0:T(1,128)S(1)}, s32[4,128]{1,0:T(4,128)S(1)}) custom-call(f32[3,128,128]{2,1,0:T(8,128)} %bitcast.3, f32[128,128]{1,0:T(8,128)} %charge_hbm.1, f32[128,128]{1,0:T(8,128)} %force_hbm.1, s32[1,128]{1,0:T(1,128)} %bitcast.5, s32[4,128]{1,0:T(4,128)} %bitcast.4), custom_call_target="tpu_custom_call" | custom-call | tf_op jit(solution)/shard_map/pack/pallas_call | solution.py:480
  1.8 0.7 collective-permute-start.1
  2.5 3.5 %collective-permute-start = (f32[5,128,128]{2,1,0:T(8,128)S(1)}, f32[5,128,128]{2,1,0:T(8,128)S(1)}, u32[]{:S(2)}, u32[]{:S(2)}) collective-permute-start(f32[5,128,128]{2,1,0:T(8,128)S(1)} %get-tuple-element.17.own_ref), channel_id=1, source_target_pairs={{0,1},{1,0},{2,3},{3,2},{4,5},{5,4},{6,7},{7,6},{8,9},{9,8},{10,11... | collective-permute-start | bytes 983048 | tf_op jit(solution)/shard_map/ppermute | solution.py:501
  5.9 6.1 %own_weights.1 = (bf16[128,128,128]{2,1,0:T(8,128)(2,1)S(1)}, f32[128,128]{1,0:T(8,128)S(1)}, f32[128,128]{1,0:T(8,128)S(1)}) custom-call(f32[5,128,128]{2,1,0:T(8,128)S(1)} %get-tuple-element.17.own_ref), custom_call_target="tpu_custom_call" | custom-call | flops 1258291200 | bytes 1048576 | tf_op jit(solution)/shard_map/own_weights/pallas_call | solution.py:255
  12.1 0.0 collective-permute-done.1.far_ref
  12.1 16.6 %other_weights.1 = (bf16[128,512,128]{2,1,0:T(8,128)(2,1)S(1)}, f32[128,128]{1,0:T(8,128)S(1)}, f32[128,128]{1,0:T(8,128)S(1)}, f32[1,128]{1,0:T(1,128)S(1)}) custom-call(s32[4,128]{1,0:T(4,128)S(1)} %get-tuple-element.16.index_ref, f32[5,128,128]{2,1,0:T(8,128)S(1)} %get-tuple-element.17.own_ref, f32[5,128,128]{2,1,0:T(8,128)S(1)} %collective-permute-done.near_ref, ...), custom_call_target="tpu_custom_call" | custom-call | tf_op jit(solution)/shard_map/other_weights/pallas_call | solution.py:292
  28.7 0.7 collective-permute-start.3
  29.4 3.4 %collective-permute-start.2 = (f32[128,128]{1,0:T(8,128)S(1)}, f32[128,128]{1,0:T(8,128)S(1)}, u32[]{:S(2)}, u32[]{:S(2)}) collective-permute-start(f32[128,128]{1,0:T(8,128)S(1)} %get-tuple-element.21.vector_ref.refs_0_.first_ref), channel_id=1, source_target_pairs={{0,1},{1,0},{2,3},{3,2},{4,5},{5,4},{6,7},{7,6},{8,9},{9,8},{10,11... | collective-permute-start | bytes 196616 | tf_op jit(solution)/shard_map/ppermute | solution.py:501
  32.7 1.4 %own_image.2.coupled_ref = f32[128,128]{1,0:T(8,128)S(1)} custom-call(f32[128,128]{1,0:T(8,128)S(1)} %get-tuple-element.21.vector_ref.refs_0_.first_ref, bf16[128,128,128]{2,1,0:T(8,128)(2,1)S(1)} %get-tuple-element.22.blocks_ref), custom_call_target="tpu_custom_call" | custom-call | flops 1073741824 | bytes 4194304 | tf_op jit(solution)/shard_map/own_image/pallas_call | solution.py:330
  34.1 3.2 %image.2 = (f32[128,128]{1,0:T(8,128)S(1)}, f32[1,128]{1,0:T(1,128)S(1)}) custom-call(s32[4,128]{1,0:T(4,128)S(1)} %get-tuple-element.16.index_ref, bf16[128,512,128]{2,1,0:T(8,128)(2,1)S(1)} %get-tuple-element.20.blocks_ref, f32[128,128]{1,0:T(8,128)S(1)} %own_image.2.coupled_ref, f32[128,128]{1,0:T(8,128)S(1)} %get-tuple-element.23.diagonal_ref, ...), custom_call_target="tpu_custom_call" | custom-call | tf_op jit(solution)/shard_map/image/pallas_call | solution.py:376
  37.4 0.7 collective-permute-start.5
  38.0 3.5 %collective-permute-start.4 = (f32[128,128]{1,0:T(8,128)S(1)}, f32[128,128]{1,0:T(8,128)S(1)}, u32[]{:S(2)}, u32[]{:S(2)}) collective-permute-start(f32[128,128]{1,0:T(8,128)S(1)} %get-tuple-element.25.vector_ref.refs_1_.second_ref), channel_id=1, source_target_pairs={{0,1},{1,0},{2,3},{3,2},{4,5},{5,4},{6,7},{7,6},{8,9},{9,8},{10,11... | collective-permute-start | bytes 196616 | tf_op jit(solution)/shard_map/ppermute | solution.py:501
  41.5 1.4 %own_image.3.coupled_ref = f32[128,128]{1,0:T(8,128)S(1)} custom-call(f32[128,128]{1,0:T(8,128)S(1)} %get-tuple-element.25.vector_ref.refs_1_.second_ref, bf16[128,128,128]{2,1,0:T(8,128)(2,1)S(1)} %get-tuple-element.22.blocks_ref), custom_call_target="tpu_custom_call" | custom-call | flops 1073741824 | bytes 4194304 | tf_op jit(solution)/shard_map/own_image/pallas_call | solution.py:330
  43.0 3.2 %image.3 = (f32[128,128]{1,0:T(8,128)S(1)}, f32[1,128]{1,0:T(1,128)S(1)}) custom-call(s32[4,128]{1,0:T(4,128)S(1)} %get-tuple-element.16.index_ref, bf16[128,512,128]{2,1,0:T(8,128)(2,1)S(1)} %get-tuple-element.20.blocks_ref, f32[128,128]{1,0:T(8,128)S(1)} %own_image.3.coupled_ref, f32[128,128]{1,0:T(8,128)S(1)} %get-tuple-element.23.diagonal_ref, ...), custom_call_target="tpu_custom_call" | custom-call | tf_op jit(solution)/shard_map/image/pallas_call | solution.py:376
  46.2 0.5 collective-permute-start.6
  46.7 0.8 %collective-permute-done.6 = f32[1,128]{1,0:T(1,128)S(1)} collective-permute-done((f32[1,128]{1,0:T(1,128)S(1)}, f32[1,128]{1,0:T(1,128)S(1)}, u32[]{:S(2)}, u32[]{:S(2)}) %collective-permute-start.6) | collective-permute-done | bytes 544 | tf_op jit(solution)/shard_map/ppermute | solution.py:518
  47.5 2.3 %collective-permute-start.9 = (f32[1,128]{1,0:T(1,128)S(1)}, f32[1,128]{1,0:T(1,128)S(1)}, u32[]{:S(2)}, u32[]{:S(2)}) collective-permute-start(f32[1,128]{1,0:T(1,128)S(1)} %add.3.parts_ref), channel_id=1, source_target_pairs={{0,6},{1,7},{2,0},{3,1},{4,2},{5,3},{6,4},{7,5},{8,14},{9,15},{10,... | collective-permute-start | bytes 1544 | tf_op jit(solution)/shard_map/ppermute | solution.py:520
  49.8 1.7 %collective-permute-start.8 = (f32[1,128]{1,0:T(1,128)S(1)}, f32[1,128]{1,0:T(1,128)S(1)}, u32[]{:S(2)}, u32[]{:S(2)}) collective-permute-start(f32[1,128]{1,0:T(1,128)S(1)} %add.3.parts_ref), channel_id=1, source_target_pairs={{0,4},{1,5},{2,6},{3,7},{4,0},{5,1},{6,2},{7,3},{8,12},{9,13},{10,... | collective-permute-start | bytes 1544 | tf_op jit(solution)/shard_map/ppermute | solution.py:520
  51.5 1.0 %collective-permute-start.7 = (f32[1,128]{1,0:T(1,128)S(1)}, f32[1,128]{1,0:T(1,128)S(1)}, u32[]{:S(2)}, u32[]{:S(2)}) collective-permute-start(f32[1,128]{1,0:T(1,128)S(1)} %add.3.parts_ref), channel_id=1, source_target_pairs={{0,2},{1,3},{2,4},{3,5},{4,6},{5,7},{6,0},{7,1},{8,10},{9,11},{10,... | collective-permute-start | bytes 1544 | tf_op jit(solution)/shard_map/ppermute | solution.py:520
  52.5 0.5 slots.1.refs_3_
  53.0 1.8 %collective-permute-done.8.refs_1_ = f32[1,128]{1,0:T(1,128)S(1)} collective-permute-done((f32[1,128]{1,0:T(1,128)S(1)}, f32[1,128]{1,0:T(1,128)S(1)}, u32[]{:S(2)}, u32[]{:S(2)}) %collective-permute-start.8) | collective-permute-done | bytes 544 | tf_op jit(solution)/shard_map/ppermute | solution.py:520
  54.8 1.5 %collective-permute-done.7.refs_0_ = f32[1,128]{1,0:T(1,128)S(1)} collective-permute-done((f32[1,128]{1,0:T(1,128)S(1)}, f32[1,128]{1,0:T(1,128)S(1)}, u32[]{:S(2)}, u32[]{:S(2)}) %collective-permute-start.7) | collective-permute-done | bytes 544 | tf_op jit(solution)/shard_map/ppermute | solution.py:520
  56.3 20.3 %all_to_all.5.arrived_ref = f32[16,104,128]{2,1,0:T(8,128)S(1)} all-to-all(f32[16,104,128]{2,1,0:T(8,128)S(1)} %join.1), channel_id=1, replica_groups=mesh['brick'=16,'slab'=8] {'brick'}, dimensions={0} | all-to-all | bytes 1703936 | tf_op jit(solution)/shard_map/all_to_all | solution.py:543
  76.6 1.0 %finish.1 = (f32[384,128]{1,0:T(8,128)}, f32[384,128]{1,0:T(8,128)}) custom-call(f32[16,104,128]{2,1,0:T(8,128)S(1)} %all_to_all.5.arrived_ref), custom_call_target="tpu_custom_call" | custom-call | tf_op jit(solution)/shard_map/finish/pallas_call | solution.py:545
  (8 shorter events, 0.0 us)
Async XLA Ops:
  1.8 10.3 %collective-permute-start.1 = (f32[5,128,128]{2,1,0:T(8,128)S(1)}, f32[5,128,128]{2,1,0:T(8,128)S(1)}, u32[]{:S(2)}, u32[]{:S(2)}) collective-permute-start(f32[5,128,128]{2,1,0:T(8,128)S(1)} %get-tuple-element.17.own_ref), channel_id=1, source_target_pairs={{1,2},{3,4},{5,6},{2,1},{4,3},{6,5},{9,10},{11,12},{13,14},{10,9},... | collective-permute-start | bytes 983048 | tf_op jit(solution)/shard_map/ppermute | solution.py:500
  2.5 9.6 %collective-permute-start = (f32[5,128,128]{2,1,0:T(8,128)S(1)}, f32[5,128,128]{2,1,0:T(8,128)S(1)}, u32[]{:S(2)}, u32[]{:S(2)}) collective-permute-start(f32[5,128,128]{2,1,0:T(8,128)S(1)} %get-tuple-element.17.own_ref), channel_id=1, source_target_pairs={{0,1},{1,0},{2,3},{3,2},{4,5},{5,4},{6,7},{7,6},{8,9},{9,8},{10,11... | collective-permute-start | bytes 983048 | tf_op jit(solution)/shard_map/ppermute | solution.py:501
  28.7 5.4 %collective-permute-start.3 = (f32[128,128]{1,0:T(8,128)S(1)}, f32[128,128]{1,0:T(8,128)S(1)}, u32[]{:S(2)}, u32[]{:S(2)}) collective-permute-start(f32[128,128]{1,0:T(8,128)S(1)} %get-tuple-element.21.vector_ref.refs_0_.first_ref), channel_id=1, source_target_pairs={{1,2},{3,4},{5,6},{2,1},{4,3},{6,5},{9,10},{11,12},{13,14},{10,9},... | collective-permute-start | bytes 196616 | tf_op jit(solution)/shard_map/ppermute | solution.py:500
  29.4 4.7 %collective-permute-start.2 = (f32[128,128]{1,0:T(8,128)S(1)}, f32[128,128]{1,0:T(8,128)S(1)}, u32[]{:S(2)}, u32[]{:S(2)}) collective-permute-start(f32[128,128]{1,0:T(8,128)S(1)} %get-tuple-element.21.vector_ref.refs_0_.first_ref), channel_id=1, source_target_pairs={{0,1},{1,0},{2,3},{3,2},{4,5},{5,4},{6,7},{7,6},{8,9},{9,8},{10,11... | collective-permute-start | bytes 196616 | tf_op jit(solution)/shard_map/ppermute | solution.py:501
  37.4 5.6 %collective-permute-start.5 = (f32[128,128]{1,0:T(8,128)S(1)}, f32[128,128]{1,0:T(8,128)S(1)}, u32[]{:S(2)}, u32[]{:S(2)}) collective-permute-start(f32[128,128]{1,0:T(8,128)S(1)} %get-tuple-element.25.vector_ref.refs_1_.second_ref), channel_id=1, source_target_pairs={{1,2},{3,4},{5,6},{2,1},{4,3},{6,5},{9,10},{11,12},{13,14},{10,9},... | collective-permute-start | bytes 196616 | tf_op jit(solution)/shard_map/ppermute | solution.py:500
  38.0 4.9 %collective-permute-start.4 = (f32[128,128]{1,0:T(8,128)S(1)}, f32[128,128]{1,0:T(8,128)S(1)}, u32[]{:S(2)}, u32[]{:S(2)}) collective-permute-start(f32[128,128]{1,0:T(8,128)S(1)} %get-tuple-element.25.vector_ref.refs_1_.second_ref), channel_id=1, source_target_pairs={{0,1},{1,0},{2,3},{3,2},{4,5},{5,4},{6,7},{7,6},{8,9},{9,8},{10,11... | collective-permute-start | bytes 196616 | tf_op jit(solution)/shard_map/ppermute | solution.py:501
  46.2 1.3 %collective-permute-start.6 = (f32[1,128]{1,0:T(1,128)S(1)}, f32[1,128]{1,0:T(1,128)S(1)}, u32[]{:S(2)}, u32[]{:S(2)}) collective-permute-start(f32[1,128]{1,0:T(1,128)S(1)} %get-tuple-element.27), channel_id=1, source_target_pairs={{0,1},{1,0},{2,3},{3,2},{4,5},{5,4},{6,7},{7,6},{8,9},{9,8},{10,11... | collective-permute-start | bytes 1544 | tf_op jit(solution)/shard_map/ppermute | solution.py:518
  47.5 5.5 %collective-permute-start.9 = (f32[1,128]{1,0:T(1,128)S(1)}, f32[1,128]{1,0:T(1,128)S(1)}, u32[]{:S(2)}, u32[]{:S(2)}) collective-permute-start(f32[1,128]{1,0:T(1,128)S(1)} %add.3.parts_ref), channel_id=1, source_target_pairs={{0,6},{1,7},{2,0},{3,1},{4,2},{5,3},{6,4},{7,5},{8,14},{9,15},{10,... | collective-permute-start | bytes 1544 | tf_op jit(solution)/shard_map/ppermute | solution.py:520
  49.8 5.1 %collective-permute-start.8 = (f32[1,128]{1,0:T(1,128)S(1)}, f32[1,128]{1,0:T(1,128)S(1)}, u32[]{:S(2)}, u32[]{:S(2)}) collective-permute-start(f32[1,128]{1,0:T(1,128)S(1)} %add.3.parts_ref), channel_id=1, source_target_pairs={{0,4},{1,5},{2,6},{3,7},{4,0},{5,1},{6,2},{7,3},{8,12},{9,13},{10,... | collective-permute-start | bytes 1544 | tf_op jit(solution)/shard_map/ppermute | solution.py:520
  51.5 4.8 %collective-permute-start.7 = (f32[1,128]{1,0:T(1,128)S(1)}, f32[1,128]{1,0:T(1,128)S(1)}, u32[]{:S(2)}, u32[]{:S(2)}) collective-permute-start(f32[1,128]{1,0:T(1,128)S(1)} %add.3.parts_ref), channel_id=1, source_target_pairs={{0,2},{1,3},{2,4},{3,5},{4,6},{5,7},{6,0},{7,1},{8,10},{9,11},{10,... | collective-permute-start | bytes 1544 | tf_op jit(solution)/shard_map/ppermute | solution.py:520
